TPU v7x, 512 devices: a whole 4x8x8 slice. The times are simulated.
512 devices in a mesh: dp: 8 (over z_lo, x), region: 64 (over y, z_hi, core).
Axes of the slice: x: 4, y: 8, z: 8 (z_hi: 4, z_lo: 2; z = z_hi * 2 + z_lo), core: 2. Of those that a mesh axis runs over, the one named last changes fastest.
Arguments:
- queries: bfloat16 [8, 8192, 1280], P('dp', 'region'), may hold values from -5 to 5
- keys: bfloat16 [8, 8192, 1280], P('dp', 'region'), may hold values from -5 to 5
- values: bfloat16 [8, 8192, 1280], P('dp', 'region'), may hold values from -6 to 6
- attn_out: bfloat16 [8, 8192, 1280], P('dp', 'region'), may hold values from -0.125 to 0.125
- d_out: bfloat16 [8, 8192, 2560], P('dp', 'region'), may hold values from -6 to 6
- w_out: bfloat16 [1280, 2560], P('dp'), may hold values from -0.15625 to 0.15625
- adjacency: int32 [64, 4, 12], P('region'), may hold values from 0 to 1, as said below
- counts: int32 [64], P('region'), may hold values from 1 to 4, as said below
Outputs:
- d_queries: bfloat16 [8, 8192, 1280], P('dp', 'region')
- d_keys: bfloat16 [8, 8192, 1280], P('dp', 'region')
- d_values: bfloat16 [8, 8192, 1280], P('dp', 'region')
- d_weight: bfloat16 [1280, 2560], P('dp')
Inputs may be any that keep to these rules, and one draw needn't show every extreme that they name: Region r has 4 token blocks, of which the first counts[r] are live; in some region all 4 are live. adjacency[r, a, j] = 1 lets query block a of region r see key block j % 4 of region (r + j // 4 - 1) mod 64; entry j = 4 + a is 1.
All inputs are finite; a program needn't handle non-finite values.
Results may differ from a plain program's by a relative error of at most 0.007.
Values may be sent and summed in bfloat16 or wider, within the bound.
No kernel may reach another device: no remote copies, remote signals or barrier semaphores. Data moves between devices by JAX's collectives and lax.ppermute only.
A program may use at most 64 MiB of HBM per device.

v0:
```python
import math

import jax
import jax.numpy as jnp
from jax import lax
from jax.sharding import PartitionSpec as P

HEADS = 8
HD = 160
BLK = 4


def from_behind(value, axis, by):
    length = lax.axis_size(axis)
    return lax.ppermute(value, axis, [(i, (i + by) % length) for i in range(length)])


def expand(blocks, block_rows):
    return jnp.repeat(jnp.repeat(blocks, block_rows, axis=0), block_rows, axis=1)


def score_block(query_rows, key_rows):
    scores = jnp.einsum("qhc,khc->hqk", query_rows, key_rows, preferred_element_type=jnp.float32)
    return scores * (1.0 / math.sqrt(HD))


def row_stats(scores, allowed):
    maxima = jnp.max(jnp.where(allowed[None], scores, -1e30), axis=2)
    totals = jnp.sum(jnp.exp(jnp.where(allowed[None], scores - maxima[:, :, None], -1e30)), axis=2)
    return (maxima, totals)


def backward_block(scores, allowed, lse, delta, query_rows, key_rows, value_rows, grad_rows):
    probs = jnp.exp(jnp.where(allowed[None], scores - lse[:, :, None], -1e30))
    probs_b = probs.astype(jnp.bfloat16)
    dvalue = jnp.einsum("hqk,qhc->khc", probs_b, grad_rows, preferred_element_type=jnp.float32)
    dprobs = jnp.einsum("qhc,khc->hqk", grad_rows, value_rows, preferred_element_type=jnp.float32)
    dscores = (probs * (dprobs - delta[:, :, None]) * (1.0 / math.sqrt(HD))).astype(jnp.bfloat16)
    dquery = jnp.einsum("hqk,khc->qhc", dscores, key_rows, preferred_element_type=jnp.float32)
    dkey = jnp.einsum("hqk,qhc->khc", dscores, query_rows, preferred_element_type=jnp.float32)
    return (dquery, dkey, dvalue)


def local(queries, keys, values, attn_out, d_out, w_out, adjacency, counts):
    tok_rows = queries.shape[1]
    block_rows = tok_rows // BLK
    width = queries.shape[2]
    live_blocks = jnp.arange(BLK) < counts[0]
    live_rows = jnp.repeat(live_blocks, block_rows)
    grads = d_out * live_rows[None, :, None].astype(jnp.bfloat16)
    gathered = lax.all_gather(grads, "dp", axis=1, tiled=True)
    out_cols = lax.all_to_all(attn_out, "dp", split_axis=2, concat_axis=1, tiled=True)
    attn_part = jnp.einsum("td,hd->th", gathered[0], w_out, preferred_element_type=jnp.float32)
    d_attn = lax.all_to_all(
        attn_part.astype(jnp.bfloat16)[None], "dp", split_axis=1, concat_axis=2, tiled=True
    )
    weight_part = jnp.einsum(
        "th,td->hd", out_cols[0], gathered[0], preferred_element_type=jnp.float32
    )
    d_weight = lax.psum(weight_part, "region").astype(jnp.bfloat16)
    query_rows = queries[0].reshape(tok_rows, HEADS, HD)
    out_rows = attn_out[0].reshape(tok_rows, HEADS, HD)
    grad_attn = d_attn[0].reshape(tok_rows, HEADS, HD)
    delta = jnp.einsum("qhc,qhc->hq", grad_attn, out_rows, preferred_element_type=jnp.float32)
    adjacent = adjacency[0] == 1
    own_block = jnp.arange(3 * BLK)[None, :] == BLK + jnp.arange(BLK)[:, None]
    key_live = live_rows.astype(jnp.bfloat16)
    fetched = {}
    for offset in (1, -1):
        fetched[offset] = from_behind((keys[0], values[0], key_live), "region", offset)
    key_window = jnp.concatenate([fetched[1][0], keys[0], fetched[-1][0]], 0).reshape(
        3 * tok_rows, HEADS, HD
    )
    value_window = jnp.concatenate([fetched[1][1], values[0], fetched[-1][1]], 0).reshape(
        3 * tok_rows, HEADS, HD
    )
    live_window = jnp.concatenate([fetched[1][2], key_live, fetched[-1][2]], 0)
    live_window = live_window.reshape(3 * BLK, block_rows)[:, 0] > 0.5
    allowed = expand(adjacent & live_window[None] | own_block, block_rows)
    scores = score_block(query_rows, key_window)
    maxima, totals = row_stats(scores, allowed)
    lse = maxima + jnp.log(totals)
    dquery, dkey_win, dvalue_win = backward_block(
        scores, allowed, lse, delta, query_rows, key_window, value_window, grad_attn
    )
    dkey = dkey_win[tok_rows : 2 * tok_rows]
    dvalue = dvalue_win[tok_rows : 2 * tok_rows]
    for offset, first in ((-1, 0), (1, 2)):
        lower = first * tok_rows
        returned = (
            from_behind(
                dkey_win[lower : lower + tok_rows].astype(jnp.bfloat16), "region", offset
            ).astype(jnp.float32),
            from_behind(
                dvalue_win[lower : lower + tok_rows].astype(jnp.bfloat16), "region", offset
            ).astype(jnp.float32),
        )
        dkey = dkey + returned[0]
        dvalue = dvalue + returned[1]
    out_shape = (1, tok_rows, width)
    return (
        dquery.astype(jnp.bfloat16).reshape(out_shape),
        dkey.astype(jnp.bfloat16).reshape(out_shape),
        dvalue.astype(jnp.bfloat16).reshape(out_shape),
        d_weight,
    )


def solution(mesh):
    return jax.shard_map(
        local,
        mesh=mesh,
        in_specs=(
            P("dp", "region", None),
            P("dp", "region", None),
            P("dp", "region", None),
            P("dp", "region", None),
            P("dp", "region", None),
            P("dp", None),
            P("region", None, None),
            P("region"),
        ),
        out_specs=(
            P("dp", "region", None),
            P("dp", "region", None),
            P("dp", "region", None),
            P("dp", None),
        ),
        check_vma=False,
    )
```

profile of v0, /device:TPU:6, one launch (start us, length us, event | category | flops | bytes accessed | tf_op | source)
XLA Modules:
  0.0 472.9 jit_solution(7799400725067004841)
XLA Ops:
  8.1 0.1 convert_element_type.56
  8.2 2.0 broadcast_multiply_fusion
  10.3 13.3 %collective-permute-start.3 = (bf16[128]{0:T(256)(128)(2,1)S(1)}, bf16[128]{0:T(256)(128)(2,1)S(1)}, u32[]{:S(2)}, u32[]{:S(2)}) collective-permute-start(bf16[128]{0:T(256)(128)(2,1)S(1)} %convert_element_type.56), channel_id=1, source_target_pairs={{0,63},{1,0},{2,1},{3,2},{4,3},{5,4},{6,5},{7,6},{8,7},{9,8},{10,9... | collective-permute-start | bytes 776 | tf_op jit(solution)/shard_map/ppermute | solution.py:15
  23.6 2.6 collective-permute-start.1
  26.1 1.9 collective-permute-start
  28.1 7.9 %collective-permute-start.5 = (bf16[128,1280]{1,0:T(8,128)(2,1)S(1)}, bf16[128,1280]{1,0:T(8,128)(2,1)}, u32[]{:S(2)}, u32[]{:S(2)}) collective-permute-start(bf16[128,1280]{1,0:T(8,128)(2,1)S(1)} %bitcast.121), channel_id=1, source_target_pairs={{0,63},{1,0},{2,1},{3,2},{4,3},{5,4},{6,5},{7,6},{8,7},{9,8},{10,9... | collective-permute-start | bytes 983048 | tf_op jit(solution)/shard_map/ppermute | solution.py:15
  36.0 1.9 collective-permute-start.4
  37.9 0.5 copy.83
  38.4 0.6 broadcast.40
  39.0 7.5 %reduce.5 = bf16[1280,128]{1,0:T(8,128)(2,1)S(1)} reduce(bf16[1280,1,128]{2,1,0:T(2,128)(2,1)S(1)} %bitcast.106, bf16[]{:T(256)} %broadcast.40), dimensions={1}, to_apply=%bitcast.90.reduce_sub_computation | reduce | bytes 655362
  46.5 0.8 reshape.81
  47.3 5.8 %all-to-all-start.1 = ((bf16[8,2,10240]{2,1,0:T(2,128)(2,1)}), bf16[8,2,10240]{2,1,0:T(2,128)(2,1)S(1)}, u32[]{:S(2)}, u32[]{:S(2)}) async-start(bf16[8,2,10240]{2,1,0:T(2,128)(2,1)} %reshape.81), calls=%async_computation.1 | async-start | bytes 655360 | tf_op jit(solution)/shard_map/all_to_all | solution.py:52
  53.2 0.2 copy.68
  53.4 2.1 collective-permute-start.2
  55.5 0.9 copy.76
  56.4 0.9 copy.102
  57.3 0.2 copy.71
  57.6 0.1 concatenate.33
  57.6 4.8 %collective-permute-done.2 = bf16[128]{0:T(256)(128)(2,1)S(1)} collective-permute-done((bf16[128]{0:T(256)(128)(2,1)S(1)}, bf16[128]{0:T(256)(128)(2,1)S(1)}, u32[]{:S(2)}, u32[]{:S(2)}) %collective-permute-start.2) | collective-permute-done | bytes 288 | tf_op jit(solution)/shard_map/ppermute | solution.py:15
  62.6 0.1 compare_reduce_fusion
  62.8 0.1 copy.70
  63.0 0.1 reshape.70
  63.1 0.2 copy.69
  63.3 1.3 copy.67
  64.6 2.0 copy.77
  66.6 1.9 copy.75
  68.5 0.7 fusion.7
  69.2 1.2 copy-done.2
  70.4 0.3 fusion.10
  70.7 0.6 log_add_fusion
  71.3 0.3 reshape.82
  71.7 0.1 copy.84
  71.8 24.5 %all-gather.2.cloned.1.call-done = bf16[1,1024,2560]{2,1,0:T(8,128)(2,1)} async-done(((bf16[1,128,2560]{2,1,0:T(8,128)(2,1)}), bf16[1,1024,2560]{2,1,0:T(8,128)(2,1)}) %all-gather.2.cloned.1.call-update) | async-done | bytes 5242896 | tf_op jit(solution)/shard_map/all_gather | solution.py:51
  96.3 3.6 fusion.4
  99.9 0.4 copy-done.1
  100.3 2.6 fusion.17
  102.9 2.4 copy.72
  105.3 4.9 %reduce.4 = bf16[1024,160]{1,0:T(8,128)(2,1)} reduce(bf16[1024,1,160]{2,1,0:T(2,128)(2,1)S(1)} %bitcast.104, bf16[]{:T(256)} %broadcast.40), dimensions={1}, to_apply=%bitcast.88.reduce_sub_computation | reduce | bytes 655362
  110.1 2.6 reshape.79
  112.7 5.8 %all-to-all-start = ((bf16[8,2,10240]{2,1,0:T(2,128)(2,1)}), bf16[8,2,10240]{2,1,0:T(2,128)(2,1)S(1)}, u32[]{:S(2)}, u32[]{:S(2)}) async-start(bf16[8,2,10240]{2,1,0:T(2,128)(2,1)} %reshape.79), calls=%async_computation | async-start | bytes 655360 | tf_op jit(solution)/shard_map/all_to_all | solution.py:54
  118.5 307.2 %all-reduce.1 = bf16[160,2560]{1,0:T(8,128)(2,1)} all-reduce(f32[160,2560]{1,0:T(8,128)S(1)} %fusion.4), channel_id=1, replica_groups=mesh['dp'=8,'region'=64] {'region'}, use_global_device_ids=true, to_apply=%region_2.3 | all-reduce | flops 409600 | bytes 2457600 | tf_op jit(solution)/shard_map/psum | solution.py:60
  425.7 2.1 reshape.80
  427.8 1.4 copy.104
  429.2 0.3 copy.74
  429.5 0.9 copy.101
  430.4 1.8 fusion.46
  432.2 1.0 fusion.43
  433.1 2.1 collective-permute-start.8
  435.3 2.4 collective-permute-start.9
  437.7 0.1 fusion.33
  437.9 0.8 multiply_convert_fusion
  438.7 0.1 copy-done.8
  438.8 0.5 fusion.45
  439.3 0.8 fusion.44
  440.1 7.6 %collective-permute-start.6 = (bf16[128,8,160]{0,2,1:T(8,128)(2,1)}, bf16[128,8,160]{0,2,1:T(8,128)(2,1)}, u32[]{:S(2)}, u32[]{:S(2)}) collective-permute-start(bf16[128,8,160]{0,2,1:T(8,128)(2,1)} %get-tuple-element.22), channel_id=1, source_target_pairs={{0,63},{1,0},{2,1},{3,2},{4,3},{5,4},{6,5},{7,6},{8,7},{9,8},{10,9... | collective-permute-start | bytes 983048 | tf_op jit(solution)/shard_map/ppermute | solution.py:15
  447.7 1.9 collective-permute-start.7
  449.7 0.4 convolution_convert_fusion
  450.1 0.9 copy.85
  451.0 0.7 collective-permute-done.9
  451.7 1.4 fusion.30
  453.1 0.9 copy.87
  454.0 9.9 %collective-permute-done.7 = bf16[128,8,160]{0,2,1:T(8,128)(2,1)} collective-permute-done((bf16[128,8,160]{0,2,1:T(8,128)(2,1)S(1)}, bf16[128,8,160]{0,2,1:T(8,128)(2,1)}, u32[]{:S(2)}, u32[]{:S(2)}) %collective-permute-start.7) | collective-permute-done | bytes 327712 | tf_op jit(solution)/shard_map/ppermute | solution.py:15
  464.0 1.2 fusion.32
  465.1 0.9 copy.86
  (62 shorter events, 0.5 us)
Async XLA Ops:
  7.2 92.8 %copy-start = (bf16[160,2560]{1,0:T(8,128)(2,1)S(1)}, bf16[160,2560]{1,0:T(8,128)(2,1)}, u32[]{:S(2)}) copy-start(bf16[160,2560]{1,0:T(8,128)(2,1)} %param.13) | copy-start | bytes 2457604
  7.2 16.4 %copy-start.10 = (bf16[1,128,1280]{2,1,0:T(8,128)(2,1)S(1)}, bf16[1,128,1280]{2,1,0:T(8,128)(2,1)}, u32[]{:S(2)}) copy-start(bf16[1,128,1280]{2,1,0:T(8,128)(2,1)} %param.9) | copy-start | bytes 983044
  7.2 20.9 %copy-start.11 = (bf16[1,128,1280]{2,1,0:T(8,128)(2,1)S(1)}, bf16[1,128,1280]{2,1,0:T(8,128)(2,1)}, u32[]{:S(2)}) copy-start(bf16[1,128,1280]{2,1,0:T(8,128)(2,1)} %param.10) | copy-start | bytes 983044
  7.2 30.7 %copy-start.6 = (bf16[1,128,1280]{2,1,0:T(8,128)(2,1)S(1)}, bf16[1,128,1280]{2,1,0:T(8,128)(2,1)}, u32[]{:S(2)}) copy-start(bf16[1,128,1280]{2,1,0:T(8,128)(2,1)} %param.11) | copy-start | bytes 983044
  7.2 89.1 %all-gather.2.cloned.1.call-start = ((), (), s32[]{:S(2)}) async-start(), calls=%async_computation.2 | async-start | bytes 5898240 | tf_op jit(solution)/shard_map/all_gather | solution.py:51
  10.3 43.1 %collective-permute-start.3 = (bf16[128]{0:T(256)(128)(2,1)S(1)}, bf16[128]{0:T(256)(128)(2,1)S(1)}, u32[]{:S(2)}, u32[]{:S(2)}) collective-permute-start(bf16[128]{0:T(256)(128)(2,1)S(1)} %convert_element_type.56), channel_id=1, source_target_pairs={{0,63},{1,0},{2,1},{3,2},{4,3},{5,4},{6,5},{7,6},{8,7},{9,8},{10,9... | collective-permute-start | bytes 776 | tf_op jit(solution)/shard_map/ppermute | solution.py:15
  23.6 39.5 %collective-permute-start.1 = (bf16[128,1280]{1,0:T(8,128)(2,1)S(1)}, bf16[128,1280]{1,0:T(8,128)(2,1)S(1)}, u32[]{:S(2)}, u32[]{:S(2)}) collective-permute-start(bf16[128,1280]{1,0:T(8,128)(2,1)S(1)} %bitcast.119), channel_id=1, source_target_pairs={{0,63},{1,0},{2,1},{3,2},{4,3},{5,4},{6,5},{7,6},{8,7},{9,8},{10,9... | collective-permute-start | bytes 983048 | tf_op jit(solution)/shard_map/ppermute | solution.py:15
  26.1 37.1 %collective-permute-start = (bf16[128,1280]{1,0:T(8,128)(2,1)S(1)}, bf16[128,1280]{1,0:T(8,128)(2,1)}, u32[]{:S(2)}, u32[]{:S(2)}) collective-permute-start(bf16[128,1280]{1,0:T(8,128)(2,1)S(1)} %bitcast.120), channel_id=1, source_target_pairs={{0,1},{1,2},{2,3},{3,4},{4,5},{5,6},{6,7},{7,8},{8,9},{9,10},{10,1... | collective-permute-start | bytes 983048 | tf_op jit(solution)/shard_map/ppermute | solution.py:15
  28.1 36.5 %collective-permute-start.5 = (bf16[128,1280]{1,0:T(8,128)(2,1)S(1)}, bf16[128,1280]{1,0:T(8,128)(2,1)}, u32[]{:S(2)}, u32[]{:S(2)}) collective-permute-start(bf16[128,1280]{1,0:T(8,128)(2,1)S(1)} %bitcast.121), channel_id=1, source_target_pairs={{0,63},{1,0},{2,1},{3,2},{4,3},{5,4},{6,5},{7,6},{8,7},{9,8},{10,9... | collective-permute-start | bytes 983048 | tf_op jit(solution)/shard_map/ppermute | solution.py:15
  36.0 30.6 %collective-permute-start.4 = (bf16[128,1280]{1,0:T(8,128)(2,1)S(1)}, bf16[128,1280]{1,0:T(8,128)(2,1)}, u32[]{:S(2)}, u32[]{:S(2)}) collective-permute-start(bf16[128,1280]{1,0:T(8,128)(2,1)S(1)} %bitcast.122), channel_id=1, source_target_pairs={{0,1},{1,2},{2,3},{3,4},{4,5},{5,6},{6,7},{7,8},{8,9},{9,10},{10,1... | collective-permute-start | bytes 983048 | tf_op jit(solution)/shard_map/ppermute | solution.py:15
  46.5 10.9 %copy-start.9 = (bf16[1,128,1280]{2,1,0:T(8,128)(2,1)S(1)}, bf16[1,128,1280]{2,1,0:T(8,128)(2,1)}, u32[]{:S(2)}) copy-start(bf16[1,128,1280]{2,1,0:T(8,128)(2,1)} %param.8) | copy-start | bytes 983044
  47.3 15.3 %copy-start.22 = (s32[1,4,12]{2,1,0:T(4,128)S(1)}, s32[1,4,12]{2,1,0:T(4,128)}, u32[]{:S(2)}) copy-start(s32[1,4,12]{2,1,0:T(4,128)} %param.14) | copy-start | bytes 580
  47.3 23.9 %all-to-all-start.1 = ((bf16[8,2,10240]{2,1,0:T(2,128)(2,1)}), bf16[8,2,10240]{2,1,0:T(2,128)(2,1)S(1)}, u32[]{:S(2)}, u32[]{:S(2)}) async-start(bf16[8,2,10240]{2,1,0:T(2,128)(2,1)} %reshape.81), calls=%async_computation.1 | async-start | bytes 655360 | tf_op jit(solution)/shard_map/all_to_all | solution.py:52
  53.4 15.1 %copy-start.12 = (bf16[1,128,1280]{1,2,0:T(8,128)(2,1)}, bf16[1,128,1280]{1,2,0:T(8,128)(2,1)S(1)}, u32[]{:S(2)}) copy-start(bf16[1,128,1280]{1,2,0:T(8,128)(2,1)S(1)} %copy.68) | copy-start | bytes 983044
  53.4 9.1 %collective-permute-start.2 = (bf16[128]{0:T(256)(128)(2,1)S(1)}, bf16[128]{0:T(256)(128)(2,1)S(1)}, u32[]{:S(2)}, u32[]{:S(2)}) collective-permute-start(bf16[128]{0:T(256)(128)(2,1)S(1)} %convert_element_type.56), channel_id=1, source_target_pairs={{0,1},{1,2},{2,3},{3,4},{4,5},{5,6},{6,7},{7,8},{8,9},{9,10},{10,1... | collective-permute-start | bytes 776 | tf_op jit(solution)/shard_map/ppermute | solution.py:15
  57.6 11.6 %copy-start.7 = (bf16[1,128,1280]{1,2,0:T(8,128)(2,1)}, bf16[1,128,1280]{1,2,0:T(8,128)(2,1)S(1)}, u32[]{:S(2)}) copy-start(bf16[1,128,1280]{1,2,0:T(8,128)(2,1)S(1)} %copy.71) | copy-start | bytes 983044
  63.3 5.9 %copy-start.15 = (bf16[128,1280]{0,1:T(8,128)(2,1)}, bf16[128,1280]{0,1:T(8,128)(2,1)S(1)}, u32[]{:S(2)}) copy-start(bf16[128,1280]{0,1:T(8,128)(2,1)S(1)} %copy.69) | copy-start | bytes 983044
  64.6 4.6 copy-start.17
  69.2 1.2 copy-start.2
  96.3 4.0 copy-start.1
  112.7 313.0 %all-to-all-start = ((bf16[8,2,10240]{2,1,0:T(2,128)(2,1)}), bf16[8,2,10240]{2,1,0:T(2,128)(2,1)S(1)}, u32[]{:S(2)}, u32[]{:S(2)}) async-start(bf16[8,2,10240]{2,1,0:T(2,128)(2,1)} %reshape.79), calls=%async_computation | async-start | bytes 655360 | tf_op jit(solution)/shard_map/all_to_all | solution.py:54
  427.8 2.6 copy-start.3
  427.8 2.6 copy-start.21
  430.4 7.3 %copy-start.4 = (bf16[1,128,1280]{1,2,0:T(8,128)(2,1)S(1)}, bf16[1,128,1280]{1,2,0:T(8,128)(2,1)}, u32[]{:S(2)}) copy-start(bf16[1,128,1280]{1,2,0:T(8,128)(2,1)} %copy.102) | copy-start | bytes 983044
  430.4 7.3 %copy-start.5 = (bf16[8,128,160]{1,2,0:T(8,128)(2,1)S(1)}, bf16[8,128,160]{1,2,0:T(8,128)(2,1)}, u32[]{:S(2)}) copy-start(bf16[8,128,160]{1,2,0:T(8,128)(2,1)} %copy.101) | copy-start | bytes 983044
  432.2 5.6 %copy-start.14 = (bf16[1,128,1280]{1,2,0:T(8,128)(2,1)S(1)}, bf16[1,128,1280]{1,2,0:T(8,128)(2,1)}, u32[]{:S(2)}) copy-start(bf16[1,128,1280]{1,2,0:T(8,128)(2,1)} %copy.76) | copy-start | bytes 983044
  432.2 5.6 %copy-start.19 = (bf16[128,1280]{0,1:T(8,128)(2,1)S(1)}, bf16[128,1280]{0,1:T(8,128)(2,1)}, u32[]{:S(2)}) copy-start(bf16[128,1280]{0,1:T(8,128)(2,1)} %copy.77) | copy-start | bytes 983044
  432.2 5.7 %copy-start.20 = (bf16[128,1280]{0,1:T(8,128)(2,1)S(1)}, bf16[128,1280]{0,1:T(8,128)(2,1)}, u32[]{:S(2)}) copy-start(bf16[128,1280]{0,1:T(8,128)(2,1)} %copy.75) | copy-start | bytes 983044
  433.1 17.9 %collective-permute-start.8 = (bf16[128,8,160]{0,2,1:T(8,128)(2,1)}, bf16[128,8,160]{0,2,1:T(8,128)(2,1)}, u32[]{:S(2)}, u32[]{:S(2)}) collective-permute-start(bf16[128,8,160]{0,2,1:T(8,128)(2,1)} %get-tuple-element.20), channel_id=1, source_target_pairs={{0,63},{1,0},{2,1},{3,2},{4,3},{5,4},{6,5},{7,6},{8,7},{9,8},{10,9... | collective-permute-start | bytes 983048 | tf_op jit(solution)/shard_map/ppermute | solution.py:15
  435.3 16.4 %collective-permute-start.9 = (bf16[128,8,160]{0,2,1:T(8,128)(2,1)}, bf16[128,8,160]{0,2,1:T(8,128)(2,1)}, u32[]{:S(2)}, u32[]{:S(2)}) collective-permute-start(bf16[128,8,160]{0,2,1:T(8,128)(2,1)} %get-tuple-element.21), channel_id=1, source_target_pairs={{0,1},{1,2},{2,3},{3,4},{4,5},{5,6},{6,7},{7,8},{8,9},{9,10},{10,1... | collective-permute-start | bytes 983048 | tf_op jit(solution)/shard_map/ppermute | solution.py:15
  437.8 1.0 copy-start.8
  438.8 10.8 %copy-start.13 = (bf16[1,128,1280]{1,2,0:T(8,128)(2,1)S(1)}, bf16[1,128,1280]{1,2,0:T(8,128)(2,1)}, u32[]{:S(2)}) copy-start(bf16[1,128,1280]{1,2,0:T(8,128)(2,1)} %copy-done.12) | copy-start | bytes 983044
  438.8 10.8 %copy-start.16 = (bf16[128,1280]{0,1:T(8,128)(2,1)S(1)}, bf16[128,1280]{0,1:T(8,128)(2,1)}, u32[]{:S(2)}) copy-start(bf16[128,1280]{0,1:T(8,128)(2,1)} %copy-done.15) | copy-start | bytes 983044
  438.8 10.9 %copy-start.18 = (bf16[128,1280]{0,1:T(8,128)(2,1)S(1)}, bf16[128,1280]{0,1:T(8,128)(2,1)}, u32[]{:S(2)}) copy-start(bf16[128,1280]{0,1:T(8,128)(2,1)} %copy-done.17) | copy-start | bytes 983044
  440.1 13.9 %collective-permute-start.6 = (bf16[128,8,160]{0,2,1:T(8,128)(2,1)}, bf16[128,8,160]{0,2,1:T(8,128)(2,1)}, u32[]{:S(2)}, u32[]{:S(2)}) collective-permute-start(bf16[128,8,160]{0,2,1:T(8,128)(2,1)} %get-tuple-element.22), channel_id=1, source_target_pairs={{0,63},{1,0},{2,1},{3,2},{4,3},{5,4},{6,5},{7,6},{8,7},{9,8},{10,9... | collective-permute-start | bytes 983048 | tf_op jit(solution)/shard_map/ppermute | solution.py:15
  447.7 16.2 %collective-permute-start.7 = (bf16[128,8,160]{0,2,1:T(8,128)(2,1)S(1)}, bf16[128,8,160]{0,2,1:T(8,128)(2,1)}, u32[]{:S(2)}, u32[]{:S(2)}) collective-permute-start(bf16[128,8,160]{0,2,1:T(8,128)(2,1)S(1)} %get-tuple-element.23), channel_id=1, source_target_pairs={{0,1},{1,2},{2,3},{3,4},{4,5},{5,6},{6,7},{7,8},{8,9},{9,10},{10,1... | collective-permute-start | bytes 983048 | tf_op jit(solution)/shard_map/ppermute | solution.py:15
Sparse Core Ops, SparseCore 0:
  10.7 85.5 all-gather.1
where the time goes:
time: 474 us; the launch traced here: 473 us
  blocking collectives  307 us (65%)
  starting transfers between devices  55.4 us (12%)
  waiting for transfers between devices  40 us (8%)
  local copies, waits for them, and re-layouts  26.6 us (6%)
  other arithmetic  18.1 us (4%)
  between operations  15.3 us (3%)
  matrix products  10.4 us (2%)
    psum x1, blocking collectives, local(): d_weight = lax.psum(weight_part, 'region').astype(jnp.bfloat16)  307 us
    ppermute x10, starting transfers between devices, from_behind(): lax.ppermute(value, axis, [(i, (i + by) % length) for i in range(length)])  43.7 us
    all_gather x1, waiting for transfers between devices, local(): gathered = lax.all_gather(grads, 'dp', axis=1, tiled=True)  24.5 us
    unnamed x62, local copies, waits for them, and re-layouts  16 us
    ppermute x10, waiting for transfers between devices, from_behind(): lax.ppermute(value, axis, [(i, (i + by) % length) for i in range(length)])  15.5 us
    unnamed x2, other arithmetic  12.4 us
  transfers between devices with their start and end apart: 13, of which 4 were waited for; matrix products, arithmetic and copies ran while one was open for 5% of the time, Pallas kernels for 0%

commit v1 on v0

v1 whole, which is shorter than its diff:
```python
import functools
import math

import jax
import jax.numpy as jnp
from jax import lax
from jax.experimental import pallas as pl
from jax.experimental.pallas import tpu as pltpu
from jax.sharding import Mesh
from jax.sharding import PartitionSpec as P

HEADS = 8
HD = 160
BLK = 4
DP = ("z_lo", "x")
YZ = ("y", "z_hi")
REGION = ("y", "z_hi", "core")
BF = jnp.bfloat16
F32 = jnp.float32
LANES = 128
EXTRA = HD - LANES
SCALE = 1.0 / math.sqrt(HD)


def nn(a, b):
    return lax.dot_general(a, b, (((1,), (0,)), ((), ())), preferred_element_type=F32)


def nt(a, b):
    return lax.dot_general(a, b, (((1,), (1,)), ((), ())), preferred_element_type=F32)


def tn(a, b):
    return lax.dot_general(a, b, (((0,), (0,)), ((), ())), preferred_element_type=F32)


def pack(rows):
    low = rows[:, :LANES]
    high = rows[:, LANES:]
    below = jnp.concatenate([high[g * EXTRA : (g + 1) * EXTRA] for g in range(LANES // EXTRA)], 1)
    return jnp.concatenate([low, below], 0)


def unpack(tile):
    below = tile[LANES:]
    high = jnp.concatenate(
        [below[:, g * EXTRA : (g + 1) * EXTRA] for g in range(LANES // EXTRA)], 0
    )
    return jnp.concatenate([tile[:LANES], high], 1)


def head(ref, h):
    return ref[:, h * HD : (h + 1) * HD]


def prepare_body(counts, d_out, attn_out, keys, values, spread, out_cols, halo):
    rows, _ = d_out.shape
    live = lax.broadcasted_iota(jnp.int32, (rows, 1), 0) // (rows // BLK) < counts[0]
    grads = jnp.where(live, d_out[...], jnp.zeros((), BF))
    for s in range(spread.shape[0]):
        spread[s] = grads
    for h in range(HEADS):
        out_cols[h] = pack(head(attn_out, h))
    halo[0:rows] = keys[...]
    halo[rows : 2 * rows] = values[...]
    count = counts[0].astype(F32)
    halo[2 * rows :] = jnp.full((8, halo.shape[1]), count, F32).astype(BF)


def probs_body(counts, adjacency, queries, keys, behind, ahead, probs):
    rows = queries.shape[0]
    block = rows // BLK
    width = 3 * rows
    lane = lax.broadcasted_iota(jnp.int32, (1, width), 1)
    key_block = lane // block
    count = jnp.concatenate(
        [
            behind[2 * rows : 2 * rows + 1, :rows].astype(F32),
            jnp.full((1, rows), counts[0].astype(F32), F32),
            ahead[2 * rows : 2 * rows + 1, :rows].astype(F32),
        ],
        1,
    )
    live = (key_block % BLK).astype(F32) < count
    bias = []
    for a in range(BLK):
        seen = jnp.zeros((1, width), jnp.int32)
        for j in range(3 * BLK):
            seen = jnp.where(key_block == j, adjacency[a, j], seen)
        ok = jnp.logical_or(
            jnp.logical_and(seen == 1, live), key_block == BLK + a
        )
        bias.append(jnp.broadcast_to(jnp.where(ok, 1.0, 0.0), (block, width)))
    allowed = jnp.concatenate(bias, 0) > 0.5
    for h in range(HEADS):
        cols = slice(h * HD, (h + 1) * HD)
        window = jnp.concatenate([behind[0:rows, cols], keys[:, cols], ahead[0:rows, cols]], 0)
        scores = jnp.where(allowed, nt(queries[:, cols], window) * SCALE, -1e30)
        maxima = jnp.max(scores, axis=1, keepdims=True)
        terms = jnp.where(allowed, jnp.exp(scores - maxima), 0.0)
        probs[h] = terms / jnp.sum(terms, axis=1, keepdims=True)


def weight_body(out_cols, gathered, weight, acc):
    step = pl.program_id(0)
    samples, rows, width = gathered.shape
    cols = jnp.concatenate([unpack(out_cols[s]) for s in range(samples)], 0)
    part = tn(cols, gathered[...].reshape(samples * rows, width))

    @pl.when(step == 0)
    def _():
        acc[...] = part

    @pl.when(step > 0)
    def _():
        acc[...] += part

    @pl.when(step == pl.num_programs(0) - 1)
    def _():
        half = HD // 2
        for c in range(2):
            for j in range(width // LANES):
                weight[c, j] = acc[
                    c * half : (c + 1) * half, j * LANES : (j + 1) * LANES
                ].astype(BF)


def project_body(gathered, w_out, packed):
    samples, rows, width = gathered.shape
    part = nt(gathered[...].reshape(samples * rows, width), w_out[...])
    for s in range(samples):
        packed[s] = pack(part[s * rows : (s + 1) * rows]).astype(BF)


def attention_body(
    probs, packed, attn_out, queries, keys, values, behind, ahead,
    d_queries, own, to_behind, to_ahead,
):
    rows = queries.shape[0]
    for h in range(HEADS):
        cols = slice(h * HD, (h + 1) * HD)
        grad = unpack(packed[h])
        delta = jnp.sum(
            grad.astype(F32) * attn_out[:, cols].astype(F32), axis=1, keepdims=True
        )
        value_win = jnp.concatenate(
            [behind[rows : 2 * rows, cols], values[:, cols], ahead[rows : 2 * rows, cols]], 0
        )
        key_win = jnp.concatenate([behind[0:rows, cols], keys[:, cols], ahead[0:rows, cols]], 0)
        prob = probs[h]
        dprobs = nt(grad, value_win)
        dscores = (prob * (dprobs - delta) * SCALE).astype(BF)
        d_queries[:, cols] = nn(dscores, key_win).astype(BF)
        for which, (left, right) in enumerate(
            ((dscores, queries[:, cols]), (prob.astype(BF), grad))
        ):
            win = tn(left, right)
            to_behind[which, :, cols] = win[:rows].astype(BF)
            own[which, :, cols] = win[rows : 2 * rows]
            to_ahead[which, :, cols] = win[2 * rows :].astype(BF)


def finish_body(own, from_behind, from_ahead, d_keys, d_values):
    for which, out in enumerate((d_keys, d_values)):
        out[...] = (
            own[which] + from_behind[which].astype(F32) + from_ahead[which].astype(F32)
        ).astype(BF)


def vmem():
    return pl.BlockSpec(memory_space=pltpu.VMEM)


def smem():
    return pl.BlockSpec(memory_space=pltpu.SMEM)


def call(body, outs, specs, **options):
    return pl.pallas_call(
        body,
        out_shape=tuple(jax.ShapeDtypeStruct(shape, dtype) for shape, dtype in outs),
        in_specs=specs,
        out_specs=tuple(vmem() for _ in outs),
        compiler_params=pltpu.CompilerParams(vmem_limit_bytes=48 << 20),
        **options,
    )


def shift(value, by):
    length = lax.axis_size(REGION)
    return lax.ppermute(value, REGION, [(i, (i + by) % length) for i in range(length)])


def local(queries, keys, values, attn_out, d_out, w_out, adjacency, counts):
    queries, keys, values, attn_out, d_out = (
        a[0] for a in (queries, keys, values, attn_out, d_out)
    )
    rows, hw = queries.shape
    width = d_out.shape[1]
    samples = lax.axis_size(DP)
    tile = (samples, HD, LANES)
    spread, out_cols, halo = call(
        prepare_body,
        [((samples, rows, width), BF), (tile, BF), ((2 * rows + 8, hw), BF)],
        [smem(), vmem(), vmem(), vmem(), vmem()],
    )(counts, d_out, attn_out, keys, values)
    gathered = lax.all_to_all(spread, DP, 0, 0)
    out_cols = lax.all_to_all(out_cols, DP, 0, 0)
    behind = shift(halo, 1)
    ahead = shift(halo, -1)
    (probs,) = call(
        probs_body,
        [((HEADS, rows, 3 * rows), F32)],
        [smem(), smem(), vmem(), vmem(), vmem(), vmem()],
    )(counts, adjacency[0], queries, keys, behind, ahead)

    group = 2
    steps = samples // group
    halves = (2, width // LANES, HD // 2, LANES)
    weight = pl.pallas_call(
        weight_body,
        out_shape=jax.ShapeDtypeStruct(halves, BF),
        grid=(steps,),
        in_specs=[
            pl.BlockSpec((group, HD, LANES), lambda i: (i, 0, 0)),
            pl.BlockSpec((group, rows, width), lambda i: (i, 0, 0)),
        ],
        out_specs=pl.BlockSpec(halves, lambda i: (0, 0, 0, 0)),
        scratch_shapes=[pltpu.VMEM((HD, width), F32)],
        compiler_params=pltpu.CompilerParams(vmem_limit_bytes=48 << 20),
    )(out_cols, gathered)
    packed = pl.pallas_call(
        project_body,
        out_shape=jax.ShapeDtypeStruct(tile, BF),
        grid=(steps,),
        in_specs=[
            pl.BlockSpec((group, rows, width), lambda i: (i, 0, 0)),
            pl.BlockSpec((HD, width), lambda i: (0, 0)),
        ],
        out_specs=pl.BlockSpec((group, HD, LANES), lambda i: (i, 0, 0)),
        compiler_params=pltpu.CompilerParams(vmem_limit_bytes=48 << 20),
    )(gathered, w_out)
    packed = lax.all_to_all(packed, DP, 0, 0)

    members = lax.axis_size(YZ)
    flat = halves[1] * halves[2]
    share = -(-flat // (8 * members)) * 8
    pair = lax.all_to_all(weight, "core", 0, 0)
    half = jnp.sum(pair.astype(F32), axis=0).astype(BF).reshape(flat, LANES)
    half = jnp.pad(half, ((0, share * members - flat), (0, 0)))
    terms = lax.all_to_all(half.reshape(members, share, LANES), YZ, 0, 0)
    total = jnp.sum(terms.astype(F32), axis=0).astype(BF)
    total = lax.all_to_all(jnp.broadcast_to(total[None], (members, share, LANES)), YZ, 0, 0)
    total = total.reshape(members * share, LANES)[:flat]
    both = lax.all_to_all(jnp.broadcast_to(total[None], (2, flat, LANES)), "core", 0, 0)
    d_weight = both.reshape(halves).transpose(0, 2, 1, 3).reshape(HD, width)

    pairs = (2, rows, hw)
    d_queries, own, to_behind, to_ahead = call(
        attention_body,
        [((rows, hw), BF), (pairs, F32), (pairs, BF), (pairs, BF)],
        [vmem()] * 8,
    )(probs, packed, attn_out, queries, keys, values, behind, ahead)
    d_keys, d_values = call(
        finish_body, [((rows, hw), BF), ((rows, hw), BF)], [vmem()] * 3
    )(own, shift(to_ahead, 1), shift(to_behind, -1))
    return d_queries[None], d_keys[None], d_values[None], d_weight


def solution(mesh):
    parts = Mesh(mesh.devices.reshape(2, 4, 8, 4, 2), DP + REGION)
    rows = P(DP, REGION, None)
    return jax.shard_map(
        local,
        mesh=parts,
        in_specs=(rows, rows, rows, rows, rows, P(DP, None), P(REGION, None, None), P(REGION)),
        out_specs=(rows, rows, rows, P(DP, None)),
        check_vma=False,
    )
```

time: 474 us -> 210 us (0.44)
  the two profiles are of different devices: /device:TPU:6 before, /device:TPU:1 now
where the time goes in v1:
time: 210 us; the launch traced here: 208 us
  blocking collectives  87.1 us (41%)
  starting transfers between devices  45.5 us (22%)
  waiting for transfers between devices  42.4 us (20%)
  Pallas kernels  23.3 us (11%)
  local copies, waits for them, and re-layouts  8.2 us (4%)
    all_to_all x1, blocking collectives, local(): gathered = lax.all_to_all(spread, DP, 0, 0)  60.6 us
    ppermute x4, waiting for transfers between devices, shift(): lax.ppermute(value, REGION, [(i, (i + by) % length) for i in range(length)])  31.3 us
    ppermute x4, starting transfers between devices, shift(): lax.ppermute(value, REGION, [(i, (i + by) % length) for i in range(length)])  18.8 us
    all_to_all x1, starting transfers between devices, local(): terms = lax.all_to_all(half.reshape(members, share, LANES), YZ, 0, 0)  15.7 us
    all_to_all x1, blocking collectives, local(): out_cols = lax.all_to_all(out_cols, DP, 0, 0)  13 us
    all_to_all x1, waiting for transfers between devices, local(): terms = lax.all_to_all(half.reshape(members, share, LANES), YZ, 0, 0)  11.1 us
    all_to_all x1, blocking collectives, local(): pair = lax.all_to_all(weight, 'core', 0, 0)  9.46 us
    all_to_all x1, starting transfers between devices, local(): lax.all_to_all(jnp.broadcast_to(total[None], (members, share, LANES)), YZ...  7.59 us
  transfers between devices with their start and end apart: 7, of which 4 were waited for; matrix products, arithmetic and copies ran while one was open for 0% of the time, Pallas kernels for 7%

profile of v1, /device:TPU:1, one launch (start us, length us, event | category | flops | bytes accessed | tf_op | source)
XLA Modules:
  0.0 208.3 jit_solution(13492055042954477671)
XLA Ops:
  1.3 0.0 copy-start.1
  1.3 1.0 copy-done.1
  2.3 0.0 copy-start.4
  2.3 1.0 copy-done.4
  3.2 0.0 copy-start.6
  3.2 1.0 copy-done.6
  4.2 0.0 copy-start.9
  4.2 1.1 copy-done.9
  5.3 3.3 %shard_map.111 = (bf16[8,128,2560]{2,1,0:T(8,128)(2,1)}, bf16[8,160,128]{2,1,0:T(8,128)(2,1)S(1)}, bf16[264,1280]{1,0:T(8,128)(2,1)}) custom-call(s32[1]{0:T(128)S(6)} %copy.17.counts, bf16[128,2560]{1,0:T(8,128)(2,1)S(1)} %bitcast.29, bf16[128,1280]{1,0:T(8,128)(2,1)S(1)} %bitcast.25, bf16[128,1280]{1,0:T(8,128)(2,1)S(1)} %bitcast.20, ...), custom_call_target="tpu_custom_call" | custom-call | tf_op jit(solution)/shard_map/pallas_call | solution.py:202
  8.6 13.0 %all_to_all.35.out_cols = bf16[8,160,128]{2,1,0:T(8,128)(2,1)S(1)} all-to-all(bf16[8,160,128]{2,1,0:T(8,128)(2,1)S(1)} %get-tuple-element.21), channel_id=1, replica_groups=mesh['z_lo'=2,'x'=4,'y'=8,'z_hi'=4,'core'=2] {'z_lo','x'}, dimensions={0} | all-to-all | bytes 655360 | tf_op jit(solution)/shard_map/all_to_all | solution.py:208
  21.6 60.6 %all_to_all.36.gathered = bf16[8,128,2560]{2,1,0:T(8,128)(2,1)} all-to-all(bf16[8,128,2560]{2,1,0:T(8,128)(2,1)} %get-tuple-element.14), channel_id=1, replica_groups=mesh['z_lo'=2,'x'=4,'y'=8,'z_hi'=4,'core'=2] {'z_lo','x'}, dimensions={0} | all-to-all | bytes 10485760 | tf_op jit(solution)/shard_map/all_to_all | solution.py:207
  82.2 0.0 copy-start.8
  82.2 4.6 %shard_map.116 = bf16[2,20,80,128]{3,2,1,0:T(8,128)(2,1)S(1)} custom-call(bf16[8,160,128]{2,1,0:T(8,128)(2,1)S(1)} %all_to_all.35.out_cols, bf16[8,128,2560]{2,1,0:T(8,128)(2,1)} %all_to_all.36.gathered), custom_call_target="tpu_custom_call" | custom-call | tf_op jit(solution)/shard_map/pallas_call | solution.py:220
  86.9 9.5 %all_to_all.37 = bf16[2,20,80,128]{3,2,1,0:T(8,128)(2,1)S(1)} all-to-all(bf16[2,20,80,128]{3,2,1,0:T(8,128)(2,1)S(1)} %shard_map.116), channel_id=1, replica_groups=mesh['z_lo'=2,'x'=4,'y'=8,'z_hi'=4,'core'=2] {'core'}, dimensions={0} | all-to-all | bytes 1638400 | tf_op jit(solution)/shard_map/all_to_all | solution.py:248
  96.3 0.2 reduce_sum.24
  96.5 0.0 copy-start.2
  96.5 0.0 copy-start.3
  96.5 0.0 copy-start.10
  96.5 0.9 pad.4
  97.4 15.7 %all-to-all-start.4 = ((bf16[32,56,128]{2,1,0:T(8,128)(2,1)}), bf16[32,56,128]{2,1,0:T(8,128)(2,1)S(1)}, u32[]{:S(2)}, u32[]{:S(2)}) async-start(bf16[32,56,128]{2,1,0:T(8,128)(2,1)} %bitcast.10), calls=%async_computation.4 | async-start | bytes 917504 | tf_op jit(solution)/shard_map/all_to_all | solution.py:251
  113.1 0.0 copy-done.8
  113.1 0.0 copy-start.5
  113.1 0.0 copy-start.7
  113.1 5.2 %shard_map.113 = bf16[8,160,128]{2,1,0:T(8,128)(2,1)} custom-call(bf16[8,128,2560]{2,1,0:T(8,128)(2,1)} %all_to_all.36.gathered, bf16[160,2560]{1,0:T(8,128)(2,1)S(1)} %copy-done.8), custom_call_target="tpu_custom_call" | custom-call | tf_op jit(solution)/shard_map/pallas_call | solution.py:232
  118.3 11.1 %all-to-all-done.4 = bf16[32,56,128]{2,1,0:T(8,128)(2,1)S(1)} async-done(((bf16[32,56,128]{2,1,0:T(8,128)(2,1)}), bf16[32,56,128]{2,1,0:T(8,128)(2,1)S(1)}, u32[]{:S(2)}, u32[]{:S(2)}) %all-to-all-start.4) | async-done | bytes 458784 | tf_op jit(solution)/shard_map/all_to_all | solution.py:251
  129.5 3.4 %all-to-all-start.1 = ((bf16[8,160,128]{2,1,0:T(8,128)(2,1)}), bf16[8,160,128]{2,1,0:T(8,128)(2,1)S(1)}, u32[]{:S(2)}, u32[]{:S(2)}) async-start(bf16[8,160,128]{2,1,0:T(8,128)(2,1)} %shard_map.113), calls=%async_computation.1 | async-start | bytes 655360 | tf_op jit(solution)/shard_map/all_to_all | solution.py:243
  132.9 3.9 %collective-permute-start.1 = (bf16[264,1280]{1,0:T(8,128)(2,1)}, bf16[264,1280]{1,0:T(8,128)(2,1)S(1)}, u32[]{:S(2)}, u32[]{:S(2)}) collective-permute-start(bf16[264,1280]{1,0:T(8,128)(2,1)} %get-tuple-element.13), channel_id=1, source_target_pairs={{0,63},{1,0},{2,1},{3,2},{4,3},{5,4},{6,5},{7,6},{8,7},{9,8},{10,9... | collective-permute-start | bytes 2027528 | tf_op jit(solution)/shard_map/ppermute | solution.py:191
  136.8 3.1 %collective-permute-start = (bf16[264,1280]{1,0:T(8,128)(2,1)}, bf16[264,1280]{1,0:T(8,128)(2,1)S(1)}, u32[]{:S(2)}, u32[]{:S(2)}) collective-permute-start(bf16[264,1280]{1,0:T(8,128)(2,1)} %get-tuple-element.13), channel_id=1, source_target_pairs={{0,1},{1,2},{2,3},{3,4},{4,5},{5,6},{6,7},{7,8},{8,9},{9,10},{10,1... | collective-permute-start | bytes 2027528 | tf_op jit(solution)/shard_map/ppermute | solution.py:191
  139.9 0.1 reduce_sum.25
  140.0 0.0 all-to-all-done.1.packed
  140.0 0.8 broadcast_in_dim.24
  140.9 7.6 %all-to-all-start.5 = ((bf16[32,56,128]{2,1,0:T(8,128)(2,1)}), bf16[32,56,128]{2,1,0:T(8,128)(2,1)S(1)}, u32[]{:S(2)}, u32[]{:S(2)}) async-start(bf16[32,56,128]{2,1,0:T(8,128)(2,1)} %broadcast_in_dim.24), calls=%async_computation.5 | async-start | bytes 917504 | tf_op jit(solution)/shard_map/all_to_all | solution.py:253
  148.5 11.6 %collective-permute-done.1.ahead = bf16[264,1280]{1,0:T(8,128)(2,1)S(1)} collective-permute-done((bf16[264,1280]{1,0:T(8,128)(2,1)}, bf16[264,1280]{1,0:T(8,128)(2,1)S(1)}, u32[]{:S(2)}, u32[]{:S(2)}) %collective-permute-start.1) | collective-permute-done | bytes 675872 | tf_op jit(solution)/shard_map/ppermute | solution.py:191
  160.0 0.0 collective-permute-done.behind
  160.0 0.0 copy-done.2
  160.0 0.0 copy-done.3
  160.1 0.0 copy-done.10
  160.1 2.2 %shard_map.112.probs = f32[8,128,384]{2,1,0:T(8,128)S(1)} custom-call(s32[1]{0:T(128)S(6)} %copy.17.counts, s32[4,12]{1,0:T(4,128)S(1)} %bitcast.30, bf16[128,1280]{1,0:T(8,128)(2,1)S(1)} %bitcast.23, bf16[128,1280]{1,0:T(8,128)(2,1)S(1)} %bitcast.21, bf16[264,1280]{1,0:T(8,128)(2,1)S(1)} %collective-permute-done.behind, ...), custom_call_target="tpu_custom_call" | custom-call | tf_op jit(solution)/shard_map/pallas_call | solution.py:211
  162.3 0.0 copy-start
  162.3 1.2 copy-done
  163.5 0.0 copy-done.5
  163.5 0.0 copy-done.7
  163.5 7.0 %shard_map.114 = (bf16[128,1280]{1,0:T(8,128)(2,1)}, f32[2,128,1280]{2,1,0:T(8,128)S(1)}, bf16[2,128,1280]{2,1,0:T(8,128)(2,1)S(1)}, bf16[2,128,1280]{2,1,0:T(8,128)(2,1)S(1)}) custom-call(f32[8,128,384]{2,1,0:T(8,128)} %copy-done, bf16[8,160,128]{2,1,0:T(8,128)(2,1)S(1)} %all-to-all-done.1.packed, bf16[128,1280]{1,0:T(8,128)(2,1)S(1)} %bitcast.26, ...), custom_call_target="tpu_custom_call" | custom-call | tf_op jit(solution)/shard_map/pallas_call | solution.py:259
  170.5 9.9 %collective-permute-start.2 = (bf16[2,128,1280]{2,1,0:T(8,128)(2,1)S(1)}, bf16[2,128,1280]{2,1,0:T(8,128)(2,1)S(1)}, u32[]{:S(2)}, u32[]{:S(2)}) collective-permute-start(bf16[2,128,1280]{2,1,0:T(8,128)(2,1)S(1)} %get-tuple-element.17), channel_id=1, source_target_pairs={{0,1},{1,2},{2,3},{3,4},{4,5},{5,6},{6,7},{7,8},{8,9},{9,10},{10,1... | collective-permute-start | bytes 1966088 | tf_op jit(solution)/shard_map/ppermute | solution.py:191
  180.4 1.9 collective-permute-start.3
  182.3 12.7 %collective-permute-done.2.from_behind = bf16[2,128,1280]{2,1,0:T(8,128)(2,1)S(1)} collective-permute-done((bf16[2,128,1280]{2,1,0:T(8,128)(2,1)S(1)}, bf16[2,128,1280]{2,1,0:T(8,128)(2,1)S(1)}, u32[]{:S(2)}, u32[]{:S(2)}) %collective-permute-start.2) | collective-permute-done | bytes 655392 | tf_op jit(solution)/shard_map/ppermute | solution.py:191
  195.0 7.1 %collective-permute-done.3.from_ahead = bf16[2,128,1280]{2,1,0:T(8,128)(2,1)S(1)} collective-permute-done((bf16[2,128,1280]{2,1,0:T(8,128)(2,1)S(1)}, bf16[2,128,1280]{2,1,0:T(8,128)(2,1)S(1)}, u32[]{:S(2)}, u32[]{:S(2)}) %collective-permute-start.3) | collective-permute-done | bytes 655392 | tf_op jit(solution)/shard_map/ppermute | solution.py:191
  202.0 1.0 shard_map.115
  203.0 0.0 all-to-all-done.5
  203.0 0.1 broadcast_in_dim.25
  203.1 4.0 %all_to_all.38 = bf16[2,1600,128]{2,1,0:T(8,128)(2,1)S(1)} all-to-all(bf16[2,1600,128]{2,1,0:T(8,128)(2,1)S(1)} %broadcast_in_dim.25), channel_id=1, replica_groups=mesh['z_lo'=2,'x'=4,'y'=8,'z_hi'=4,'core'=2] {'core'}, dimensions={0} | all-to-all | bytes 1638400 | tf_op jit(solution)/shard_map/all_to_all | solution.py:255
  207.1 0.2 copy.13
  207.3 1.0 copy.16
  (1 shorter events, 0.0 us)
Async XLA Ops:
  1.3 1.0 copy-start.1
  2.3 1.0 copy-start.4
  3.2 1.0 copy-start.6
  4.2 1.1 copy-start.9
  82.2 30.9 %copy-start.8 = (bf16[160,2560]{1,0:T(8,128)(2,1)S(1)}, bf16[160,2560]{1,0:T(8,128)(2,1)}, u32[]{:S(2)}) copy-start(bf16[160,2560]{1,0:T(8,128)(2,1)} %w_out.1) | copy-start | bytes 2457604
  96.5 63.6 %copy-start.2 = (bf16[1,128,1280]{2,1,0:T(8,128)(2,1)S(1)}, bf16[1,128,1280]{2,1,0:T(8,128)(2,1)}, u32[]{:S(2)}) copy-start(bf16[1,128,1280]{2,1,0:T(8,128)(2,1)} %param.9) | copy-start | bytes 983044
  96.5 63.5 %copy-start.3 = (bf16[1,128,1280]{2,1,0:T(8,128)(2,1)S(1)}, bf16[1,128,1280]{2,1,0:T(8,128)(2,1)}, u32[]{:S(2)}) copy-start(bf16[1,128,1280]{2,1,0:T(8,128)(2,1)} %param.8) | copy-start | bytes 983044
  96.5 63.5 %copy-start.10 = (s32[1,4,12]{2,1,0:T(4,128)S(1)}, s32[1,4,12]{2,1,0:T(4,128)}, u32[]{:S(2)}) copy-start(s32[1,4,12]{2,1,0:T(4,128)} %param.14) | copy-start | bytes 580
  97.4 32.1 %all-to-all-start.4 = ((bf16[32,56,128]{2,1,0:T(8,128)(2,1)}), bf16[32,56,128]{2,1,0:T(8,128)(2,1)S(1)}, u32[]{:S(2)}, u32[]{:S(2)}) async-start(bf16[32,56,128]{2,1,0:T(8,128)(2,1)} %bitcast.10), calls=%async_computation.4 | async-start | bytes 917504 | tf_op jit(solution)/shard_map/all_to_all | solution.py:251
  113.1 50.4 %copy-start.5 = (bf16[1,128,1280]{2,1,0:T(8,128)(2,1)S(1)}, bf16[1,128,1280]{2,1,0:T(8,128)(2,1)}, u32[]{:S(2)}) copy-start(bf16[1,128,1280]{2,1,0:T(8,128)(2,1)} %param.11) | copy-start | bytes 983044
  113.1 50.4 %copy-start.7 = (bf16[1,128,1280]{2,1,0:T(8,128)(2,1)S(1)}, bf16[1,128,1280]{2,1,0:T(8,128)(2,1)}, u32[]{:S(2)}) copy-start(bf16[1,128,1280]{2,1,0:T(8,128)(2,1)} %param.10) | copy-start | bytes 983044
  129.5 10.5 %all-to-all-start.1 = ((bf16[8,160,128]{2,1,0:T(8,128)(2,1)}), bf16[8,160,128]{2,1,0:T(8,128)(2,1)S(1)}, u32[]{:S(2)}, u32[]{:S(2)}) async-start(bf16[8,160,128]{2,1,0:T(8,128)(2,1)} %shard_map.113), calls=%async_computation.1 | async-start | bytes 655360 | tf_op jit(solution)/shard_map/all_to_all | solution.py:243
  132.9 27.1 %collective-permute-start.1 = (bf16[264,1280]{1,0:T(8,128)(2,1)}, bf16[264,1280]{1,0:T(8,128)(2,1)S(1)}, u32[]{:S(2)}, u32[]{:S(2)}) collective-permute-start(bf16[264,1280]{1,0:T(8,128)(2,1)} %get-tuple-element.13), channel_id=1, source_target_pairs={{0,63},{1,0},{2,1},{3,2},{4,3},{5,4},{6,5},{7,6},{8,7},{9,8},{10,9... | collective-permute-start | bytes 2027528 | tf_op jit(solution)/shard_map/ppermute | solution.py:191
  136.8 23.2 %collective-permute-start = (bf16[264,1280]{1,0:T(8,128)(2,1)}, bf16[264,1280]{1,0:T(8,128)(2,1)S(1)}, u32[]{:S(2)}, u32[]{:S(2)}) collective-permute-start(bf16[264,1280]{1,0:T(8,128)(2,1)} %get-tuple-element.13), channel_id=1, source_target_pairs={{0,1},{1,2},{2,3},{3,4},{4,5},{5,6},{6,7},{7,8},{8,9},{9,10},{10,1... | collective-permute-start | bytes 2027528 | tf_op jit(solution)/shard_map/ppermute | solution.py:191
  140.9 62.1 %all-to-all-start.5 = ((bf16[32,56,128]{2,1,0:T(8,128)(2,1)}), bf16[32,56,128]{2,1,0:T(8,128)(2,1)S(1)}, u32[]{:S(2)}, u32[]{:S(2)}) async-start(bf16[32,56,128]{2,1,0:T(8,128)(2,1)} %broadcast_in_dim.24), calls=%async_computation.5 | async-start | bytes 917504 | tf_op jit(solution)/shard_map/all_to_all | solution.py:253
  162.3 1.2 copy-start
  170.5 24.5 %collective-permute-start.2 = (bf16[2,128,1280]{2,1,0:T(8,128)(2,1)S(1)}, bf16[2,128,1280]{2,1,0:T(8,128)(2,1)S(1)}, u32[]{:S(2)}, u32[]{:S(2)}) collective-permute-start(bf16[2,128,1280]{2,1,0:T(8,128)(2,1)S(1)} %get-tuple-element.17), channel_id=1, source_target_pairs={{0,1},{1,2},{2,3},{3,4},{4,5},{5,6},{6,7},{7,8},{8,9},{9,10},{10,1... | collective-permute-start | bytes 1966088 | tf_op jit(solution)/shard_map/ppermute | solution.py:191
  180.4 21.6 %collective-permute-start.3 = (bf16[2,128,1280]{2,1,0:T(8,128)(2,1)S(1)}, bf16[2,128,1280]{2,1,0:T(8,128)(2,1)S(1)}, u32[]{:S(2)}, u32[]{:S(2)}) collective-permute-start(bf16[2,128,1280]{2,1,0:T(8,128)(2,1)S(1)} %get-tuple-element.18), channel_id=1, source_target_pairs={{0,63},{1,0},{2,1},{3,2},{4,3},{5,4},{6,5},{7,6},{8,7},{9,8},{10,9... | collective-permute-start | bytes 1966088 | tf_op jit(solution)/shard_map/ppermute | solution.py:191

commit v2 on v1

--- a/solution.py
+++ b/solution.py
@@ -1,4 +1,3 @@
-import functools
 import math
 
 import jax
@@ -13,7 +12,6 @@
 HD = 160
 BLK = 4
 DP = ("z_lo", "x")
-YZ = ("y", "z_hi")
 REGION = ("y", "z_hi", "core")
 BF = jnp.bfloat16
 F32 = jnp.float32
@@ -53,18 +51,40 @@
     return ref[:, h * HD : (h + 1) * HD]
 
 
-def prepare_body(counts, d_out, attn_out, keys, values, spread, out_cols, halo):
-    rows, _ = d_out.shape
+def prepare_body(
+    counts, d_out, attn_out, keys, values, spread, halo,
+    grads_in, attn_in, sending, tail, sem_in, sem_out, sem_halo,
+):
+    rows, width = d_out.shape
+    loads = [
+        pltpu.make_async_copy(d_out, grads_in, sem_in.at[0]),
+        pltpu.make_async_copy(attn_out, attn_in, sem_in.at[1]),
+    ]
+    for copy in loads:
+        copy.start()
+    tail[...] = jnp.full(tail.shape, counts[0].astype(F32), F32).astype(BF)
+    moves = [
+        pltpu.make_async_copy(keys, halo.at[pl.ds(0, rows)], sem_halo.at[0]),
+        pltpu.make_async_copy(values, halo.at[pl.ds(rows, rows)], sem_halo.at[1]),
+        pltpu.make_async_copy(tail, halo.at[pl.ds(2 * rows, 8)], sem_halo.at[2]),
+    ]
+    loads[0].wait()
     live = lax.broadcasted_iota(jnp.int32, (rows, 1), 0) // (rows // BLK) < counts[0]
-    grads = jnp.where(live, d_out[...], jnp.zeros((), BF))
-    for s in range(spread.shape[0]):
-        spread[s] = grads
+    grads = jnp.where(live, grads_in[...], jnp.zeros((), BF))
+    for s in range(HEADS):
+        sending[s, 0:rows] = grads
+    loads[1].wait()
+    stores = []
     for h in range(HEADS):
-        out_cols[h] = pack(head(attn_out, h))
-    halo[0:rows] = keys[...]
-    halo[rows : 2 * rows] = values[...]
-    count = counts[0].astype(F32)
-    halo[2 * rows :] = jnp.full((8, halo.shape[1]), count, F32).astype(BF)
+        tile = pack(head(attn_in, h))
+        for j in range(width // LANES):
+            sending[h, rows : rows + 8, j * LANES : (j + 1) * LANES] = tile[8 * j : 8 * j + 8]
+        stores.append(pltpu.make_async_copy(sending.at[h], spread.at[h], sem_out.at[h]))
+        stores[h].start()
+    for copy in moves:
+        copy.start()
+    for copy in stores + moves:
+        copy.wait()
 
 
 def probs_body(counts, adjacency, queries, keys, behind, ahead, probs):
@@ -101,11 +121,17 @@
         probs[h] = terms / jnp.sum(terms, axis=1, keepdims=True)
 
 
-def weight_body(out_cols, gathered, weight, acc):
+def weight_body(gathered, weight, acc):
     step = pl.program_id(0)
-    samples, rows, width = gathered.shape
-    cols = jnp.concatenate([unpack(out_cols[s]) for s in range(samples)], 0)
-    part = tn(cols, gathered[...].reshape(samples * rows, width))
+    samples, _, width = gathered.shape
+    tiles = width // LANES
+    part = jnp.zeros(acc.shape, F32)
+    cols = []
+    for s in range(samples):
+        below = [gathered[s, LANES:, j * LANES : (j + 1) * LANES] for j in range(tiles)]
+        cols.append(unpack(jnp.concatenate(below, 0)))
+    grads = gathered[:, :LANES, :].reshape(samples * LANES, width)
+    part = tn(jnp.concatenate(cols, 0), grads)
 
     @pl.when(step == 0)
     def _():
@@ -119,17 +145,18 @@
     def _():
         half = HD // 2
         for c in range(2):
-            for j in range(width // LANES):
+            for j in range(tiles):
                 weight[c, j] = acc[
                     c * half : (c + 1) * half, j * LANES : (j + 1) * LANES
                 ].astype(BF)
 
 
 def project_body(gathered, w_out, packed):
-    samples, rows, width = gathered.shape
-    part = nt(gathered[...].reshape(samples * rows, width), w_out[...])
+    samples, _, width = gathered.shape
+    grads = gathered[:, :LANES, :].reshape(samples * LANES, width)
+    part = nt(grads, w_out[...])
     for s in range(samples):
-        packed[s] = pack(part[s * rows : (s + 1) * rows]).astype(BF)
+        packed[s] = pack(part[s * LANES : (s + 1) * LANES]).astype(BF)
 
 
 def attention_body(
@@ -175,14 +202,20 @@
     return pl.BlockSpec(memory_space=pltpu.SMEM)
 
 
-def call(body, outs, specs, **options):
+def hbm():
+    return pl.BlockSpec(memory_space=pltpu.HBM)
+
+
+PARAMS = pltpu.CompilerParams(vmem_limit_bytes=48 << 20)
+
+
+def call(body, outs, specs):
     return pl.pallas_call(
         body,
         out_shape=tuple(jax.ShapeDtypeStruct(shape, dtype) for shape, dtype in outs),
         in_specs=specs,
         out_specs=tuple(vmem() for _ in outs),
-        compiler_params=pltpu.CompilerParams(vmem_limit_bytes=48 << 20),
-        **options,
+        compiler_params=PARAMS,
     )
 
 
@@ -191,6 +224,10 @@
     return lax.ppermute(value, REGION, [(i, (i + by) % length) for i in range(length)])
 
 
+def spread_out(value, ways):
+    return jnp.broadcast_to(value[None], (ways,) + value.shape)
+
+
 def local(queries, keys, values, attn_out, d_out, w_out, adjacency, counts):
     queries, keys, values, attn_out, d_out = (
         a[0] for a in (queries, keys, values, attn_out, d_out)
@@ -198,14 +235,27 @@
     rows, hw = queries.shape
     width = d_out.shape[1]
     samples = lax.axis_size(DP)
-    tile = (samples, HD, LANES)
-    spread, out_cols, halo = call(
+    sent = (samples, rows + 8, width)
+    spread, halo = pl.pallas_call(
         prepare_body,
-        [((samples, rows, width), BF), (tile, BF), ((2 * rows + 8, hw), BF)],
-        [smem(), vmem(), vmem(), vmem(), vmem()],
+        out_shape=(
+            jax.ShapeDtypeStruct(sent, BF),
+            jax.ShapeDtypeStruct((2 * rows + 8, hw), BF),
+        ),
+        in_specs=[smem()] + [hbm()] * 4,
+        out_specs=(hbm(), hbm()),
+        scratch_shapes=[
+            pltpu.VMEM((rows, width), BF),
+            pltpu.VMEM((rows, hw), BF),
+            pltpu.VMEM(sent, BF),
+            pltpu.VMEM((8, hw), BF),
+            pltpu.SemaphoreType.DMA((2,)),
+            pltpu.SemaphoreType.DMA((samples,)),
+            pltpu.SemaphoreType.DMA((3,)),
+        ],
+        compiler_params=PARAMS,
     )(counts, d_out, attn_out, keys, values)
     gathered = lax.all_to_all(spread, DP, 0, 0)
-    out_cols = lax.all_to_all(out_cols, DP, 0, 0)
     behind = shift(halo, 1)
     ahead = shift(halo, -1)
     (probs,) = call(
@@ -213,46 +263,42 @@
         [((HEADS, rows, 3 * rows), F32)],
         [smem(), smem(), vmem(), vmem(), vmem(), vmem()],
     )(counts, adjacency[0], queries, keys, behind, ahead)
+    gathered, probs = lax.optimization_barrier((gathered, probs))
 
     group = 2
     steps = samples // group
     halves = (2, width // LANES, HD // 2, LANES)
+    rows_in = pl.BlockSpec((group, rows + 8, width), lambda i: (i, 0, 0))
     weight = pl.pallas_call(
         weight_body,
         out_shape=jax.ShapeDtypeStruct(halves, BF),
         grid=(steps,),
-        in_specs=[
-            pl.BlockSpec((group, HD, LANES), lambda i: (i, 0, 0)),
-            pl.BlockSpec((group, rows, width), lambda i: (i, 0, 0)),
-        ],
+        in_specs=[rows_in],
         out_specs=pl.BlockSpec(halves, lambda i: (0, 0, 0, 0)),
         scratch_shapes=[pltpu.VMEM((HD, width), F32)],
-        compiler_params=pltpu.CompilerParams(vmem_limit_bytes=48 << 20),
-    )(out_cols, gathered)
+        compiler_params=PARAMS,
+    )(gathered)
+    ways = lax.axis_size("y")
+    flat = halves[1] * halves[2]
+    pair = lax.all_to_all(weight, "core", 0, 0)
+    half = jnp.sum(pair.astype(F32), axis=0).astype(BF)
+    gathered, half = lax.optimization_barrier((gathered, half))
     packed = pl.pallas_call(
         project_body,
-        out_shape=jax.ShapeDtypeStruct(tile, BF),
+        out_shape=jax.ShapeDtypeStruct((samples, HD, LANES), BF),
         grid=(steps,),
-        in_specs=[
-            pl.BlockSpec((group, rows, width), lambda i: (i, 0, 0)),
-            pl.BlockSpec((HD, width), lambda i: (0, 0)),
-        ],
+        in_specs=[rows_in, pl.BlockSpec((HD, width), lambda i: (0, 0))],
         out_specs=pl.BlockSpec((group, HD, LANES), lambda i: (i, 0, 0)),
-        compiler_params=pltpu.CompilerParams(vmem_limit_bytes=48 << 20),
+        compiler_params=PARAMS,
     )(gathered, w_out)
+    terms = lax.all_to_all(half.reshape(ways, flat // ways, LANES), "y", 0, 0)
+    terms, packed = lax.optimization_barrier((terms, packed))
     packed = lax.all_to_all(packed, DP, 0, 0)
-
-    members = lax.axis_size(YZ)
-    flat = halves[1] * halves[2]
-    share = -(-flat // (8 * members)) * 8
-    pair = lax.all_to_all(weight, "core", 0, 0)
-    half = jnp.sum(pair.astype(F32), axis=0).astype(BF).reshape(flat, LANES)
-    half = jnp.pad(half, ((0, share * members - flat), (0, 0)))
-    terms = lax.all_to_all(half.reshape(members, share, LANES), YZ, 0, 0)
+    terms = jnp.sum(terms.astype(F32), axis=0).astype(BF)
+    terms = lax.all_to_all(spread_out(terms, lax.axis_size("z_hi")), "z_hi", 0, 0)
     total = jnp.sum(terms.astype(F32), axis=0).astype(BF)
-    total = lax.all_to_all(jnp.broadcast_to(total[None], (members, share, LANES)), YZ, 0, 0)
-    total = total.reshape(members * share, LANES)[:flat]
-    both = lax.all_to_all(jnp.broadcast_to(total[None], (2, flat, LANES)), "core", 0, 0)
+    total = lax.all_to_all(spread_out(total, ways), "y", 0, 0).reshape(flat, LANES)
+    both = lax.all_to_all(spread_out(total, 2), "core", 0, 0)
     d_weight = both.reshape(halves).transpose(0, 2, 1, 3).reshape(HD, width)
 
     pairs = (2, rows, hw)

time: 210 us -> 203 us (0.967)
  blocking collectives: 87.1 us -> 32.4 us
  waiting for transfers between devices: 42.4 us -> 92.9 us
  starting transfers between devices: 45.5 us -> 40.1 us
    all_to_all x3 -> x2, blocking collectives: 77.7 us -> 28.4 us  [the longest x1 18.4 us: local(): lax.all_to_all(spread_out(terms, lax.axis_size('z_hi')), 'z_hi', 0, 0)]
    ppermute x4, waiting for transfers between devices: 31.3 us -> 77.5 us  [shift(): lax.ppermute(value, REGION, [(i, (i + by) % length) for i in range(length)])]
    all_to_all x1, waiting for transfers between devices: 0.01 us -> 6.3 us  [local(): packed = lax.all_to_all(packed, DP, 0, 0)]
    all_to_all x2 -> x3, starting transfers between devices: 23.3 us -> 17.3 us  [the longest x1 7 us: local(): terms = lax.all_to_all(half.reshape(ways, flat // ways, LANES), 'y', 0, 0)]
    all_to_all x1, blocking collectives: 9.46 us -> 4.01 us  [local(): pair = lax.all_to_all(weight, 'core', 0, 0)]
    all_to_all x1, starting transfers between devices: 3.43 us -> 6.85 us  [local(): packed = lax.all_to_all(packed, DP, 0, 0)]
    ppermute x4, starting transfers between devices: 18.8 us -> 16 us  [shift(): lax.ppermute(value, REGION, [(i, (i + by) % length) for i in range(length)])]
    unnamed x23 -> x27, local copies, waits for them, and re-layouts: 6.2 us -> 8.42 us
  transfers between devices with their start and end apart: 7 -> 8, of which waited for: 4 -> 5; matrix products, arithmetic and copies ran while one was open for 0% -> 1% of each run, Pallas kernels for 7% -> 7%
where the time goes in v2:
time: 203 us; the launch traced here: 201 us
  waiting for transfers between devices  92.9 us (46%)
  starting transfers between devices  40.1 us (20%)
  blocking collectives  32.4 us (16%)
  Pallas kernels  24 us (12%)
  local copies, waits for them, and re-layouts  9.54 us (5%)
    ppermute x4, waiting for transfers between devices, shift(): lax.ppermute(value, REGION, [(i, (i + by) % length) for i in range(length)])  77.5 us
    all_to_all x1, blocking collectives, local(): lax.all_to_all(spread_out(terms, lax.axis_size('z_hi')), 'z_hi', 0, 0)  18.4 us
    ppermute x4, starting transfers between devices, shift(): lax.ppermute(value, REGION, [(i, (i + by) % length) for i in range(length)])  16 us
    all_to_all x1, blocking collectives, local(): both = lax.all_to_all(spread_out(total, 2), 'core', 0, 0)  9.95 us
    all_to_all x1, waiting for transfers between devices, local(): terms = lax.all_to_all(half.reshape(ways, flat // ways, LANES), 'y', 0, 0)  9.12 us
    unnamed x27, local copies, waits for them, and re-layouts  8.42 us
    pallas_call x1, Pallas kernels, local(): call(attention_body, [((rows, hw), BF), (pairs, F32), (pairs, BF), (pairs...  7.52 us
    all_to_all x1, starting transfers between devices, local(): terms = lax.all_to_all(half.reshape(ways, flat // ways, LANES), 'y', 0, 0)  7 us
  transfers between devices with their start and end apart: 8, of which 5 were waited for; matrix products, arithmetic and copies ran while one was open for 1% of the time, Pallas kernels for 7%

profile of v2, /device:TPU:1, one launch (start us, length us, event | category | flops | bytes accessed | tf_op | source)
XLA Modules:
  0.0 201.5 jit_solution(8569054345250249332)
XLA Ops:
  1.3 0.0 copy-start.1
  1.3 1.0 copy-done.1
  2.3 0.0 copy-start.4
  2.3 1.0 copy-done.4
  3.2 0.0 copy-start.6
  3.2 1.0 copy-done.6
  4.2 0.0 copy-start.11
  4.2 1.1 copy-done.11
  5.3 3.4 %shard_map.111 = (bf16[8,136,2560]{2,1,0:T(8,128)(2,1)}, bf16[264,1280]{1,0:T(8,128)(2,1)S(1)}) custom-call(s32[1]{0:T(128)S(6)} %copy.17.counts, bf16[128,2560]{1,0:T(8,128)(2,1)S(1)} %bitcast.28, bf16[128,1280]{1,0:T(8,128)(2,1)S(1)} %bitcast.24, bf16[128,1280]{1,0:T(8,128)(2,1)S(1)} %bitcast.19, bf16[128,1280]{1,0:T(8,128)(2,1)S(1)} %bitcast.26), custom_call_target="tpu_custom_call" | custom-call | tf_op jit(solution)/shard_map/pallas_call | solution.py:239
  8.7 0.0 copy-start.2
  8.7 0.0 copy-start.3
  8.7 0.0 copy-start.12
  8.7 6.8 %all-to-all-start = ((bf16[8,136,2560]{2,1,0:T(8,128)(2,1)}), bf16[8,136,2560]{2,1,0:T(8,128)(2,1)}, u32[]{:S(2)}, u32[]{:S(2)}) async-start(bf16[8,136,2560]{2,1,0:T(8,128)(2,1)} %get-tuple-element.18), calls=%async_computation | async-start | bytes 11141120 | tf_op jit(solution)/shard_map/all_to_all | solution.py:258
  15.5 6.8 %collective-permute-start.1 = (bf16[264,1280]{1,0:T(8,128)(2,1)S(1)}, bf16[264,1280]{1,0:T(8,128)(2,1)S(1)}, u32[]{:S(2)}, u32[]{:S(2)}) collective-permute-start(bf16[264,1280]{1,0:T(8,128)(2,1)S(1)} %get-tuple-element.19), channel_id=1, source_target_pairs={{0,63},{1,0},{2,1},{3,2},{4,3},{5,4},{6,5},{7,6},{8,7},{9,8},{10,9... | collective-permute-start | bytes 2027528 | tf_op jit(solution)/shard_map/ppermute | solution.py:224
  22.3 1.9 collective-permute-start
  24.3 8.0 %collective-permute-done.1.ahead = bf16[264,1280]{1,0:T(8,128)(2,1)S(1)} collective-permute-done((bf16[264,1280]{1,0:T(8,128)(2,1)S(1)}, bf16[264,1280]{1,0:T(8,128)(2,1)S(1)}, u32[]{:S(2)}, u32[]{:S(2)}) %collective-permute-start.1) | collective-permute-done | bytes 675872 | tf_op jit(solution)/shard_map/ppermute | solution.py:224
  32.3 58.2 %collective-permute-done.behind = bf16[264,1280]{1,0:T(8,128)(2,1)S(1)} collective-permute-done((bf16[264,1280]{1,0:T(8,128)(2,1)S(1)}, bf16[264,1280]{1,0:T(8,128)(2,1)S(1)}, u32[]{:S(2)}, u32[]{:S(2)}) %collective-permute-start) | collective-permute-done | bytes 675872 | tf_op jit(solution)/shard_map/ppermute | solution.py:224
  90.4 0.0 copy-done.2
  90.4 0.0 copy-done.3
  90.4 0.0 copy-done.12
  90.4 2.2 %shard_map.112.probs = f32[8,128,384]{2,1,0:T(8,128)S(1)} custom-call(s32[1]{0:T(128)S(6)} %copy.17.counts, s32[4,12]{1,0:T(4,128)S(1)} %bitcast.29, bf16[128,1280]{1,0:T(8,128)(2,1)S(1)} %bitcast.22, bf16[128,1280]{1,0:T(8,128)(2,1)S(1)} %bitcast.20, bf16[264,1280]{1,0:T(8,128)(2,1)S(1)} %collective-permute-done.behind, ...), custom_call_target="tpu_custom_call" | custom-call | tf_op jit(solution)/shard_map/pallas_call | solution.py:261
  92.7 0.0 copy-start
  92.7 1.2 copy-done
  93.9 0.0 all-to-all-done.gathered
  93.9 4.6 %shard_map.113 = bf16[2,20,80,128]{3,2,1,0:T(8,128)(2,1)S(1)} custom-call(bf16[8,136,2560]{2,1,0:T(8,128)(2,1)} %all-to-all-done.gathered), custom_call_target="tpu_custom_call" | custom-call | tf_op jit(solution)/shard_map/pallas_call | solution.py:272
  98.5 4.0 %all_to_all.35 = bf16[2,20,80,128]{3,2,1,0:T(8,128)(2,1)S(1)} all-to-all(bf16[2,20,80,128]{3,2,1,0:T(8,128)(2,1)S(1)} %shard_map.113), channel_id=1, replica_groups=mesh['z_lo'=2,'x'=4,'y'=8,'z_hi'=4,'core'=2] {'core'}, dimensions={0} | all-to-all | bytes 1638400 | tf_op jit(solution)/shard_map/all_to_all | solution.py:283
  102.5 1.0 reduce_sum.36
  103.5 0.0 copy-start.5
  103.5 0.0 copy-start.7
  103.5 7.0 %all-to-all-start.2 = ((bf16[8,200,128]{2,1,0:T(8,128)(2,1)}), bf16[8,200,128]{2,1,0:T(8,128)(2,1)S(1)}, u32[]{:S(2)}, u32[]{:S(2)}) async-start(bf16[8,200,128]{2,1,0:T(8,128)(2,1)} %bitcast.6), calls=%async_computation.2 | async-start | bytes 819200 | tf_op jit(solution)/shard_map/all_to_all | solution.py:294
  110.5 0.0 copy-start.10
  110.5 1.1 copy-done.10
  111.6 5.2 %shard_map.114 = bf16[8,160,128]{2,1,0:T(8,128)(2,1)} custom-call(bf16[8,136,2560]{2,1,0:T(8,128)(2,1)} %all-to-all-done.gathered, bf16[160,2560]{1,0:T(8,128)(2,1)S(1)} %copy-done.10), custom_call_target="tpu_custom_call" | custom-call | tf_op jit(solution)/shard_map/pallas_call | solution.py:286
  116.9 9.1 %all-to-all-done.2 = bf16[8,200,128]{2,1,0:T(8,128)(2,1)S(1)} async-done(((bf16[8,200,128]{2,1,0:T(8,128)(2,1)}), bf16[8,200,128]{2,1,0:T(8,128)(2,1)S(1)}, u32[]{:S(2)}, u32[]{:S(2)}) %all-to-all-start.2) | async-done | bytes 409632 | tf_op jit(solution)/shard_map/all_to_all | solution.py:294
  126.0 0.1 reduce_sum.37
  126.1 18.4 %all_to_all.36 = bf16[4,200,128]{2,1,0:T(8,128)(2,1)S(1)} all-to-all(bf16[4,200,128]{2,1,0:T(8,128)(2,1)S(1)} %broadcast_in_dim.31), channel_id=1, replica_groups=mesh['z_lo'=2,'x'=4,'y'=8,'z_hi'=4,'core'=2] {'z_hi'}, dimensions={0} | all-to-all | bytes 409600 | tf_op jit(solution)/shard_map/all_to_all | solution.py:298
  144.5 6.8 %all-to-all-start.3 = ((bf16[8,160,128]{2,1,0:T(8,128)(2,1)}), bf16[8,160,128]{2,1,0:T(8,128)(2,1)S(1)}, u32[]{:S(2)}, u32[]{:S(2)}) async-start(bf16[8,160,128]{2,1,0:T(8,128)(2,1)} %shard_map.114), calls=%async_computation.3 | async-start | bytes 655360 | tf_op jit(solution)/shard_map/all_to_all | solution.py:296
  151.4 6.3 %all-to-all-done.3.packed = bf16[8,160,128]{2,1,0:T(8,128)(2,1)S(1)} async-done(((bf16[8,160,128]{2,1,0:T(8,128)(2,1)}), bf16[8,160,128]{2,1,0:T(8,128)(2,1)S(1)}, u32[]{:S(2)}, u32[]{:S(2)}) %all-to-all-start.3) | async-done | bytes 327712 | tf_op jit(solution)/shard_map/all_to_all | solution.py:296
  157.7 0.8 broadcast_in_dim.32
  158.5 3.5 %all-to-all-start.5 = ((bf16[8,200,128]{2,1,0:T(8,128)(2,1)}), bf16[8,200,128]{2,1,0:T(8,128)(2,1)S(1)}, u32[]{:S(2)}, u32[]{:S(2)}) async-start(bf16[8,200,128]{2,1,0:T(8,128)(2,1)} %broadcast_in_dim.32), calls=%async_computation.5 | async-start | bytes 819200 | tf_op jit(solution)/shard_map/all_to_all | solution.py:300
  162.0 0.0 copy-done.5
  162.0 0.0 copy-done.7
  162.0 7.5 %shard_map.115 = (bf16[128,1280]{1,0:T(8,128)(2,1)}, f32[2,128,1280]{2,1,0:T(8,128)S(1)}, bf16[2,128,1280]{2,1,0:T(8,128)(2,1)}, bf16[2,128,1280]{2,1,0:T(8,128)(2,1)}) custom-call(f32[8,128,384]{2,1,0:T(8,128)} %copy-done, bf16[8,160,128]{2,1,0:T(8,128)(2,1)S(1)} %all-to-all-done.3.packed, bf16[128,1280]{1,0:T(8,128)(2,1)S(1)} %bitcast.25, ...), custom_call_target="tpu_custom_call" | custom-call | tf_op jit(solution)/shard_map/pallas_call | solution.py:305
  169.5 0.0 copy-start.8
  169.5 1.1 copy-done.8
  170.6 0.0 copy-start.9
  170.6 5.3 %collective-permute-start.2 = (bf16[2,128,1280]{2,1,0:T(8,128)(2,1)}, bf16[2,128,1280]{2,1,0:T(8,128)(2,1)S(1)}, u32[]{:S(2)}, u32[]{:S(2)}) collective-permute-start(bf16[2,128,1280]{2,1,0:T(8,128)(2,1)} %get-tuple-element.27), channel_id=1, source_target_pairs={{0,1},{1,2},{2,3},{3,4},{4,5},{5,6},{6,7},{7,8},{8,9},{9,10},{10,1... | collective-permute-start | bytes 1966088 | tf_op jit(solution)/shard_map/ppermute | solution.py:224
  175.9 2.0 collective-permute-start.3
  177.9 0.0 all-to-all-done.5
  177.9 0.1 broadcast_in_dim.34
  178.0 10.0 %all_to_all.37 = bf16[2,1600,128]{2,1,0:T(8,128)(2,1)S(1)} all-to-all(bf16[2,1600,128]{2,1,0:T(8,128)(2,1)S(1)} %broadcast_in_dim.34), channel_id=1, replica_groups=mesh['z_lo'=2,'x'=4,'y'=8,'z_hi'=4,'core'=2] {'core'}, dimensions={0} | all-to-all | bytes 1638400 | tf_op jit(solution)/shard_map/all_to_all | solution.py:301
  187.9 0.2 copy.13
  188.2 1.0 copy.16
  189.2 0.0 collective-permute-done.2.from_behind
  189.2 11.3 %collective-permute-done.3.from_ahead = bf16[2,128,1280]{2,1,0:T(8,128)(2,1)S(1)} collective-permute-done((bf16[2,128,1280]{2,1,0:T(8,128)(2,1)}, bf16[2,128,1280]{2,1,0:T(8,128)(2,1)S(1)}, u32[]{:S(2)}, u32[]{:S(2)}) %collective-permute-start.3) | collective-permute-done | bytes 655392 | tf_op jit(solution)/shard_map/ppermute | solution.py:224
  200.5 0.0 copy-done.9
  200.5 1.0 shard_map.116
  (2 shorter events, 0.1 us)
Async XLA Ops:
  1.3 1.0 copy-start.1
  2.3 1.0 copy-start.4
  3.2 1.0 copy-start.6
  4.2 1.1 copy-start.11
  8.7 81.8 %copy-start.2 = (bf16[1,128,1280]{2,1,0:T(8,128)(2,1)S(1)}, bf16[1,128,1280]{2,1,0:T(8,128)(2,1)}, u32[]{:S(2)}) copy-start(bf16[1,128,1280]{2,1,0:T(8,128)(2,1)} %param.9) | copy-start | bytes 983044
  8.7 81.8 %copy-start.3 = (bf16[1,128,1280]{2,1,0:T(8,128)(2,1)S(1)}, bf16[1,128,1280]{2,1,0:T(8,128)(2,1)}, u32[]{:S(2)}) copy-start(bf16[1,128,1280]{2,1,0:T(8,128)(2,1)} %param.8) | copy-start | bytes 983044
  8.7 81.8 %copy-start.12 = (s32[1,4,12]{2,1,0:T(4,128)S(1)}, s32[1,4,12]{2,1,0:T(4,128)}, u32[]{:S(2)}) copy-start(s32[1,4,12]{2,1,0:T(4,128)} %param.14) | copy-start | bytes 580
  8.7 85.2 %all-to-all-start = ((bf16[8,136,2560]{2,1,0:T(8,128)(2,1)}), bf16[8,136,2560]{2,1,0:T(8,128)(2,1)}, u32[]{:S(2)}, u32[]{:S(2)}) async-start(bf16[8,136,2560]{2,1,0:T(8,128)(2,1)} %get-tuple-element.18), calls=%async_computation | async-start | bytes 11141120 | tf_op jit(solution)/shard_map/all_to_all | solution.py:258
  15.5 16.8 %collective-permute-start.1 = (bf16[264,1280]{1,0:T(8,128)(2,1)S(1)}, bf16[264,1280]{1,0:T(8,128)(2,1)S(1)}, u32[]{:S(2)}, u32[]{:S(2)}) collective-permute-start(bf16[264,1280]{1,0:T(8,128)(2,1)S(1)} %get-tuple-element.19), channel_id=1, source_target_pairs={{0,63},{1,0},{2,1},{3,2},{4,3},{5,4},{6,5},{7,6},{8,7},{9,8},{10,9... | collective-permute-start | bytes 2027528 | tf_op jit(solution)/shard_map/ppermute | solution.py:224
  22.3 68.1 %collective-permute-start = (bf16[264,1280]{1,0:T(8,128)(2,1)S(1)}, bf16[264,1280]{1,0:T(8,128)(2,1)S(1)}, u32[]{:S(2)}, u32[]{:S(2)}) collective-permute-start(bf16[264,1280]{1,0:T(8,128)(2,1)S(1)} %get-tuple-element.19), channel_id=1, source_target_pairs={{0,1},{1,2},{2,3},{3,4},{4,5},{5,6},{6,7},{7,8},{8,9},{9,10},{10,1... | collective-permute-start | bytes 2027528 | tf_op jit(solution)/shard_map/ppermute | solution.py:224
  92.7 1.2 copy-start
  103.5 58.5 %copy-start.5 = (bf16[1,128,1280]{2,1,0:T(8,128)(2,1)S(1)}, bf16[1,128,1280]{2,1,0:T(8,128)(2,1)}, u32[]{:S(2)}) copy-start(bf16[1,128,1280]{2,1,0:T(8,128)(2,1)} %param.11) | copy-start | bytes 983044
  103.5 58.5 %copy-start.7 = (bf16[1,128,1280]{2,1,0:T(8,128)(2,1)S(1)}, bf16[1,128,1280]{2,1,0:T(8,128)(2,1)}, u32[]{:S(2)}) copy-start(bf16[1,128,1280]{2,1,0:T(8,128)(2,1)} %param.10) | copy-start | bytes 983044
  103.5 22.5 %all-to-all-start.2 = ((bf16[8,200,128]{2,1,0:T(8,128)(2,1)}), bf16[8,200,128]{2,1,0:T(8,128)(2,1)S(1)}, u32[]{:S(2)}, u32[]{:S(2)}) async-start(bf16[8,200,128]{2,1,0:T(8,128)(2,1)} %bitcast.6), calls=%async_computation.2 | async-start | bytes 819200 | tf_op jit(solution)/shard_map/all_to_all | solution.py:294
  110.5 1.1 copy-start.10
  144.5 13.2 %all-to-all-start.3 = ((bf16[8,160,128]{2,1,0:T(8,128)(2,1)}), bf16[8,160,128]{2,1,0:T(8,128)(2,1)S(1)}, u32[]{:S(2)}, u32[]{:S(2)}) async-start(bf16[8,160,128]{2,1,0:T(8,128)(2,1)} %shard_map.114), calls=%async_computation.3 | async-start | bytes 655360 | tf_op jit(solution)/shard_map/all_to_all | solution.py:296
  158.5 19.4 %all-to-all-start.5 = ((bf16[8,200,128]{2,1,0:T(8,128)(2,1)}), bf16[8,200,128]{2,1,0:T(8,128)(2,1)S(1)}, u32[]{:S(2)}, u32[]{:S(2)}) async-start(bf16[8,200,128]{2,1,0:T(8,128)(2,1)} %broadcast_in_dim.32), calls=%async_computation.5 | async-start | bytes 819200 | tf_op jit(solution)/shard_map/all_to_all | solution.py:300
  169.5 1.1 copy-start.8
  170.6 29.9 %copy-start.9 = (f32[2,128,1280]{2,1,0:T(8,128)S(1)}, f32[2,128,1280]{2,1,0:T(8,128)}, u32[]{:S(2)}) copy-start(f32[2,128,1280]{2,1,0:T(8,128)} %copy-done.8) | copy-start | bytes 3932164
  170.6 18.6 %collective-permute-start.2 = (bf16[2,128,1280]{2,1,0:T(8,128)(2,1)}, bf16[2,128,1280]{2,1,0:T(8,128)(2,1)S(1)}, u32[]{:S(2)}, u32[]{:S(2)}) collective-permute-start(bf16[2,128,1280]{2,1,0:T(8,128)(2,1)} %get-tuple-element.27), channel_id=1, source_target_pairs={{0,1},{1,2},{2,3},{3,4},{4,5},{5,6},{6,7},{7,8},{8,9},{9,10},{10,1... | collective-permute-start | bytes 1966088 | tf_op jit(solution)/shard_map/ppermute | solution.py:224
  175.9 24.6 %collective-permute-start.3 = (bf16[2,128,1280]{2,1,0:T(8,128)(2,1)}, bf16[2,128,1280]{2,1,0:T(8,128)(2,1)S(1)}, u32[]{:S(2)}, u32[]{:S(2)}) collective-permute-start(bf16[2,128,1280]{2,1,0:T(8,128)(2,1)} %get-tuple-element.28), channel_id=1, source_target_pairs={{0,63},{1,0},{2,1},{3,2},{4,3},{5,4},{6,5},{7,6},{8,7},{9,8},{10,9... | collective-permute-start | bytes 1966088 | tf_op jit(solution)/shard_map/ppermute | solution.py:224

commit v3 on v2

v3 whole, which is shorter than its diff:
```python
import math

import jax
import jax.numpy as jnp
from jax import lax
from jax.experimental import pallas as pl
from jax.experimental.pallas import tpu as pltpu
from jax.sharding import Mesh
from jax.sharding import PartitionSpec as P

HEADS = 8
HD = 160
BLK = 4
DP = ("z_lo", "x")
REGION = ("y", "z_hi", "core")
BF = jnp.bfloat16
F32 = jnp.float32
LANES = 128
SCALE = 1.0 / math.sqrt(HD)


def nn(a, b):
    return lax.dot_general(a, b, (((1,), (0,)), ((), ())), preferred_element_type=F32)


def nt(a, b):
    return lax.dot_general(a, b, (((1,), (1,)), ((), ())), preferred_element_type=F32)


def tn(a, b):
    return lax.dot_general(a, b, (((0,), (0,)), ((), ())), preferred_element_type=F32)


def prepare_body(
    counts, d_out, attn_out, keys, values, spread, grads, halo,
    grads_in, tail, sem_in, sem_attn, sem_out, sem_halo,
):
    rows, width = d_out.shape
    samples, _, part = spread.shape
    load = pltpu.make_async_copy(d_out, grads_in, sem_in.at[0])
    load.start()
    copies = []
    down = width // part
    for s in range(samples):
        half = pl.ds(s // down * part, part)
        copies.append(
            pltpu.make_async_copy(
                attn_out.at[:, half], spread.at[s, pl.ds(0, rows)], sem_attn.at[s]
            )
        )
    tail[...] = jnp.full(tail.shape, counts[0].astype(F32), F32).astype(BF)
    copies += [
        pltpu.make_async_copy(keys, halo.at[pl.ds(0, rows)], sem_halo.at[0]),
        pltpu.make_async_copy(values, halo.at[pl.ds(rows, rows)], sem_halo.at[1]),
        pltpu.make_async_copy(tail, halo.at[pl.ds(2 * rows, 8)], sem_halo.at[2]),
    ]
    for copy in copies:
        copy.start()
    load.wait()
    live = lax.broadcasted_iota(jnp.int32, (rows, 1), 0) // (rows // BLK) < counts[0]
    grads_in[...] = jnp.where(live, grads_in[...], jnp.zeros((), BF))
    stores = [pltpu.make_async_copy(grads_in, grads, sem_in.at[1])]
    for s in range(samples):
        quarter = pl.ds(s % down * part, part)
        stores.append(
            pltpu.make_async_copy(
                grads_in.at[:, quarter], spread.at[s, pl.ds(rows, rows)], sem_out.at[s]
            )
        )
    for copy in stores:
        copy.start()
    for copy in copies + stores:
        copy.wait()


def probs_body(counts, adjacency, queries, keys, behind, ahead, probs):
    rows = queries.shape[0]
    block = rows // BLK
    width = 3 * rows
    lane = lax.broadcasted_iota(jnp.int32, (1, width), 1)
    key_block = lane // block
    count = jnp.concatenate(
        [
            behind[2 * rows : 2 * rows + 1, :rows].astype(F32),
            jnp.full((1, rows), counts[0].astype(F32), F32),
            ahead[2 * rows : 2 * rows + 1, :rows].astype(F32),
        ],
        1,
    )
    live = (key_block % BLK).astype(F32) < count
    bias = []
    for a in range(BLK):
        seen = jnp.zeros((1, width), jnp.int32)
        for j in range(3 * BLK):
            seen = jnp.where(key_block == j, adjacency[a, j], seen)
        ok = jnp.logical_or(jnp.logical_and(seen == 1, live), key_block == BLK + a)
        bias.append(jnp.broadcast_to(jnp.where(ok, 1.0, 0.0), (block, width)))
    allowed = jnp.concatenate(bias, 0) > 0.5
    for h in range(HEADS):
        cols = slice(h * HD, (h + 1) * HD)
        window = jnp.concatenate([behind[0:rows, cols], keys[:, cols], ahead[0:rows, cols]], 0)
        scores = jnp.where(allowed, nt(queries[:, cols], window) * SCALE, -1e30)
        maxima = jnp.max(scores, axis=1, keepdims=True)
        terms = jnp.where(allowed, jnp.exp(scores - maxima), 0.0)
        probs[h] = terms / jnp.sum(terms, axis=1, keepdims=True)


def weight_body(gathered, weight, acc):
    step = pl.program_id(0)
    samples, both, part = gathered.shape
    cores, chips, heads, share, _ = weight.shape
    rows = both // 2
    left = gathered[:, :rows, :].reshape(samples * rows, part)
    right = gathered[:, rows:, :].reshape(samples * rows, part)
    term = tn(left, right)

    @pl.when(step == 0)
    def _():
        acc[...] = term

    @pl.when(step > 0)
    def _():
        acc[...] += term

    @pl.when(step == pl.num_programs(0) - 1)
    def _():
        half = HD // cores
        tiles = part // LANES
        for c in range(cores):
            for h in range(heads):
                first = h * HD + c * half
                pieces = [
                    acc[first : first + half, j * LANES : (j + 1) * LANES] for j in range(tiles)
                ]
                pieces.append(jnp.zeros((chips * share - tiles * half, LANES), F32))
                flat = jnp.concatenate(pieces, 0).reshape(chips, share, LANES)
                for m in range(chips):
                    weight[c, m, h] = flat[m].astype(BF)


def assemble_body(both, d_weight):
    cores, chips, quarters, _, _ = both.shape
    half = HD // cores
    part = d_weight.shape[1] // quarters
    for c in range(cores):
        for q in range(quarters):
            flat = jnp.concatenate([both[c, m, q].astype(F32) for m in range(chips)], 0)
            for j in range(part // LANES):
                first = q * part + j * LANES
                d_weight[c * half : (c + 1) * half, first : first + LANES] = flat[
                    j * half : (j + 1) * half
                ].astype(BF)


def attention_body(
    w_all, probs, grads, attn_out, queries, keys, values, behind, ahead,
    d_queries, own, to_behind, to_ahead, w_in, sem,
):
    rows = queries.shape[0]
    loads = [pltpu.make_async_copy(w_all.at[h], w_in.at[h], sem.at[h]) for h in range(HEADS)]
    for load in loads:
        load.start()
    for h in range(HEADS):
        cols = slice(h * HD, (h + 1) * HD)
        loads[h].wait()
        grad = nt(grads[...], w_in[h]).astype(BF)
        delta = jnp.sum(
            grad.astype(F32) * attn_out[:, cols].astype(F32), axis=1, keepdims=True
        )
        value_win = jnp.concatenate(
            [behind[rows : 2 * rows, cols], values[:, cols], ahead[rows : 2 * rows, cols]], 0
        )
        key_win = jnp.concatenate([behind[0:rows, cols], keys[:, cols], ahead[0:rows, cols]], 0)
        prob = probs[h]
        dprobs = nt(grad, value_win)
        dscores = (prob * (dprobs - delta) * SCALE).astype(BF)
        d_queries[:, cols] = nn(dscores, key_win).astype(BF)
        for which, (left, right) in enumerate(
            ((dscores, queries[:, cols]), (prob.astype(BF), grad))
        ):
            win = tn(left, right)
            to_behind[which, :, cols] = win[:rows].astype(BF)
            own[which, :, cols] = win[rows : 2 * rows]
            to_ahead[which, :, cols] = win[2 * rows :].astype(BF)


def finish_body(own, from_behind, from_ahead, d_keys, d_values):
    for which, out in enumerate((d_keys, d_values)):
        out[...] = (
            own[which] + from_behind[which].astype(F32) + from_ahead[which].astype(F32)
        ).astype(BF)


def vmem():
    return pl.BlockSpec(memory_space=pltpu.VMEM)


def smem():
    return pl.BlockSpec(memory_space=pltpu.SMEM)


def hbm():
    return pl.BlockSpec(memory_space=pltpu.HBM)


def in_hbm(value):
    return pltpu.with_memory_space_constraint(value, pltpu.HBM)


PARAMS = pltpu.CompilerParams(vmem_limit_bytes=28 << 20)


def call(body, outs, specs, scratch=()):
    return pl.pallas_call(
        body,
        out_shape=tuple(jax.ShapeDtypeStruct(shape, dtype) for shape, dtype in outs),
        in_specs=specs,
        out_specs=tuple(vmem() for _ in outs),
        scratch_shapes=scratch,
        compiler_params=PARAMS,
    )


def shift(value, by):
    length = lax.axis_size(REGION)
    return lax.ppermute(value, REGION, [(i, (i + by) % length) for i in range(length)])


def spread_out(value, ways):
    return jnp.broadcast_to(value[None], (ways,) + value.shape)


def local(queries, keys, values, attn_out, d_out, w_out, adjacency, counts):
    queries, keys, values, attn_out, d_out = (
        a[0] for a in (queries, keys, values, attn_out, d_out)
    )
    rows, hw = queries.shape
    width = d_out.shape[1]
    samples = lax.axis_size(DP)
    cores = lax.axis_size("core")
    chips = lax.axis_size("y")
    down = lax.axis_size("x")
    across = lax.axis_size("z_hi")
    part = width // down
    half = HD // cores

    w_half = lax.dynamic_slice_in_dim(w_out, lax.axis_index("core") * half, half, 0)
    w_all = lax.all_gather(w_half, DP + ("core",), axis=0, tiled=True)

    sent = (samples, 2 * rows, part)
    spread, grads, halo = pl.pallas_call(
        prepare_body,
        out_shape=(
            pltpu.HBM(sent, BF),
            pltpu.HBM((rows, width), BF),
            pltpu.HBM((2 * rows + 8, hw), BF),
        ),
        in_specs=[smem()] + [hbm()] * 4,
        out_specs=(hbm(), hbm(), hbm()),
        scratch_shapes=[
            pltpu.VMEM((rows, width), BF),
            pltpu.VMEM((8, hw), BF),
            pltpu.SemaphoreType.DMA((2,)),
            pltpu.SemaphoreType.DMA((samples,)),
            pltpu.SemaphoreType.DMA((samples,)),
            pltpu.SemaphoreType.DMA((3,)),
        ],
        compiler_params=PARAMS,
    )(counts, in_hbm(d_out), in_hbm(attn_out), in_hbm(keys), in_hbm(values))
    gathered = lax.all_to_all(spread, DP, 0, 0)
    behind = shift(halo, 1)
    ahead = shift(halo, -1)

    group = 2
    share = -(-(half * part // LANES) // (8 * chips)) * 8
    pieces = (cores, chips, down, share, LANES)
    weight = pl.pallas_call(
        weight_body,
        out_shape=jax.ShapeDtypeStruct(pieces, BF),
        grid=(samples // group,),
        in_specs=[pl.BlockSpec((group, 2 * rows, part), lambda i: (i, 0, 0))],
        out_specs=pl.BlockSpec(pieces, lambda i: (0, 0, 0, 0, 0)),
        scratch_shapes=[pltpu.VMEM((part, part), F32)],
        compiler_params=PARAMS,
    )(gathered)

    pair = lax.all_to_all(weight, "core", 0, 0)
    terms = jnp.sum(pair.astype(F32), axis=0).astype(BF)
    terms, behind, ahead = lax.optimization_barrier((terms, behind, ahead))
    (probs,) = call(
        probs_body,
        [((HEADS, rows, 3 * rows), F32)],
        [smem(), smem(), vmem(), vmem(), vmem(), vmem()],
    )(counts, adjacency[0], queries, keys, behind, ahead)
    terms = lax.all_to_all(terms, "y", 0, 0)
    terms, probs = lax.optimization_barrier((terms, probs))
    terms = jnp.sum(terms.astype(F32), axis=0).astype(BF)
    terms = jnp.broadcast_to(terms[:, None], (down, across, share, LANES))
    terms = terms.reshape(down * across, share, LANES)
    terms = lax.all_to_all(terms, ("x", "z_hi"), 0, 0).reshape(down, across, share, LANES)
    total = jnp.sum(terms.astype(F32), axis=1).astype(BF)
    total = lax.all_to_all(spread_out(total, chips), "y", 0, 0)
    both = lax.all_to_all(spread_out(total, cores), "core", 0, 0)
    (d_weight,) = call(assemble_body, [((HD, width), BF)], [vmem()])(both)

    pairs = (2, rows, hw)
    d_queries, own, to_behind, to_ahead = call(
        attention_body,
        [((rows, hw), BF), (pairs, F32), (pairs, BF), (pairs, BF)],
        [hbm()] + [vmem()] * 8,
        [pltpu.VMEM((HEADS, HD, width), BF), pltpu.SemaphoreType.DMA((HEADS,))],
    )(
        in_hbm(w_all.reshape(HEADS, HD, width)),
        probs, grads, attn_out, queries, keys, values, behind, ahead,
    )
    d_keys, d_values = call(
        finish_body, [((rows, hw), BF), ((rows, hw), BF)], [vmem()] * 3
    )(own, shift(to_ahead, 1), shift(to_behind, -1))
    return d_queries[None], d_keys[None], d_values[None], d_weight


def solution(mesh):
    parts = Mesh(mesh.devices.reshape(2, 4, 8, 4, 2), DP + REGION)
    rows = P(DP, REGION, None)
    return jax.shard_map(
        local,
        mesh=parts,
        in_specs=(rows, rows, rows, rows, rows, P(DP, None), P(REGION, None, None), P(REGION)),
        out_specs=(rows, rows, rows, P(DP, None)),
        check_vma=False,
    )
```

time: 203 us -> 233 us (1.15)
  Pallas kernels: 24 us -> 80.8 us
  waiting for transfers between devices: 92.9 us -> 54.5 us
  between operations: 1.45 us -> 14.9 us
  blocking collectives: 32.4 us -> 39.6 us
  starting transfers between devices: 40.1 us -> 33.1 us
  local copies, waits for them, and re-layouts: 9.54 us -> 7.01 us
    ppermute x4, waiting for transfers between devices: 77.5 us -> 8.14 us  [shift(): lax.ppermute(value, REGION, [(i, (i + by) % length) for i in range(length)])]
    pallas_call x3, Pallas kernels: 13.2 us -> 64.5 us  [the longest x1 60.9 us: local(): pl.pallas_call(prepare_body, out_shape=(pltpu.HBM(sent, BF), pltpu.HBM((r...]
    all_to_all x1, waiting for transfers between devices: 0.01 us -> 32.7 us  [local(): gathered = lax.all_to_all(spread, DP, 0, 0)]
    all_to_all x3 -> x2, starting transfers between devices: 17.3 us -> 10.9 us  [the longest x1 6.82 us: local(): terms = lax.all_to_all(terms, 'y', 0, 0)]
    all_to_all x1, blocking collectives: 4.01 us -> 8.88 us  [local(): pair = lax.all_to_all(weight, 'core', 0, 0)]
    pallas_call x1, Pallas kernels: 7.52 us -> 12.4 us  [local(): call(attention_body, [((rows, hw), BF), (pairs, F32), (pairs, BF), (pairs...]
    unnamed x27 -> x18, local copies, waits for them, and re-layouts: 8.42 us -> 4.24 us
    all_to_all x2, blocking collectives: 28.4 us -> 30.7 us  [the longest x1 20.7 us: local(): lax.all_to_all(terms, ('x', 'z_hi'), 0, 0)]
  transfers between devices with their start and end apart: 8 -> 8, of which waited for: 5 -> 3; matrix products, arithmetic and copies ran while one was open for 1% -> 2% of each run, Pallas kernels for 7% -> 34%
where the time goes in v3:
time: 233 us; the launch traced here: 232 us
  Pallas kernels  80.8 us (35%)
  waiting for transfers between devices  54.5 us (23%)
  blocking collectives  39.6 us (17%)
  starting transfers between devices  33.1 us (14%)
  between operations  14.9 us (6%)
  local copies, waits for them, and re-layouts  7.01 us (3%)
    pallas_call x1, Pallas kernels, local(): pl.pallas_call(prepare_body, out_shape=(pltpu.HBM(sent, BF), pltpu.HBM((r...  60.9 us
    all_to_all x1, waiting for transfers between devices, local(): gathered = lax.all_to_all(spread, DP, 0, 0)  32.7 us
    all_to_all x1, blocking collectives, local(): lax.all_to_all(terms, ('x', 'z_hi'), 0, 0)  20.7 us
    ppermute x4, starting transfers between devices, shift(): lax.ppermute(value, REGION, [(i, (i + by) % length) for i in range(length)])  15.4 us
    all_to_all x1, waiting for transfers between devices, local(): terms = lax.all_to_all(terms, 'y', 0, 0)  13.6 us
    pallas_call x1, Pallas kernels, local(): call(attention_body, [((rows, hw), BF), (pairs, F32), (pairs, BF), (pairs...  12.4 us
    all_to_all x1, blocking collectives, local(): both = lax.all_to_all(spread_out(total, cores), 'core', 0, 0)  10.1 us
    all_to_all x1, blocking collectives, local(): pair = lax.all_to_all(weight, 'core', 0, 0)  8.88 us
  transfers between devices with their start and end apart: 8, of which 3 were waited for; matrix products, arithmetic and copies ran while one was open for 2% of the time, Pallas kernels for 34%

profile of v3, /device:TPU:1, one launch (start us, length us, event | category | flops | bytes accessed | tf_op | source)
XLA Modules:
  0.0 232.0 jit_solution(11882578291642447655)
XLA Ops:
  7.2 0.0 copy-start
  7.2 0.0 all-gather.2.cloned.1.call-start
  7.2 1.1 copy-done
  8.3 0.8 constant_dynamic-slice_fusion
  9.1 0.0 all-gather.2.cloned.1.call-update
  9.8 60.9 %shard_map.111 = (bf16[8,256,640]{2,1,0:T(8,128)(2,1)}, bf16[128,2560]{1,0:T(8,128)(2,1)}, bf16[264,1280]{1,0:T(8,128)(2,1)}) custom-call(s32[1]{0:T(128)S(6)} %copy.12.counts, bf16[128,2560]{1,0:T(8,128)(2,1)} %bitcast.25, bf16[128,1280]{1,0:T(8,128)(2,1)} %bitcast.18, bf16[128,1280]{1,0:T(8,128)(2,1)} %bitcast.13, bf16[128,1280]{1,0:T(8,128)(2,1)} %bitcast.20), custom_call_target="tpu_custom_call" | custom-call | tf_op jit(solution)/shard_map/pallas_call | solution.py:251
  70.6 6.7 %all-to-all-start = ((bf16[8,256,640]{2,1,0:T(8,128)(2,1)}), bf16[8,256,640]{2,1,0:T(8,128)(2,1)S(1)}, u32[]{:S(2)}, u32[]{:S(2)}) async-start(bf16[8,256,640]{2,1,0:T(8,128)(2,1)} %get-tuple-element.18), calls=%async_computation | async-start | bytes 5242880 | tf_op jit(solution)/shard_map/all_to_all | solution.py:270
  77.3 5.8 %collective-permute-start.1 = (bf16[264,1280]{1,0:T(8,128)(2,1)}, bf16[264,1280]{1,0:T(8,128)(2,1)}, u32[]{:S(2)}, u32[]{:S(2)}) collective-permute-start(bf16[264,1280]{1,0:T(8,128)(2,1)} %get-tuple-element.19), channel_id=1, source_target_pairs={{0,63},{1,0},{2,1},{3,2},{4,3},{5,4},{6,5},{7,6},{8,7},{9,8},{10,9... | collective-permute-start | bytes 2027528 | tf_op jit(solution)/shard_map/ppermute | solution.py:226
  83.1 2.8 %collective-permute-start = (bf16[264,1280]{1,0:T(8,128)(2,1)}, bf16[264,1280]{1,0:T(8,128)(2,1)}, u32[]{:S(2)}, u32[]{:S(2)}) collective-permute-start(bf16[264,1280]{1,0:T(8,128)(2,1)} %get-tuple-element.19), channel_id=1, source_target_pairs={{0,1},{1,2},{2,3},{3,4},{4,5},{5,6},{6,7},{7,8},{8,9},{9,10},{10,1... | collective-permute-start | bytes 2027528 | tf_op jit(solution)/shard_map/ppermute | solution.py:226
  85.9 32.7 %all-to-all-done.gathered = bf16[8,256,640]{2,1,0:T(8,128)(2,1)S(1)} async-done(((bf16[8,256,640]{2,1,0:T(8,128)(2,1)}), bf16[8,256,640]{2,1,0:T(8,128)(2,1)S(1)}, u32[]{:S(2)}, u32[]{:S(2)}) %all-to-all-start) | async-done | bytes 2621472 | tf_op jit(solution)/shard_map/all_to_all | solution.py:270
  118.6 2.6 %shard_map.112 = bf16[2,8,4,56,128]{4,3,2,1,0:T(8,128)(2,1)S(1)} custom-call(bf16[8,256,640]{2,1,0:T(8,128)(2,1)S(1)} %all-to-all-done.gathered), custom_call_target="tpu_custom_call" | custom-call | tf_op jit(solution)/shard_map/pallas_call | solution.py:277
  121.2 0.0 copy-start.1
  121.2 0.0 copy-start.2
  121.2 0.0 copy-start.8
  121.2 8.9 %all_to_all.30 = bf16[2,8,4,56,128]{4,3,2,1,0:T(8,128)(2,1)S(1)} all-to-all(bf16[2,8,4,56,128]{4,3,2,1,0:T(8,128)(2,1)S(1)} %shard_map.112), channel_id=1, replica_groups=mesh['z_lo'=2,'x'=4,'y'=8,'z_hi'=4,'core'=2] {'core'}, dimensions={0} | all-to-all | bytes 1835008 | tf_op jit(solution)/shard_map/all_to_all | solution.py:287
  130.1 1.0 reduce_sum.36
  131.1 0.0 collective-permute-done.1.ahead
  131.1 0.0 collective-permute-done.behind
  131.1 6.8 %all-to-all-start.2 = ((bf16[8,4,56,128]{3,2,1,0:T(8,128)(2,1)}), bf16[8,4,56,128]{3,2,1,0:T(8,128)(2,1)}, u32[]{:S(2)}, u32[]{:S(2)}) async-start(bf16[8,4,56,128]{3,2,1,0:T(8,128)(2,1)} %reduce_sum.36), calls=%async_computation.2 | async-start | bytes 917504 | tf_op jit(solution)/shard_map/all_to_all | solution.py:295
  137.9 0.0 copy-done.1
  138.0 0.0 copy-done.2
  138.0 0.0 copy-done.8
  138.0 0.0 copy-start.3
  138.0 3.0 %shard_map.113.probs = f32[8,128,384]{2,1,0:T(8,128)S(1)} custom-call(s32[1]{0:T(128)S(6)} %copy.12.counts, s32[4,12]{1,0:T(4,128)S(1)} %bitcast.22, bf16[128,1280]{1,0:T(8,128)(2,1)S(1)} %bitcast.16, bf16[128,1280]{1,0:T(8,128)(2,1)S(1)} %bitcast.14, bf16[264,1280]{1,0:T(8,128)(2,1)} %collective-permute-done.behind, ...), custom_call_target="tpu_custom_call" | custom-call | tf_op jit(solution)/shard_map/pallas_call | solution.py:290
  141.0 13.6 %all-to-all-done.2 = bf16[8,4,56,128]{3,2,1,0:T(8,128)(2,1)} async-done(((bf16[8,4,56,128]{3,2,1,0:T(8,128)(2,1)}), bf16[8,4,56,128]{3,2,1,0:T(8,128)(2,1)}, u32[]{:S(2)}, u32[]{:S(2)}) %all-to-all-start.2) | async-done | bytes 458784 | tf_op jit(solution)/shard_map/all_to_all | solution.py:295
  154.6 1.1 reduce_sum.37
  155.7 20.7 %all_to_all.31 = bf16[16,56,128]{2,1,0:T(8,128)(2,1)S(1)} all-to-all(bf16[16,56,128]{2,1,0:T(8,128)(2,1)S(1)} %bitcast.24), channel_id=1, replica_groups=mesh['z_lo'=2,'x'=4,'y'=8,'z_hi'=4,'core'=2] {'x','z_hi'}, dimensions={0} | all-to-all | bytes 458752 | tf_op jit(solution)/shard_map/all_to_all | solution.py:300
  176.5 0.8 broadcast_in_dim.31
  177.3 4.1 %all-to-all-start.4 = ((bf16[8,4,56,128]{3,2,1,0:T(8,128)(2,1)}), bf16[8,4,56,128]{3,2,1,0:T(8,128)(2,1)}, u32[]{:S(2)}, u32[]{:S(2)}) async-start(bf16[8,4,56,128]{3,2,1,0:T(8,128)(2,1)} %broadcast_in_dim.31), calls=%async_computation.4 | async-start | bytes 917504 | tf_op jit(solution)/shard_map/all_to_all | solution.py:302
  181.4 0.0 all-gather.2.cloned.1.call-done
  181.4 0.0 copy-done.3
  181.4 0.0 copy-start.4
  181.5 1.0 copy-done.4
  182.4 0.0 copy-start.7
  182.4 1.1 copy-done.7
  183.5 12.4 %shard_map.114 = (bf16[128,1280]{1,0:T(8,128)(2,1)}, f32[2,128,1280]{2,1,0:T(8,128)S(1)}, bf16[2,128,1280]{2,1,0:T(8,128)(2,1)}, bf16[2,128,1280]{2,1,0:T(8,128)(2,1)}) custom-call(bf16[8,160,2560]{2,1,0:T(8,128)(2,1)} %bitcast.23, f32[8,128,384]{2,1,0:T(8,128)S(1)} %shard_map.113.probs, bf16[128,2560]{1,0:T(8,128)(2,1)S(1)} %copy-done.7, ...), custom_call_target="tpu_custom_call" | custom-call | tf_op jit(solution)/shard_map/pallas_call | solution.py:307
  195.9 0.0 copy-start.5
  195.9 1.1 copy-done.5
  196.9 0.0 copy-start.6
  196.9 3.4 %collective-permute-start.2 = (bf16[2,128,1280]{2,1,0:T(8,128)(2,1)}, bf16[2,128,1280]{2,1,0:T(8,128)(2,1)S(1)}, u32[]{:S(2)}, u32[]{:S(2)}) collective-permute-start(bf16[2,128,1280]{2,1,0:T(8,128)(2,1)} %get-tuple-element.27), channel_id=1, source_target_pairs={{0,1},{1,2},{2,3},{3,4},{4,5},{5,6},{6,7},{7,8},{8,9},{9,10},{10,1... | collective-permute-start | bytes 1966088 | tf_op jit(solution)/shard_map/ppermute | solution.py:226
  200.3 3.5 %collective-permute-start.3 = (bf16[2,128,1280]{2,1,0:T(8,128)(2,1)}, bf16[2,128,1280]{2,1,0:T(8,128)(2,1)S(1)}, u32[]{:S(2)}, u32[]{:S(2)}) collective-permute-start(bf16[2,128,1280]{2,1,0:T(8,128)(2,1)} %get-tuple-element.28), channel_id=1, source_target_pairs={{0,63},{1,0},{2,1},{3,2},{4,3},{5,4},{6,5},{7,6},{8,7},{9,8},{10,9... | collective-permute-start | bytes 1966088 | tf_op jit(solution)/shard_map/ppermute | solution.py:226
  203.8 0.0 all-to-all-done.4
  203.8 1.1 broadcast_in_dim.32
  205.0 10.1 %all_to_all.32.both = bf16[2,8,4,56,128]{4,3,2,1,0:T(8,128)(2,1)S(1)} all-to-all(bf16[2,8,4,56,128]{4,3,2,1,0:T(8,128)(2,1)S(1)} %broadcast_in_dim.32), channel_id=1, replica_groups=mesh['z_lo'=2,'x'=4,'y'=8,'z_hi'=4,'core'=2] {'core'}, dimensions={0} | all-to-all | bytes 1835008 | tf_op jit(solution)/shard_map/all_to_all | solution.py:303
  215.0 1.0 shard_map.116
  216.1 0.0 collective-permute-done.2.from_behind
  216.1 8.1 %collective-permute-done.3.from_ahead = bf16[2,128,1280]{2,1,0:T(8,128)(2,1)S(1)} collective-permute-done((bf16[2,128,1280]{2,1,0:T(8,128)(2,1)}, bf16[2,128,1280]{2,1,0:T(8,128)(2,1)S(1)}, u32[]{:S(2)}, u32[]{:S(2)}) %collective-permute-start.3) | collective-permute-done | bytes 655392 | tf_op jit(solution)/shard_map/ppermute | solution.py:226
  224.2 0.0 copy-done.6
  224.2 1.0 shard_map.115
  (2 shorter events, 0.1 us)
Async XLA Ops:
  7.2 1.2 copy-start
  7.2 174.3 %all-gather.2.cloned.1.call-start = ((), (), s32[]{:S(2)}) async-start(), calls=%async_computation.6 | async-start | bytes 6963200 | tf_op jit(solution)/shard_map/all_gather | solution.py:248
  70.6 47.9 %all-to-all-start = ((bf16[8,256,640]{2,1,0:T(8,128)(2,1)}), bf16[8,256,640]{2,1,0:T(8,128)(2,1)S(1)}, u32[]{:S(2)}, u32[]{:S(2)}) async-start(bf16[8,256,640]{2,1,0:T(8,128)(2,1)} %get-tuple-element.18), calls=%async_computation | async-start | bytes 5242880 | tf_op jit(solution)/shard_map/all_to_all | solution.py:270
  77.3 53.8 %collective-permute-start.1 = (bf16[264,1280]{1,0:T(8,128)(2,1)}, bf16[264,1280]{1,0:T(8,128)(2,1)}, u32[]{:S(2)}, u32[]{:S(2)}) collective-permute-start(bf16[264,1280]{1,0:T(8,128)(2,1)} %get-tuple-element.19), channel_id=1, source_target_pairs={{0,63},{1,0},{2,1},{3,2},{4,3},{5,4},{6,5},{7,6},{8,7},{9,8},{10,9... | collective-permute-start | bytes 2027528 | tf_op jit(solution)/shard_map/ppermute | solution.py:226
  83.1 48.0 %collective-permute-start = (bf16[264,1280]{1,0:T(8,128)(2,1)}, bf16[264,1280]{1,0:T(8,128)(2,1)}, u32[]{:S(2)}, u32[]{:S(2)}) collective-permute-start(bf16[264,1280]{1,0:T(8,128)(2,1)} %get-tuple-element.19), channel_id=1, source_target_pairs={{0,1},{1,2},{2,3},{3,4},{4,5},{5,6},{6,7},{7,8},{8,9},{9,10},{10,1... | collective-permute-start | bytes 2027528 | tf_op jit(solution)/shard_map/ppermute | solution.py:226
  121.2 16.8 %copy-start.1 = (bf16[1,128,1280]{2,1,0:T(8,128)(2,1)S(1)}, bf16[1,128,1280]{2,1,0:T(8,128)(2,1)}, u32[]{:S(2)}) copy-start(bf16[1,128,1280]{2,1,0:T(8,128)(2,1)} %param.9) | copy-start | bytes 983044
  121.2 16.8 %copy-start.2 = (bf16[1,128,1280]{2,1,0:T(8,128)(2,1)S(1)}, bf16[1,128,1280]{2,1,0:T(8,128)(2,1)}, u32[]{:S(2)}) copy-start(bf16[1,128,1280]{2,1,0:T(8,128)(2,1)} %param.8) | copy-start | bytes 983044
  121.2 16.8 %copy-start.8 = (s32[1,4,12]{2,1,0:T(4,128)S(1)}, s32[1,4,12]{2,1,0:T(4,128)}, u32[]{:S(2)}) copy-start(s32[1,4,12]{2,1,0:T(4,128)} %param.14) | copy-start | bytes 580
  131.1 23.5 %all-to-all-start.2 = ((bf16[8,4,56,128]{3,2,1,0:T(8,128)(2,1)}), bf16[8,4,56,128]{3,2,1,0:T(8,128)(2,1)}, u32[]{:S(2)}, u32[]{:S(2)}) async-start(bf16[8,4,56,128]{3,2,1,0:T(8,128)(2,1)} %reduce_sum.36), calls=%async_computation.2 | async-start | bytes 917504 | tf_op jit(solution)/shard_map/all_to_all | solution.py:295
  138.0 43.5 %copy-start.3 = (bf16[1,128,1280]{2,1,0:T(8,128)(2,1)S(1)}, bf16[1,128,1280]{2,1,0:T(8,128)(2,1)}, u32[]{:S(2)}) copy-start(bf16[1,128,1280]{2,1,0:T(8,128)(2,1)} %param.11) | copy-start | bytes 983044
  177.3 26.5 %all-to-all-start.4 = ((bf16[8,4,56,128]{3,2,1,0:T(8,128)(2,1)}), bf16[8,4,56,128]{3,2,1,0:T(8,128)(2,1)}, u32[]{:S(2)}, u32[]{:S(2)}) async-start(bf16[8,4,56,128]{3,2,1,0:T(8,128)(2,1)} %broadcast_in_dim.31), calls=%async_computation.4 | async-start | bytes 917504 | tf_op jit(solution)/shard_map/all_to_all | solution.py:302
  181.4 1.0 copy-start.4
  182.4 1.1 copy-start.7
  195.9 1.1 copy-start.5
  196.9 27.3 %copy-start.6 = (f32[2,128,1280]{2,1,0:T(8,128)S(1)}, f32[2,128,1280]{2,1,0:T(8,128)}, u32[]{:S(2)}) copy-start(f32[2,128,1280]{2,1,0:T(8,128)} %copy-done.5) | copy-start | bytes 3932164
  196.9 19.1 %collective-permute-start.2 = (bf16[2,128,1280]{2,1,0:T(8,128)(2,1)}, bf16[2,128,1280]{2,1,0:T(8,128)(2,1)S(1)}, u32[]{:S(2)}, u32[]{:S(2)}) collective-permute-start(bf16[2,128,1280]{2,1,0:T(8,128)(2,1)} %get-tuple-element.27), channel_id=1, source_target_pairs={{0,1},{1,2},{2,3},{3,4},{4,5},{5,6},{6,7},{7,8},{8,9},{9,10},{10,1... | collective-permute-start | bytes 1966088 | tf_op jit(solution)/shard_map/ppermute | solution.py:226
  200.3 23.9 %collective-permute-start.3 = (bf16[2,128,1280]{2,1,0:T(8,128)(2,1)}, bf16[2,128,1280]{2,1,0:T(8,128)(2,1)S(1)}, u32[]{:S(2)}, u32[]{:S(2)}) collective-permute-start(bf16[2,128,1280]{2,1,0:T(8,128)(2,1)} %get-tuple-element.28), channel_id=1, source_target_pairs={{0,63},{1,0},{2,1},{3,2},{4,3},{5,4},{6,5},{7,6},{8,7},{9,8},{10,9... | collective-permute-start | bytes 1966088 | tf_op jit(solution)/shard_map/ppermute | solution.py:226
Sparse Core Ops, SparseCore 0:
  10.2 72.9 all-gather.1

commit v4 on v3

--- a/solution.py
+++ b/solution.py
@@ -32,34 +32,31 @@
 
 
 def prepare_body(
-    counts, d_out, attn_out, keys, values, spread, grads, halo,
-    grads_in, tail, sem_in, sem_attn, sem_out, sem_halo,
+    counts, core, d_out, attn_out, keys, values, w_out, w_half, spread, grads, halo,
+    w_in, grads_in, attn_in, tail, halo_in, sem_in, sem_attn, sem_out, sem_halo,
 ):
     rows, width = d_out.shape
     samples, _, part = spread.shape
-    load = pltpu.make_async_copy(d_out, grads_in, sem_in.at[0])
-    load.start()
-    copies = []
     down = width // part
-    for s in range(samples):
-        half = pl.ds(s // down * part, part)
-        copies.append(
-            pltpu.make_async_copy(
-                attn_out.at[:, half], spread.at[s, pl.ds(0, rows)], sem_attn.at[s]
-            )
-        )
+    half_rows = w_half.shape[0]
+    first_row = pl.multiple_of(core[0] * half_rows, half_rows)
+    w_load = pltpu.make_async_copy(w_out.at[pl.ds(first_row, half_rows)], w_in, sem_in.at[4])
+    w_load.start()
+    loads = [
+        pltpu.make_async_copy(d_out, grads_in, sem_in.at[0]),
+        pltpu.make_async_copy(attn_out, attn_in, sem_in.at[1]),
+        pltpu.make_async_copy(keys, halo_in.at[pl.ds(0, rows)], sem_in.at[2]),
+        pltpu.make_async_copy(values, halo_in.at[pl.ds(rows, rows)], sem_in.at[3]),
+    ]
+    for load in loads:
+        load.start()
     tail[...] = jnp.full(tail.shape, counts[0].astype(F32), F32).astype(BF)
-    copies += [
-        pltpu.make_async_copy(keys, halo.at[pl.ds(0, rows)], sem_halo.at[0]),
-        pltpu.make_async_copy(values, halo.at[pl.ds(rows, rows)], sem_halo.at[1]),
-        pltpu.make_async_copy(tail, halo.at[pl.ds(2 * rows, 8)], sem_halo.at[2]),
-    ]
-    for copy in copies:
-        copy.start()
-    load.wait()
+    stores = [pltpu.make_async_copy(tail, halo.at[pl.ds(2 * rows, 8)], sem_halo.at[1])]
     live = lax.broadcasted_iota(jnp.int32, (rows, 1), 0) // (rows // BLK) < counts[0]
+    w_load.wait()
+    stores.append(pltpu.make_async_copy(w_in, w_half, sem_halo.at[3]))
+    loads[0].wait()
     grads_in[...] = jnp.where(live, grads_in[...], jnp.zeros((), BF))
-    stores = [pltpu.make_async_copy(grads_in, grads, sem_in.at[1])]
     for s in range(samples):
         quarter = pl.ds(s % down * part, part)
         stores.append(
@@ -67,18 +64,32 @@
                 grads_in.at[:, quarter], spread.at[s, pl.ds(rows, rows)], sem_out.at[s]
             )
         )
-    for copy in stores:
-        copy.start()
-    for copy in copies + stores:
-        copy.wait()
-
-
-def probs_body(counts, adjacency, queries, keys, behind, ahead, probs):
-    rows = queries.shape[0]
+    stores.append(pltpu.make_async_copy(grads_in, grads, sem_halo.at[2]))
+    for store in stores:
+        store.start()
+    loads[1].wait()
+    for s in range(samples):
+        half = pl.ds(s // down * part, part)
+        stores.append(
+            pltpu.make_async_copy(
+                attn_in.at[:, half], spread.at[s, pl.ds(0, rows)], sem_attn.at[s]
+            )
+        )
+        stores[-1].start()
+    loads[2].wait()
+    loads[3].wait()
+    stores.append(
+        pltpu.make_async_copy(halo_in, halo.at[pl.ds(0, 2 * rows)], sem_halo.at[0])
+    )
+    stores[-1].start()
+    for store in stores:
+        store.wait()
+
+
+def allowed_pairs(counts, adjacency, behind, ahead, rows):
     block = rows // BLK
     width = 3 * rows
-    lane = lax.broadcasted_iota(jnp.int32, (1, width), 1)
-    key_block = lane // block
+    key_block = lax.broadcasted_iota(jnp.int32, (1, width), 1) // block
     count = jnp.concatenate(
         [
             behind[2 * rows : 2 * rows + 1, :rows].astype(F32),
@@ -95,14 +106,7 @@
             seen = jnp.where(key_block == j, adjacency[a, j], seen)
         ok = jnp.logical_or(jnp.logical_and(seen == 1, live), key_block == BLK + a)
         bias.append(jnp.broadcast_to(jnp.where(ok, 1.0, 0.0), (block, width)))
-    allowed = jnp.concatenate(bias, 0) > 0.5
-    for h in range(HEADS):
-        cols = slice(h * HD, (h + 1) * HD)
-        window = jnp.concatenate([behind[0:rows, cols], keys[:, cols], ahead[0:rows, cols]], 0)
-        scores = jnp.where(allowed, nt(queries[:, cols], window) * SCALE, -1e30)
-        maxima = jnp.max(scores, axis=1, keepdims=True)
-        terms = jnp.where(allowed, jnp.exp(scores - maxima), 0.0)
-        probs[h] = terms / jnp.sum(terms, axis=1, keepdims=True)
+    return jnp.concatenate(bias, 0) > 0.5
 
 
 def weight_body(gathered, weight, acc):
@@ -152,17 +156,35 @@
                 ].astype(BF)
 
 
-def attention_body(
-    w_all, probs, grads, attn_out, queries, keys, values, behind, ahead,
-    d_queries, own, to_behind, to_ahead, w_in, sem,
-):
+def attention_body(counts, adjacency, *refs):
+    sources, rest = refs[:8], refs[8:]
+    targets, rest = rest[:4], rest[4:]
+    arrays, rest = rest[:8], rest[8:]
+    results, (sem_w, sem_in, sem_out) = rest[:4], rest[4:]
+    w_all, *sources = sources
+    w_in, *arrays = arrays
+    queries, keys, behind, ahead, grads, attn_out, values = arrays
+    d_queries, own, to_behind, to_ahead = results
     rows = queries.shape[0]
-    loads = [pltpu.make_async_copy(w_all.at[h], w_in.at[h], sem.at[h]) for h in range(HEADS)]
+    loads = [
+        pltpu.make_async_copy(source, array, sem_in.at[i])
+        for i, (source, array) in enumerate(zip(sources, arrays))
+    ]
+    w_loads = [pltpu.make_async_copy(w_all.at[h], w_in.at[h], sem_w.at[h]) for h in range(HEADS)]
+    for load in loads + w_loads:
+        load.start()
     for load in loads:
-        load.start()
+        load.wait()
+    allowed = allowed_pairs(counts, adjacency, behind, ahead, rows)
     for h in range(HEADS):
         cols = slice(h * HD, (h + 1) * HD)
-        loads[h].wait()
+        key_win = jnp.concatenate([behind[0:rows, cols], keys[:, cols], ahead[0:rows, cols]], 0)
+        query = queries[:, cols]
+        scores = jnp.where(allowed, nt(query, key_win) * SCALE, -1e30)
+        terms = jnp.exp(scores - jnp.max(scores, axis=1, keepdims=True))
+        terms = jnp.where(allowed, terms, 0.0)
+        prob = terms / jnp.sum(terms, axis=1, keepdims=True)
+        w_loads[h].wait()
         grad = nt(grads[...], w_in[h]).astype(BF)
         delta = jnp.sum(
             grad.astype(F32) * attn_out[:, cols].astype(F32), axis=1, keepdims=True
@@ -170,18 +192,22 @@
         value_win = jnp.concatenate(
             [behind[rows : 2 * rows, cols], values[:, cols], ahead[rows : 2 * rows, cols]], 0
         )
-        key_win = jnp.concatenate([behind[0:rows, cols], keys[:, cols], ahead[0:rows, cols]], 0)
-        prob = probs[h]
         dprobs = nt(grad, value_win)
         dscores = (prob * (dprobs - delta) * SCALE).astype(BF)
         d_queries[:, cols] = nn(dscores, key_win).astype(BF)
-        for which, (left, right) in enumerate(
-            ((dscores, queries[:, cols]), (prob.astype(BF), grad))
-        ):
+        for which, (left, right) in enumerate(((dscores, query), (prob.astype(BF), grad))):
             win = tn(left, right)
             to_behind[which, :, cols] = win[:rows].astype(BF)
             own[which, :, cols] = win[rows : 2 * rows]
             to_ahead[which, :, cols] = win[2 * rows :].astype(BF)
+    stores = [
+        pltpu.make_async_copy(result, target, sem_out.at[i])
+        for i, (result, target) in enumerate(zip(results, targets))
+    ]
+    for store in stores:
+        store.start()
+    for store in stores:
+        store.wait()
 
 
 def finish_body(own, from_behind, from_ahead, d_keys, d_values):
@@ -207,7 +233,7 @@
     return pltpu.with_memory_space_constraint(value, pltpu.HBM)
 
 
-PARAMS = pltpu.CompilerParams(vmem_limit_bytes=28 << 20)
+PARAMS = pltpu.CompilerParams(vmem_limit_bytes=20 << 20)
 
 
 def call(body, outs, specs, scratch=()):
@@ -244,32 +270,33 @@
     part = width // down
     half = HD // cores
 
-    w_half = lax.dynamic_slice_in_dim(w_out, lax.axis_index("core") * half, half, 0)
-    w_all = lax.all_gather(w_half, DP + ("core",), axis=0, tiled=True)
-
-    sent = (samples, 2 * rows, part)
-    spread, grads, halo = pl.pallas_call(
+    core = lax.axis_index("core").reshape(1)
+    w_half, spread, grads, halo = pl.pallas_call(
         prepare_body,
         out_shape=(
-            pltpu.HBM(sent, BF),
+            pltpu.HBM((half, width), BF),
+            pltpu.HBM((samples, 2 * rows, part), BF),
             pltpu.HBM((rows, width), BF),
             pltpu.HBM((2 * rows + 8, hw), BF),
         ),
-        in_specs=[smem()] + [hbm()] * 4,
-        out_specs=(hbm(), hbm(), hbm()),
+        in_specs=[smem()] * 2 + [hbm()] * 5,
+        out_specs=(hbm(),) * 4,
         scratch_shapes=[
+            pltpu.VMEM((half, width), BF),
             pltpu.VMEM((rows, width), BF),
+            pltpu.VMEM((rows, hw), BF),
             pltpu.VMEM((8, hw), BF),
-            pltpu.SemaphoreType.DMA((2,)),
+            pltpu.VMEM((2 * rows, hw), BF),
+            pltpu.SemaphoreType.DMA((5,)),
             pltpu.SemaphoreType.DMA((samples,)),
             pltpu.SemaphoreType.DMA((samples,)),
-            pltpu.SemaphoreType.DMA((3,)),
+            pltpu.SemaphoreType.DMA((4,)),
         ],
         compiler_params=PARAMS,
-    )(counts, in_hbm(d_out), in_hbm(attn_out), in_hbm(keys), in_hbm(values))
+    )(counts, core, *(in_hbm(a) for a in (d_out, attn_out, keys, values, w_out)))
+    w_all = lax.all_gather(w_half, DP + ("core",), axis=0, tiled=True)
+
     gathered = lax.all_to_all(spread, DP, 0, 0)
-    behind = shift(halo, 1)
-    ahead = shift(halo, -1)
 
     group = 2
     share = -(-(half * part // LANES) // (8 * chips)) * 8
@@ -286,33 +313,40 @@
 
     pair = lax.all_to_all(weight, "core", 0, 0)
     terms = jnp.sum(pair.astype(F32), axis=0).astype(BF)
-    terms, behind, ahead = lax.optimization_barrier((terms, behind, ahead))
-    (probs,) = call(
-        probs_body,
-        [((HEADS, rows, 3 * rows), F32)],
-        [smem(), smem(), vmem(), vmem(), vmem(), vmem()],
-    )(counts, adjacency[0], queries, keys, behind, ahead)
+    terms, halo = lax.optimization_barrier((terms, halo))
+    behind = shift(halo, 1)
+    ahead = shift(halo, -1)
     terms = lax.all_to_all(terms, "y", 0, 0)
-    terms, probs = lax.optimization_barrier((terms, probs))
     terms = jnp.sum(terms.astype(F32), axis=0).astype(BF)
     terms = jnp.broadcast_to(terms[:, None], (down, across, share, LANES))
     terms = terms.reshape(down * across, share, LANES)
+    terms, grads = lax.optimization_barrier((terms, grads))
+    operands = (
+        w_all.reshape(HEADS, HD, width), queries, keys, behind, ahead, grads, attn_out, values,
+    )
+    pairs = (2, rows, hw)
+    results = (((rows, hw), BF), (pairs, F32), (pairs, BF), (pairs, BF))
+    d_queries, own, to_behind, to_ahead = pl.pallas_call(
+        attention_body,
+        out_shape=tuple(pltpu.HBM(shape, dtype) for shape, dtype in results),
+        in_specs=[smem()] * 2 + [hbm()] * len(operands),
+        out_specs=(hbm(),) * len(results),
+        scratch_shapes=[pltpu.VMEM(a.shape, a.dtype) for a in operands]
+        + [pltpu.VMEM(shape, dtype) for shape, dtype in results]
+        + [
+            pltpu.SemaphoreType.DMA((HEADS,)),
+            pltpu.SemaphoreType.DMA((len(operands) - 1,)),
+            pltpu.SemaphoreType.DMA((len(results),)),
+        ],
+        compiler_params=PARAMS,
+    )(counts, adjacency[0], *(in_hbm(a) for a in operands))
     terms = lax.all_to_all(terms, ("x", "z_hi"), 0, 0).reshape(down, across, share, LANES)
+    terms, own = lax.optimization_barrier((terms, own))
     total = jnp.sum(terms.astype(F32), axis=1).astype(BF)
     total = lax.all_to_all(spread_out(total, chips), "y", 0, 0)
     both = lax.all_to_all(spread_out(total, cores), "core", 0, 0)
     (d_weight,) = call(assemble_body, [((HD, width), BF)], [vmem()])(both)
 
-    pairs = (2, rows, hw)
-    d_queries, own, to_behind, to_ahead = call(
-        attention_body,
-        [((rows, hw), BF), (pairs, F32), (pairs, BF), (pairs, BF)],
-        [hbm()] + [vmem()] * 8,
-        [pltpu.VMEM((HEADS, HD, width), BF), pltpu.SemaphoreType.DMA((HEADS,))],
-    )(
-        in_hbm(w_all.reshape(HEADS, HD, width)),
-        probs, grads, attn_out, queries, keys, values, behind, ahead,
-    )
     d_keys, d_values = call(
         finish_body, [((rows, hw), BF), ((rows, hw), BF)], [vmem()] * 3
     )(own, shift(to_ahead, 1), shift(to_behind, -1))

time: 233 us -> 177 us (0.76)
  Pallas kernels: 80.8 us -> 24.1 us
  waiting for transfers between devices: 54.5 us -> 27 us
  blocking collectives: 39.6 us -> 64.4 us
  starting transfers between devices: 33.1 us -> 42.2 us
  local copies, waits for them, and re-layouts: 7.01 us -> 2.53 us
    pallas_call x3 -> x2, Pallas kernels: 76.3 us -> 19.6 us  [the longest x1 16.1 us: local(): pl.pallas_call(attention_body, out_shape=tuple((pltpu.HBM(shape, dtype) f...]
    all_to_all x1, waiting for transfers between devices: 32.7 us -> 0.01 us  [local(): lax.all_to_all(terms, ('x', 'z_hi'), 0, 0)]
    all_to_all x1, blocking collectives: 20.7 us -> 42.6 us  [local(): gathered = lax.all_to_all(spread, DP, 0, 0)]
    ppermute x4, waiting for transfers between devices: 8.14 us -> 19.3 us  [shift(): lax.ppermute(value, REGION, [(i, (i + by) % length) for i in range(length)])]
    all_to_all x1, blocking collectives: 8.88 us -> 15.8 us  [local(): pair = lax.all_to_all(weight, 'core', 0, 0)]
    all_to_all x1, starting transfers between devices: 4.12 us -> 10.9 us  [local(): total = lax.all_to_all(spread_out(total, chips), 'y', 0, 0)]
    all_to_all x1, waiting for transfers between devices: 13.6 us -> 7.71 us  [local(): terms = lax.all_to_all(terms, 'y', 0, 0)]
    all_to_all x1, starting transfers between devices: 6.67 us -> 12 us  [local(): lax.all_to_all(terms, ('x', 'z_hi'), 0, 0)]
  transfers between devices with their start and end apart: 8 -> 8, of which waited for: 3 -> 4; matrix products, arithmetic and copies ran while one was open for 2% -> 1% of each run, Pallas kernels for 34% -> 11%
where the time goes in v4:
time: 177 us; the launch traced here: 176 us
  blocking collectives  64.4 us (36%)
  starting transfers between devices  42.2 us (24%)
  waiting for transfers between devices  27 us (15%)
  Pallas kernels  24.1 us (14%)
  between operations  14.8 us (8%)
  local copies, waits for them, and re-layouts  2.53 us (1%)
    all_to_all x1, blocking collectives, local(): gathered = lax.all_to_all(spread, DP, 0, 0)  42.6 us
    ppermute x4, waiting for transfers between devices, shift(): lax.ppermute(value, REGION, [(i, (i + by) % length) for i in range(length)])  19.3 us
    pallas_call x1, Pallas kernels, local(): pl.pallas_call(attention_body, out_shape=tuple((pltpu.HBM(shape, dtype) f...  16.1 us
    all_to_all x1, blocking collectives, local(): pair = lax.all_to_all(weight, 'core', 0, 0)  15.8 us
    ppermute x4, starting transfers between devices, shift(): lax.ppermute(value, REGION, [(i, (i + by) % length) for i in range(length)])  13.9 us
    all_to_all x1, starting transfers between devices, local(): lax.all_to_all(terms, ('x', 'z_hi'), 0, 0)  12 us
    all_to_all x1, starting transfers between devices, local(): total = lax.all_to_all(spread_out(total, chips), 'y', 0, 0)  10.9 us
    all_to_all x1, waiting for transfers between devices, local(): terms = lax.all_to_all(terms, 'y', 0, 0)  7.71 us
  transfers between devices with their start and end apart: 8, of which 4 were waited for; matrix products, arithmetic and copies ran while one was open for 1% of the time, Pallas kernels for 11%

profile of v4, /device:TPU:1, one launch (start us, length us, event | category | flops | bytes accessed | tf_op | source)
XLA Modules:
  0.0 176.2 jit_solution(9879490282810904663)
XLA Ops:
  7.2 0.0 all-gather.2.cloned.1.call-start
  7.9 3.5 %shard_map.111 = (bf16[80,2560]{1,0:T(8,128)(2,1)}, bf16[8,256,640]{2,1,0:T(8,128)(2,1)}, bf16[128,2560]{1,0:T(8,128)(2,1)}, bf16[264,1280]{1,0:T(8,128)(2,1)}) custom-call(s32[1]{0:T(128)S(6)} %copy.12.counts, s32[1]{0:T(128)} %bitcast.1.core, bf16[128,2560]{1,0:T(8,128)(2,1)} %bitcast.22, bf16[128,1280]{1,0:T(8,128)(2,1)} %bitcast.15, ...), custom_call_target="tpu_custom_call" | custom-call | tf_op jit(solution)/shard_map/pallas_call | solution.py:274
  11.4 0.0 all-gather.2.cloned.1.call-update
  11.4 42.6 %all_to_all.30.gathered = bf16[8,256,640]{2,1,0:T(8,128)(2,1)S(1)} all-to-all(bf16[8,256,640]{2,1,0:T(8,128)(2,1)} %get-tuple-element.21), channel_id=1, replica_groups=mesh['z_lo'=2,'x'=4,'y'=8,'z_hi'=4,'core'=2] {'z_lo','x'}, dimensions={0} | all-to-all | bytes 5242880 | tf_op jit(solution)/shard_map/all_to_all | solution.py:299
  54.0 2.6 %shard_map.112 = bf16[2,8,4,56,128]{4,3,2,1,0:T(8,128)(2,1)S(1)} custom-call(bf16[8,256,640]{2,1,0:T(8,128)(2,1)S(1)} %all_to_all.30.gathered), custom_call_target="tpu_custom_call" | custom-call | tf_op jit(solution)/shard_map/pallas_call | solution.py:304
  56.6 0.0 copy-start.4
  56.6 0.0 copy-start.1
  56.6 15.8 %all_to_all.31 = bf16[2,8,4,56,128]{4,3,2,1,0:T(8,128)(2,1)S(1)} all-to-all(bf16[2,8,4,56,128]{4,3,2,1,0:T(8,128)(2,1)S(1)} %shard_map.112), channel_id=1, replica_groups=mesh['z_lo'=2,'x'=4,'y'=8,'z_hi'=4,'core'=2] {'core'}, dimensions={0} | all-to-all | bytes 1835008 | tf_op jit(solution)/shard_map/all_to_all | solution.py:314
  72.4 1.0 reduce_sum.36
  73.5 5.4 %all-to-all-start.2 = ((bf16[8,4,56,128]{3,2,1,0:T(8,128)(2,1)}), bf16[8,4,56,128]{3,2,1,0:T(8,128)(2,1)S(1)}, u32[]{:S(2)}, u32[]{:S(2)}) async-start(bf16[8,4,56,128]{3,2,1,0:T(8,128)(2,1)} %reduce_sum.36), calls=%async_computation.2 | async-start | bytes 917504 | tf_op jit(solution)/shard_map/all_to_all | solution.py:319
  78.9 0.0 copy-done.4
  78.9 6.9 %collective-permute-start = (bf16[264,1280]{1,0:T(8,128)(2,1)S(1)}, bf16[264,1280]{1,0:T(8,128)(2,1)S(1)}, u32[]{:S(2)}, u32[]{:S(2)}) collective-permute-start(bf16[264,1280]{1,0:T(8,128)(2,1)S(1)} %copy-done.4), channel_id=1, source_target_pairs={{0,1},{1,2},{2,3},{3,4},{4,5},{5,6},{6,7},{7,8},{8,9},{9,10},{10,1... | collective-permute-start | bytes 2027528 | tf_op jit(solution)/shard_map/ppermute | solution.py:252
  85.8 1.9 %collective-permute-start.1 = (bf16[264,1280]{1,0:T(8,128)(2,1)S(1)}, bf16[264,1280]{1,0:T(8,128)(2,1)S(1)}, u32[]{:S(2)}, u32[]{:S(2)}) collective-permute-start(bf16[264,1280]{1,0:T(8,128)(2,1)S(1)} %copy-done.4), channel_id=1, source_target_pairs={{0,63},{1,0},{2,1},{3,2},{4,3},{5,4},{6,5},{7,6},{8,7},{9,8},{10,9... | collective-permute-start | bytes 2027528 | tf_op jit(solution)/shard_map/ppermute | solution.py:252
  87.7 7.7 %all-to-all-done.2 = bf16[8,4,56,128]{3,2,1,0:T(8,128)(2,1)S(1)} async-done(((bf16[8,4,56,128]{3,2,1,0:T(8,128)(2,1)}), bf16[8,4,56,128]{3,2,1,0:T(8,128)(2,1)S(1)}, u32[]{:S(2)}, u32[]{:S(2)}) %all-to-all-start.2) | async-done | bytes 458784 | tf_op jit(solution)/shard_map/all_to_all | solution.py:319
  95.4 0.1 reduce_sum.37
  95.5 0.7 broadcast_in_dim.12
  96.2 12.0 %all-to-all-start.3 = ((bf16[16,56,128]{2,1,0:T(8,128)(2,1)}), bf16[16,56,128]{2,1,0:T(8,128)(2,1)S(1)}, u32[]{:S(2)}, u32[]{:S(2)}) async-start(bf16[16,56,128]{2,1,0:T(8,128)(2,1)} %bitcast.8), calls=%async_computation.3 | async-start | bytes 458752 | tf_op jit(solution)/shard_map/all_to_all | solution.py:343
  108.2 0.0 collective-permute-done.refs_3_
  108.2 0.0 copy-start.2
  108.2 1.9 %collective-permute-done.1.refs_4_ = bf16[264,1280]{1,0:T(8,128)(2,1)S(1)} collective-permute-done((bf16[264,1280]{1,0:T(8,128)(2,1)S(1)}, bf16[264,1280]{1,0:T(8,128)(2,1)S(1)}, u32[]{:S(2)}, u32[]{:S(2)}) %collective-permute-start.1) | collective-permute-done | bytes 675872 | tf_op jit(solution)/shard_map/ppermute | solution.py:252
  110.1 0.0 copy-start.3
  110.1 0.0 all-gather.2.cloned.1.call-done
  110.1 0.0 copy-done.2
  110.1 0.8 copy-done.3
  110.9 0.0 copy-done.1
  110.9 16.1 %shard_map.113 = (bf16[128,1280]{1,0:T(8,128)(2,1)}, f32[2,128,1280]{2,1,0:T(8,128)}, bf16[2,128,1280]{2,1,0:T(8,128)(2,1)}, bf16[2,128,1280]{2,1,0:T(8,128)(2,1)}) custom-call(s32[1]{0:T(128)S(6)} %copy.12.counts, s32[4,12]{1,0:T(4,128)S(1)} %bitcast.13, bf16[8,160,2560]{2,1,0:T(8,128)(2,1)} %bitcast.14, bf16[128,1280]{1,0:T(8,128)(2,1)} %bitcast.23, ...), custom_call_target="tpu_custom_call" | custom-call | tf_op jit(solution)/shard_map/pallas_call | solution.py:329
  127.0 0.0 copy-start
  127.0 0.0 all-to-all-done.3
  127.1 0.8 broadcast_in_dim.31
  127.9 10.9 %all-to-all-start.4 = ((bf16[8,4,56,128]{3,2,1,0:T(8,128)(2,1)}), bf16[8,4,56,128]{3,2,1,0:T(8,128)(2,1)S(1)}, u32[]{:S(2)}, u32[]{:S(2)}) async-start(bf16[8,4,56,128]{3,2,1,0:T(8,128)(2,1)} %broadcast_in_dim.31), calls=%async_computation.4 | async-start | bytes 917504 | tf_op jit(solution)/shard_map/all_to_all | solution.py:346
  138.8 1.9 %collective-permute-start.2 = (bf16[2,128,1280]{2,1,0:T(8,128)(2,1)}, bf16[2,128,1280]{2,1,0:T(8,128)(2,1)S(1)}, u32[]{:S(2)}, u32[]{:S(2)}) collective-permute-start(bf16[2,128,1280]{2,1,0:T(8,128)(2,1)} %get-tuple-element.31), channel_id=1, source_target_pairs={{0,1},{1,2},{2,3},{3,4},{4,5},{5,6},{6,7},{7,8},{8,9},{9,10},{10,1... | collective-permute-start | bytes 1966088 | tf_op jit(solution)/shard_map/ppermute | solution.py:252
  140.8 3.1 %collective-permute-start.3 = (bf16[2,128,1280]{2,1,0:T(8,128)(2,1)}, bf16[2,128,1280]{2,1,0:T(8,128)(2,1)S(1)}, u32[]{:S(2)}, u32[]{:S(2)}) collective-permute-start(bf16[2,128,1280]{2,1,0:T(8,128)(2,1)} %get-tuple-element.32), channel_id=1, source_target_pairs={{0,63},{1,0},{2,1},{3,2},{4,3},{5,4},{6,5},{7,6},{8,7},{9,8},{10,9... | collective-permute-start | bytes 1966088 | tf_op jit(solution)/shard_map/ppermute | solution.py:252
  143.9 6.4 %collective-permute-done.2.from_behind = bf16[2,128,1280]{2,1,0:T(8,128)(2,1)S(1)} collective-permute-done((bf16[2,128,1280]{2,1,0:T(8,128)(2,1)}, bf16[2,128,1280]{2,1,0:T(8,128)(2,1)S(1)}, u32[]{:S(2)}, u32[]{:S(2)}) %collective-permute-start.2) | collective-permute-done | bytes 655392 | tf_op jit(solution)/shard_map/ppermute | solution.py:252
  150.4 10.9 %collective-permute-done.3.from_ahead = bf16[2,128,1280]{2,1,0:T(8,128)(2,1)S(1)} collective-permute-done((bf16[2,128,1280]{2,1,0:T(8,128)(2,1)}, bf16[2,128,1280]{2,1,0:T(8,128)(2,1)S(1)}, u32[]{:S(2)}, u32[]{:S(2)}) %collective-permute-start.3) | collective-permute-done | bytes 655392 | tf_op jit(solution)/shard_map/ppermute | solution.py:252
  161.3 0.0 copy-done
  161.3 1.0 shard_map.114
  162.3 0.0 all-to-all-done.4
  162.3 0.1 broadcast_in_dim.32
  162.4 6.0 %all_to_all.32.both = bf16[2,8,4,56,128]{4,3,2,1,0:T(8,128)(2,1)S(1)} all-to-all(bf16[2,8,4,56,128]{4,3,2,1,0:T(8,128)(2,1)S(1)} %broadcast_in_dim.32), channel_id=1, replica_groups=mesh['z_lo'=2,'x'=4,'y'=8,'z_hi'=4,'core'=2] {'core'}, dimensions={0} | all-to-all | bytes 1835008 | tf_op jit(solution)/shard_map/all_to_all | solution.py:347
  168.3 1.0 shard_map.115
  (1 shorter events, 0.0 us)
Async XLA Ops:
  7.2 102.9 %all-gather.2.cloned.1.call-start = ((), (), s32[]{:S(2)}) async-start(), calls=%async_computation.6 | async-start | bytes 6963200 | tf_op jit(solution)/shard_map/all_gather | solution.py:297
  56.6 22.3 %copy-start.4 = (bf16[264,1280]{1,0:T(8,128)(2,1)S(1)}, bf16[264,1280]{1,0:T(8,128)(2,1)}, u32[]{:S(2)}) copy-start(bf16[264,1280]{1,0:T(8,128)(2,1)} %get-tuple-element.23) | copy-start | bytes 2027524
  56.6 54.3 %copy-start.1 = (s32[1,4,12]{2,1,0:T(4,128)S(1)}, s32[1,4,12]{2,1,0:T(4,128)}, u32[]{:S(2)}) copy-start(s32[1,4,12]{2,1,0:T(4,128)} %param.14) | copy-start | bytes 580
  73.5 22.0 %all-to-all-start.2 = ((bf16[8,4,56,128]{3,2,1,0:T(8,128)(2,1)}), bf16[8,4,56,128]{3,2,1,0:T(8,128)(2,1)S(1)}, u32[]{:S(2)}, u32[]{:S(2)}) async-start(bf16[8,4,56,128]{3,2,1,0:T(8,128)(2,1)} %reduce_sum.36), calls=%async_computation.2 | async-start | bytes 917504 | tf_op jit(solution)/shard_map/all_to_all | solution.py:319
  78.9 29.3 %collective-permute-start = (bf16[264,1280]{1,0:T(8,128)(2,1)S(1)}, bf16[264,1280]{1,0:T(8,128)(2,1)S(1)}, u32[]{:S(2)}, u32[]{:S(2)}) collective-permute-start(bf16[264,1280]{1,0:T(8,128)(2,1)S(1)} %copy-done.4), channel_id=1, source_target_pairs={{0,1},{1,2},{2,3},{3,4},{4,5},{5,6},{6,7},{7,8},{8,9},{9,10},{10,1... | collective-permute-start | bytes 2027528 | tf_op jit(solution)/shard_map/ppermute | solution.py:252
  85.8 24.3 %collective-permute-start.1 = (bf16[264,1280]{1,0:T(8,128)(2,1)S(1)}, bf16[264,1280]{1,0:T(8,128)(2,1)S(1)}, u32[]{:S(2)}, u32[]{:S(2)}) collective-permute-start(bf16[264,1280]{1,0:T(8,128)(2,1)S(1)} %copy-done.4), channel_id=1, source_target_pairs={{0,63},{1,0},{2,1},{3,2},{4,3},{5,4},{6,5},{7,6},{8,7},{9,8},{10,9... | collective-permute-start | bytes 2027528 | tf_op jit(solution)/shard_map/ppermute | solution.py:252
  96.2 30.8 %all-to-all-start.3 = ((bf16[16,56,128]{2,1,0:T(8,128)(2,1)}), bf16[16,56,128]{2,1,0:T(8,128)(2,1)S(1)}, u32[]{:S(2)}, u32[]{:S(2)}) async-start(bf16[16,56,128]{2,1,0:T(8,128)(2,1)} %bitcast.8), calls=%async_computation.3 | async-start | bytes 458752 | tf_op jit(solution)/shard_map/all_to_all | solution.py:343
  108.2 1.9 %copy-start.2 = (bf16[264,1280]{1,0:T(8,128)(2,1)}, bf16[264,1280]{1,0:T(8,128)(2,1)S(1)}, u32[]{:S(2)}) copy-start(bf16[264,1280]{1,0:T(8,128)(2,1)S(1)} %collective-permute-done.refs_3_) | copy-start | bytes 2027524
  110.1 0.8 copy-start.3
  127.0 34.3 %copy-start = (f32[2,128,1280]{2,1,0:T(8,128)S(1)}, f32[2,128,1280]{2,1,0:T(8,128)}, u32[]{:S(2)}) copy-start(f32[2,128,1280]{2,1,0:T(8,128)} %get-tuple-element.30.own) | copy-start | bytes 3932164
  127.9 34.4 %all-to-all-start.4 = ((bf16[8,4,56,128]{3,2,1,0:T(8,128)(2,1)}), bf16[8,4,56,128]{3,2,1,0:T(8,128)(2,1)S(1)}, u32[]{:S(2)}, u32[]{:S(2)}) async-start(bf16[8,4,56,128]{3,2,1,0:T(8,128)(2,1)} %broadcast_in_dim.31), calls=%async_computation.4 | async-start | bytes 917504 | tf_op jit(solution)/shard_map/all_to_all | solution.py:346
  138.8 11.5 %collective-permute-start.2 = (bf16[2,128,1280]{2,1,0:T(8,128)(2,1)}, bf16[2,128,1280]{2,1,0:T(8,128)(2,1)S(1)}, u32[]{:S(2)}, u32[]{:S(2)}) collective-permute-start(bf16[2,128,1280]{2,1,0:T(8,128)(2,1)} %get-tuple-element.31), channel_id=1, source_target_pairs={{0,1},{1,2},{2,3},{3,4},{4,5},{5,6},{6,7},{7,8},{8,9},{9,10},{10,1... | collective-permute-start | bytes 1966088 | tf_op jit(solution)/shard_map/ppermute | solution.py:252
  140.8 20.5 %collective-permute-start.3 = (bf16[2,128,1280]{2,1,0:T(8,128)(2,1)}, bf16[2,128,1280]{2,1,0:T(8,128)(2,1)S(1)}, u32[]{:S(2)}, u32[]{:S(2)}) collective-permute-start(bf16[2,128,1280]{2,1,0:T(8,128)(2,1)} %get-tuple-element.32), channel_id=1, source_target_pairs={{0,63},{1,0},{2,1},{3,2},{4,3},{5,4},{6,5},{7,6},{8,7},{9,8},{10,9... | collective-permute-start | bytes 1966088 | tf_op jit(solution)/shard_map/ppermute | solution.py:252
Sparse Core Ops, SparseCore 0:
  11.5 70.2 all-gather.1

commit v5 on v4

--- a/solution.py
+++ b/solution.py
@@ -173,7 +173,7 @@
     w_loads = [pltpu.make_async_copy(w_all.at[h], w_in.at[h], sem_w.at[h]) for h in range(HEADS)]
     for load in loads + w_loads:
         load.start()
-    for load in loads:
+    for load in loads + w_loads:
         load.wait()
     allowed = allowed_pairs(counts, adjacency, behind, ahead, rows)
     for h in range(HEADS):
@@ -184,7 +184,6 @@
         terms = jnp.exp(scores - jnp.max(scores, axis=1, keepdims=True))
         terms = jnp.where(allowed, terms, 0.0)
         prob = terms / jnp.sum(terms, axis=1, keepdims=True)
-        w_loads[h].wait()
         grad = nt(grads[...], w_in[h]).astype(BF)
         delta = jnp.sum(
             grad.astype(F32) * attn_out[:, cols].astype(F32), axis=1, keepdims=True
@@ -347,6 +346,7 @@
     both = lax.all_to_all(spread_out(total, cores), "core", 0, 0)
     (d_weight,) = call(assemble_body, [((HD, width), BF)], [vmem()])(both)
 
+    d_weight, own = lax.optimization_barrier((d_weight, own))
     d_keys, d_values = call(
         finish_body, [((rows, hw), BF), ((rows, hw), BF)], [vmem()] * 3
     )(own, shift(to_ahead, 1), shift(to_behind, -1))

time: 177 us -> 168 us (0.949)
  waiting for transfers between devices: 27 us -> 20 us
  Pallas kernels: 24.1 us -> 22.1 us
    ppermute x4, waiting for transfers between devices: 19.3 us -> 2.19 us  [shift(): lax.ppermute(value, REGION, [(i, (i + by) % length) for i in range(length)])]
    all_to_all x1, waiting for transfers between devices: 0.01 us -> 10 us  [local(): total = lax.all_to_all(spread_out(total, chips), 'y', 0, 0)]
    pallas_call x1, Pallas kernels: 16.1 us -> 14 us  [local(): pl.pallas_call(attention_body, out_shape=tuple((pltpu.HBM(shape, dtype) f...]
where the time goes in v5:
time: 168 us; the launch traced here: 167 us
  blocking collectives  64.3 us (38%)
  starting transfers between devices  42.4 us (25%)
  Pallas kernels  22.1 us (13%)
  waiting for transfers between devices  20 us (12%)
  between operations  14.8 us (9%)
  local copies, waits for them, and re-layouts  2.53 us (2%)
    all_to_all x1, blocking collectives, local(): gathered = lax.all_to_all(spread, DP, 0, 0)  42.6 us
    all_to_all x1, blocking collectives, local(): pair = lax.all_to_all(weight, 'core', 0, 0)  15.8 us
    ppermute x4, starting transfers between devices, shift(): lax.ppermute(value, REGION, [(i, (i + by) % length) for i in range(length)])  14 us
    pallas_call x1, Pallas kernels, local(): pl.pallas_call(attention_body, out_shape=tuple((pltpu.HBM(shape, dtype) f...  14 us
    all_to_all x1, starting transfers between devices, local(): lax.all_to_all(terms, ('x', 'z_hi'), 0, 0)  12 us
    all_to_all x1, starting transfers between devices, local(): total = lax.all_to_all(spread_out(total, chips), 'y', 0, 0)  11 us
    all_to_all x1, waiting for transfers between devices, local(): total = lax.all_to_all(spread_out(total, chips), 'y', 0, 0)  10 us
    all_to_all x1, waiting for transfers between devices, local(): terms = lax.all_to_all(terms, 'y', 0, 0)  7.71 us
  transfers between devices with their start and end apart: 8, of which 4 were waited for; matrix products, arithmetic and copies ran while one was open for 1% of the time, Pallas kernels for 11%

profile of v5, /device:TPU:1, one launch (start us, length us, event | category | flops | bytes accessed | tf_op | source)
XLA Modules:
  0.0 167.2 jit_solution(3917945590645719119)
XLA Ops:
  7.2 0.0 all-gather.2.cloned.1.call-start
  7.9 3.5 %shard_map.111 = (bf16[80,2560]{1,0:T(8,128)(2,1)}, bf16[8,256,640]{2,1,0:T(8,128)(2,1)}, bf16[128,2560]{1,0:T(8,128)(2,1)}, bf16[264,1280]{1,0:T(8,128)(2,1)}) custom-call(s32[1]{0:T(128)S(6)} %copy.12.counts, s32[1]{0:T(128)} %bitcast.1.core, bf16[128,2560]{1,0:T(8,128)(2,1)} %bitcast.22, bf16[128,1280]{1,0:T(8,128)(2,1)} %bitcast.15, ...), custom_call_target="tpu_custom_call" | custom-call | tf_op jit(solution)/shard_map/pallas_call | solution.py:273
  11.4 0.0 all-gather.2.cloned.1.call-update
  11.4 42.6 %all_to_all.30.gathered = bf16[8,256,640]{2,1,0:T(8,128)(2,1)S(1)} all-to-all(bf16[8,256,640]{2,1,0:T(8,128)(2,1)} %get-tuple-element.23), channel_id=1, replica_groups=mesh['z_lo'=2,'x'=4,'y'=8,'z_hi'=4,'core'=2] {'z_lo','x'}, dimensions={0} | all-to-all | bytes 5242880 | tf_op jit(solution)/shard_map/all_to_all | solution.py:298
  54.0 2.6 %shard_map.112 = bf16[2,8,4,56,128]{4,3,2,1,0:T(8,128)(2,1)S(1)} custom-call(bf16[8,256,640]{2,1,0:T(8,128)(2,1)S(1)} %all_to_all.30.gathered), custom_call_target="tpu_custom_call" | custom-call | tf_op jit(solution)/shard_map/pallas_call | solution.py:303
  56.6 0.0 copy-start.4
  56.6 0.0 copy-start.1
  56.6 15.8 %all_to_all.31 = bf16[2,8,4,56,128]{4,3,2,1,0:T(8,128)(2,1)S(1)} all-to-all(bf16[2,8,4,56,128]{4,3,2,1,0:T(8,128)(2,1)S(1)} %shard_map.112), channel_id=1, replica_groups=mesh['z_lo'=2,'x'=4,'y'=8,'z_hi'=4,'core'=2] {'core'}, dimensions={0} | all-to-all | bytes 1835008 | tf_op jit(solution)/shard_map/all_to_all | solution.py:313
  72.4 1.0 reduce_sum.36
  73.5 5.4 %all-to-all-start.2 = ((bf16[8,4,56,128]{3,2,1,0:T(8,128)(2,1)}), bf16[8,4,56,128]{3,2,1,0:T(8,128)(2,1)S(1)}, u32[]{:S(2)}, u32[]{:S(2)}) async-start(bf16[8,4,56,128]{3,2,1,0:T(8,128)(2,1)} %reduce_sum.36), calls=%async_computation.2 | async-start | bytes 917504 | tf_op jit(solution)/shard_map/all_to_all | solution.py:318
  78.9 0.0 copy-done.4
  78.9 6.9 %collective-permute-start = (bf16[264,1280]{1,0:T(8,128)(2,1)S(1)}, bf16[264,1280]{1,0:T(8,128)(2,1)S(1)}, u32[]{:S(2)}, u32[]{:S(2)}) collective-permute-start(bf16[264,1280]{1,0:T(8,128)(2,1)S(1)} %copy-done.4), channel_id=1, source_target_pairs={{0,1},{1,2},{2,3},{3,4},{4,5},{5,6},{6,7},{7,8},{8,9},{9,10},{10,1... | collective-permute-start | bytes 2027528 | tf_op jit(solution)/shard_map/ppermute | solution.py:251
  85.8 1.9 %collective-permute-start.1 = (bf16[264,1280]{1,0:T(8,128)(2,1)S(1)}, bf16[264,1280]{1,0:T(8,128)(2,1)S(1)}, u32[]{:S(2)}, u32[]{:S(2)}) collective-permute-start(bf16[264,1280]{1,0:T(8,128)(2,1)S(1)} %copy-done.4), channel_id=1, source_target_pairs={{0,63},{1,0},{2,1},{3,2},{4,3},{5,4},{6,5},{7,6},{8,7},{9,8},{10,9... | collective-permute-start | bytes 2027528 | tf_op jit(solution)/shard_map/ppermute | solution.py:251
  87.7 7.7 %all-to-all-done.2 = bf16[8,4,56,128]{3,2,1,0:T(8,128)(2,1)S(1)} async-done(((bf16[8,4,56,128]{3,2,1,0:T(8,128)(2,1)}), bf16[8,4,56,128]{3,2,1,0:T(8,128)(2,1)S(1)}, u32[]{:S(2)}, u32[]{:S(2)}) %all-to-all-start.2) | async-done | bytes 458784 | tf_op jit(solution)/shard_map/all_to_all | solution.py:318
  95.4 0.1 reduce_sum.37
  95.5 0.7 broadcast_in_dim.12
  96.2 12.0 %all-to-all-start.3 = ((bf16[16,56,128]{2,1,0:T(8,128)(2,1)}), bf16[16,56,128]{2,1,0:T(8,128)(2,1)S(1)}, u32[]{:S(2)}, u32[]{:S(2)}) async-start(bf16[16,56,128]{2,1,0:T(8,128)(2,1)} %bitcast.8), calls=%async_computation.3 | async-start | bytes 458752 | tf_op jit(solution)/shard_map/all_to_all | solution.py:342
  108.2 0.0 collective-permute-done.refs_3_
  108.2 0.0 copy-start.2
  108.2 1.9 %collective-permute-done.1.refs_4_ = bf16[264,1280]{1,0:T(8,128)(2,1)S(1)} collective-permute-done((bf16[264,1280]{1,0:T(8,128)(2,1)S(1)}, bf16[264,1280]{1,0:T(8,128)(2,1)S(1)}, u32[]{:S(2)}, u32[]{:S(2)}) %collective-permute-start.1) | collective-permute-done | bytes 675872 | tf_op jit(solution)/shard_map/ppermute | solution.py:251
  110.1 0.0 copy-start.3
  110.1 0.0 all-gather.2.cloned.1.call-done
  110.1 0.0 copy-done.2
  110.1 0.8 copy-done.3
  110.9 0.0 copy-done.1
  110.9 14.0 %shard_map.113 = (bf16[128,1280]{1,0:T(8,128)(2,1)}, f32[2,128,1280]{2,1,0:T(8,128)}, bf16[2,128,1280]{2,1,0:T(8,128)(2,1)}, bf16[2,128,1280]{2,1,0:T(8,128)(2,1)}) custom-call(s32[1]{0:T(128)S(6)} %copy.12.counts, s32[4,12]{1,0:T(4,128)S(1)} %bitcast.13, bf16[8,160,2560]{2,1,0:T(8,128)(2,1)} %bitcast.14, bf16[128,1280]{1,0:T(8,128)(2,1)} %bitcast.23, ...), custom_call_target="tpu_custom_call" | custom-call | tf_op jit(solution)/shard_map/pallas_call | solution.py:328
  124.9 0.0 all-to-all-done.3
  125.0 0.8 broadcast_in_dim.14
  125.8 11.0 %all-to-all-start.4 = ((bf16[8,4,56,128]{3,2,1,0:T(8,128)(2,1)}), bf16[8,4,56,128]{3,2,1,0:T(8,128)(2,1)S(1)}, u32[]{:S(2)}, u32[]{:S(2)}) async-start(bf16[8,4,56,128]{3,2,1,0:T(8,128)(2,1)} %broadcast_in_dim.14), calls=%async_computation.4 | async-start | bytes 917504 | tf_op jit(solution)/shard_map/all_to_all | solution.py:345
  136.8 0.0 copy-start
  136.8 2.1 %collective-permute-start.2 = (bf16[2,128,1280]{2,1,0:T(8,128)(2,1)}, bf16[2,128,1280]{2,1,0:T(8,128)(2,1)S(1)}, u32[]{:S(2)}, u32[]{:S(2)}) collective-permute-start(bf16[2,128,1280]{2,1,0:T(8,128)(2,1)} %get-tuple-element.35), channel_id=1, source_target_pairs={{0,1},{1,2},{2,3},{3,4},{4,5},{5,6},{6,7},{7,8},{8,9},{9,10},{10,1... | collective-permute-start | bytes 1966088 | tf_op jit(solution)/shard_map/ppermute | solution.py:251
  138.8 3.1 %collective-permute-start.3 = (bf16[2,128,1280]{2,1,0:T(8,128)(2,1)}, bf16[2,128,1280]{2,1,0:T(8,128)(2,1)S(1)}, u32[]{:S(2)}, u32[]{:S(2)}) collective-permute-start(bf16[2,128,1280]{2,1,0:T(8,128)(2,1)} %get-tuple-element.36), channel_id=1, source_target_pairs={{0,63},{1,0},{2,1},{3,2},{4,3},{5,4},{6,5},{7,6},{8,7},{9,8},{10,9... | collective-permute-start | bytes 1966088 | tf_op jit(solution)/shard_map/ppermute | solution.py:251
  142.0 10.0 %all-to-all-done.4 = bf16[8,4,56,128]{3,2,1,0:T(8,128)(2,1)S(1)} async-done(((bf16[8,4,56,128]{3,2,1,0:T(8,128)(2,1)}), bf16[8,4,56,128]{3,2,1,0:T(8,128)(2,1)S(1)}, u32[]{:S(2)}, u32[]{:S(2)}) %all-to-all-start.4) | async-done | bytes 458784 | tf_op jit(solution)/shard_map/all_to_all | solution.py:345
  152.0 0.1 broadcast_in_dim.30
  152.1 5.9 %all_to_all.32.both = bf16[2,8,4,56,128]{4,3,2,1,0:T(8,128)(2,1)S(1)} all-to-all(bf16[2,8,4,56,128]{4,3,2,1,0:T(8,128)(2,1)S(1)} %broadcast_in_dim.30), channel_id=1, replica_groups=mesh['z_lo'=2,'x'=4,'y'=8,'z_hi'=4,'core'=2] {'core'}, dimensions={0} | all-to-all | bytes 1835008 | tf_op jit(solution)/shard_map/all_to_all | solution.py:346
  158.0 1.0 shard_map.114
  159.1 0.0 collective-permute-done.2.from_behind
  159.1 0.3 collective-permute-done.3.from_ahead
  159.4 0.0 copy-done
  159.4 1.0 shard_map.115
  (1 shorter events, 0.0 us)
Async XLA Ops:
  7.2 102.9 %all-gather.2.cloned.1.call-start = ((), (), s32[]{:S(2)}) async-start(), calls=%async_computation.6 | async-start | bytes 6963200 | tf_op jit(solution)/shard_map/all_gather | solution.py:296
  56.6 22.3 %copy-start.4 = (bf16[264,1280]{1,0:T(8,128)(2,1)S(1)}, bf16[264,1280]{1,0:T(8,128)(2,1)}, u32[]{:S(2)}) copy-start(bf16[264,1280]{1,0:T(8,128)(2,1)} %get-tuple-element.25) | copy-start | bytes 2027524
  56.6 54.3 %copy-start.1 = (s32[1,4,12]{2,1,0:T(4,128)S(1)}, s32[1,4,12]{2,1,0:T(4,128)}, u32[]{:S(2)}) copy-start(s32[1,4,12]{2,1,0:T(4,128)} %param.14) | copy-start | bytes 580
  73.5 22.0 %all-to-all-start.2 = ((bf16[8,4,56,128]{3,2,1,0:T(8,128)(2,1)}), bf16[8,4,56,128]{3,2,1,0:T(8,128)(2,1)S(1)}, u32[]{:S(2)}, u32[]{:S(2)}) async-start(bf16[8,4,56,128]{3,2,1,0:T(8,128)(2,1)} %reduce_sum.36), calls=%async_computation.2 | async-start | bytes 917504 | tf_op jit(solution)/shard_map/all_to_all | solution.py:318
  78.9 29.3 %collective-permute-start = (bf16[264,1280]{1,0:T(8,128)(2,1)S(1)}, bf16[264,1280]{1,0:T(8,128)(2,1)S(1)}, u32[]{:S(2)}, u32[]{:S(2)}) collective-permute-start(bf16[264,1280]{1,0:T(8,128)(2,1)S(1)} %copy-done.4), channel_id=1, source_target_pairs={{0,1},{1,2},{2,3},{3,4},{4,5},{5,6},{6,7},{7,8},{8,9},{9,10},{10,1... | collective-permute-start | bytes 2027528 | tf_op jit(solution)/shard_map/ppermute | solution.py:251
  85.8 24.3 %collective-permute-start.1 = (bf16[264,1280]{1,0:T(8,128)(2,1)S(1)}, bf16[264,1280]{1,0:T(8,128)(2,1)S(1)}, u32[]{:S(2)}, u32[]{:S(2)}) collective-permute-start(bf16[264,1280]{1,0:T(8,128)(2,1)S(1)} %copy-done.4), channel_id=1, source_target_pairs={{0,63},{1,0},{2,1},{3,2},{4,3},{5,4},{6,5},{7,6},{8,7},{9,8},{10,9... | collective-permute-start | bytes 2027528 | tf_op jit(solution)/shard_map/ppermute | solution.py:251
  96.2 28.7 %all-to-all-start.3 = ((bf16[16,56,128]{2,1,0:T(8,128)(2,1)}), bf16[16,56,128]{2,1,0:T(8,128)(2,1)S(1)}, u32[]{:S(2)}, u32[]{:S(2)}) async-start(bf16[16,56,128]{2,1,0:T(8,128)(2,1)} %bitcast.8), calls=%async_computation.3 | async-start | bytes 458752 | tf_op jit(solution)/shard_map/all_to_all | solution.py:342
  108.2 1.9 %copy-start.2 = (bf16[264,1280]{1,0:T(8,128)(2,1)}, bf16[264,1280]{1,0:T(8,128)(2,1)S(1)}, u32[]{:S(2)}) copy-start(bf16[264,1280]{1,0:T(8,128)(2,1)S(1)} %collective-permute-done.refs_3_) | copy-start | bytes 2027524
  110.1 0.8 copy-start.3
  125.8 26.2 %all-to-all-start.4 = ((bf16[8,4,56,128]{3,2,1,0:T(8,128)(2,1)}), bf16[8,4,56,128]{3,2,1,0:T(8,128)(2,1)S(1)}, u32[]{:S(2)}, u32[]{:S(2)}) async-start(bf16[8,4,56,128]{3,2,1,0:T(8,128)(2,1)} %broadcast_in_dim.14), calls=%async_computation.4 | async-start | bytes 917504 | tf_op jit(solution)/shard_map/all_to_all | solution.py:345
  136.8 22.6 %copy-start = (f32[2,128,1280]{2,1,0:T(8,128)S(1)}, f32[2,128,1280]{2,1,0:T(8,128)}, u32[]{:S(2)}) copy-start(f32[2,128,1280]{2,1,0:T(8,128)} %get-tuple-element.34.own) | copy-start | bytes 3932164
  136.8 22.3 %collective-permute-start.2 = (bf16[2,128,1280]{2,1,0:T(8,128)(2,1)}, bf16[2,128,1280]{2,1,0:T(8,128)(2,1)S(1)}, u32[]{:S(2)}, u32[]{:S(2)}) collective-permute-start(bf16[2,128,1280]{2,1,0:T(8,128)(2,1)} %get-tuple-element.35), channel_id=1, source_target_pairs={{0,1},{1,2},{2,3},{3,4},{4,5},{5,6},{6,7},{7,8},{8,9},{9,10},{10,1... | collective-permute-start | bytes 1966088 | tf_op jit(solution)/shard_map/ppermute | solution.py:251
  138.8 20.5 %collective-permute-start.3 = (bf16[2,128,1280]{2,1,0:T(8,128)(2,1)}, bf16[2,128,1280]{2,1,0:T(8,128)(2,1)S(1)}, u32[]{:S(2)}, u32[]{:S(2)}) collective-permute-start(bf16[2,128,1280]{2,1,0:T(8,128)(2,1)} %get-tuple-element.36), channel_id=1, source_target_pairs={{0,63},{1,0},{2,1},{3,2},{4,3},{5,4},{6,5},{7,6},{8,7},{9,8},{10,9... | collective-permute-start | bytes 1966088 | tf_op jit(solution)/shard_map/ppermute | solution.py:251
Sparse Core Ops, SparseCore 0:
  11.5 70.2 all-gather.1

commit v6 on v5

--- a/solution.py
+++ b/solution.py
@@ -156,24 +156,33 @@
                 ].astype(BF)
 
 
-def attention_body(counts, adjacency, *refs):
-    sources, rest = refs[:8], refs[8:]
+def project_body(w_all, grads, d_attn, w_in, grads_in, sem_w, sem):
+    load = pltpu.make_async_copy(grads, grads_in, sem.at[0])
+    w_loads = [pltpu.make_async_copy(w_all.at[h], w_in.at[h], sem_w.at[h]) for h in range(HEADS)]
+    load.start()
+    for w_load in w_loads:
+        w_load.start()
+    load.wait()
+    for h in range(HEADS):
+        w_loads[h].wait()
+        d_attn[:, h * HD : (h + 1) * HD] = nt(grads_in[...], w_in[h]).astype(BF)
+
+
+def attention_body(counts, adjacency, d_attn, behind, ahead, *refs):
+    sources, rest = refs[:4], refs[4:]
     targets, rest = rest[:4], rest[4:]
-    arrays, rest = rest[:8], rest[8:]
-    results, (sem_w, sem_in, sem_out) = rest[:4], rest[4:]
-    w_all, *sources = sources
-    w_in, *arrays = arrays
-    queries, keys, behind, ahead, grads, attn_out, values = arrays
+    arrays, rest = rest[:4], rest[4:]
+    results, (sem_in, sem_out) = rest[:4], rest[4:]
+    queries, keys, attn_out, values = arrays
     d_queries, own, to_behind, to_ahead = results
     rows = queries.shape[0]
     loads = [
         pltpu.make_async_copy(source, array, sem_in.at[i])
         for i, (source, array) in enumerate(zip(sources, arrays))
     ]
-    w_loads = [pltpu.make_async_copy(w_all.at[h], w_in.at[h], sem_w.at[h]) for h in range(HEADS)]
-    for load in loads + w_loads:
+    for load in loads:
         load.start()
-    for load in loads + w_loads:
+    for load in loads:
         load.wait()
     allowed = allowed_pairs(counts, adjacency, behind, ahead, rows)
     for h in range(HEADS):
@@ -184,7 +193,7 @@
         terms = jnp.exp(scores - jnp.max(scores, axis=1, keepdims=True))
         terms = jnp.where(allowed, terms, 0.0)
         prob = terms / jnp.sum(terms, axis=1, keepdims=True)
-        grad = nt(grads[...], w_in[h]).astype(BF)
+        grad = d_attn[:, cols]
         delta = jnp.sum(
             grad.astype(F32) * attn_out[:, cols].astype(F32), axis=1, keepdims=True
         )
@@ -320,25 +329,33 @@
     terms = jnp.broadcast_to(terms[:, None], (down, across, share, LANES))
     terms = terms.reshape(down * across, share, LANES)
     terms, grads = lax.optimization_barrier((terms, grads))
-    operands = (
-        w_all.reshape(HEADS, HD, width), queries, keys, behind, ahead, grads, attn_out, values,
-    )
+    (d_attn,) = call(
+        project_body,
+        [((rows, hw), BF)],
+        [hbm(), hbm()],
+        [
+            pltpu.VMEM((HEADS, HD, width), BF),
+            pltpu.VMEM((rows, width), BF),
+            pltpu.SemaphoreType.DMA((HEADS,)),
+            pltpu.SemaphoreType.DMA((1,)),
+        ],
+    )(in_hbm(w_all.reshape(HEADS, HD, width)), in_hbm(grads))
+    operands = (queries, keys, attn_out, values)
     pairs = (2, rows, hw)
     results = (((rows, hw), BF), (pairs, F32), (pairs, BF), (pairs, BF))
     d_queries, own, to_behind, to_ahead = pl.pallas_call(
         attention_body,
         out_shape=tuple(pltpu.HBM(shape, dtype) for shape, dtype in results),
-        in_specs=[smem()] * 2 + [hbm()] * len(operands),
+        in_specs=[smem()] * 2 + [vmem()] * 3 + [hbm()] * len(operands),
         out_specs=(hbm(),) * len(results),
         scratch_shapes=[pltpu.VMEM(a.shape, a.dtype) for a in operands]
         + [pltpu.VMEM(shape, dtype) for shape, dtype in results]
         + [
-            pltpu.SemaphoreType.DMA((HEADS,)),
-            pltpu.SemaphoreType.DMA((len(operands) - 1,)),
+            pltpu.SemaphoreType.DMA((len(operands),)),
             pltpu.SemaphoreType.DMA((len(results),)),
         ],
         compiler_params=PARAMS,
-    )(counts, adjacency[0], *(in_hbm(a) for a in operands))
+    )(counts, adjacency[0], d_attn, behind, ahead, *(in_hbm(a) for a in operands))
     terms = lax.all_to_all(terms, ("x", "z_hi"), 0, 0).reshape(down, across, share, LANES)
     terms, own = lax.optimization_barrier((terms, own))
     total = jnp.sum(terms.astype(F32), axis=1).astype(BF)

time: 168 us -> 166 us (0.988)
  starting transfers between devices: 42.4 us -> 37.2 us
  Pallas kernels: 22.1 us -> 24.8 us
    pallas_call x0 -> x1, Pallas kernels: none -> 7.87 us  [local(): call(project_body, [((rows, hw), BF)], [hbm(), hbm()], [pltpu.VMEM((HEADS...]
    all_to_all x1, starting transfers between devices: 11 us -> 4.89 us  [local(): total = lax.all_to_all(spread_out(total, chips), 'y', 0, 0)]
    pallas_call x1, Pallas kernels: 14 us -> 8.9 us  [local(): pl.pallas_call(attention_body, out_shape=tuple((pltpu.HBM(shape, dtype) f...]
  transfers between devices with their start and end apart: 8 -> 8, of which waited for: 4 -> 3; matrix products, arithmetic and copies ran while one was open for 1% -> 1% of each run, Pallas kernels for 11% -> 12%
where the time goes in v6:
time: 166 us; the launch traced here: 164 us
  blocking collectives  63.8 us (38%)
  starting transfers between devices  37.2 us (22%)
  Pallas kernels  24.8 us (15%)
  waiting for transfers between devices  20.7 us (12%)
  between operations  14.8 us (9%)
  local copies, waits for them, and re-layouts  1.68 us (1%)
    all_to_all x1, blocking collectives, local(): gathered = lax.all_to_all(spread, DP, 0, 0)  42.6 us
    all_to_all x1, blocking collectives, local(): pair = lax.all_to_all(weight, 'core', 0, 0)  15.8 us
    ppermute x4, starting transfers between devices, shift(): lax.ppermute(value, REGION, [(i, (i + by) % length) for i in range(length)])  14.9 us
    all_to_all x1, starting transfers between devices, local(): lax.all_to_all(terms, ('x', 'z_hi'), 0, 0)  12 us
    all_to_all x1, waiting for transfers between devices, local(): total = lax.all_to_all(spread_out(total, chips), 'y', 0, 0)  9.69 us
    pallas_call x1, Pallas kernels, local(): pl.pallas_call(attention_body, out_shape=tuple((pltpu.HBM(shape, dtype) f...  8.9 us
    pallas_call x1, Pallas kernels, local(): call(project_body, [((rows, hw), BF)], [hbm(), hbm()], [pltpu.VMEM((HEADS...  7.87 us
    all_to_all x1, waiting for transfers between devices, local(): terms = lax.all_to_all(terms, 'y', 0, 0)  7.71 us
  transfers between devices with their start and end apart: 8, of which 3 were waited for; matrix products, arithmetic and copies ran while one was open for 1% of the time, Pallas kernels for 12%

profile of v6, /device:TPU:1, one launch (start us, length us, event | category | flops | bytes accessed | tf_op | source)
XLA Modules:
  0.0 164.2 jit_solution(13333152742917696639)
XLA Ops:
  7.2 0.0 all-gather.2.cloned.1.call-start
  7.9 3.5 %shard_map.111 = (bf16[80,2560]{1,0:T(8,128)(2,1)}, bf16[8,256,640]{2,1,0:T(8,128)(2,1)}, bf16[128,2560]{1,0:T(8,128)(2,1)}, bf16[264,1280]{1,0:T(8,128)(2,1)}) custom-call(s32[1]{0:T(128)S(6)} %copy.12.counts, s32[1]{0:T(128)} %bitcast.1.core, bf16[128,2560]{1,0:T(8,128)(2,1)} %bitcast.22, bf16[128,1280]{1,0:T(8,128)(2,1)} %bitcast.15, ...), custom_call_target="tpu_custom_call" | custom-call | tf_op jit(solution)/shard_map/pallas_call | solution.py:282
  11.4 0.0 all-gather.2.cloned.1.call-update
  11.4 42.6 %all_to_all.30.gathered = bf16[8,256,640]{2,1,0:T(8,128)(2,1)S(1)} all-to-all(bf16[8,256,640]{2,1,0:T(8,128)(2,1)} %get-tuple-element.23), channel_id=1, replica_groups=mesh['z_lo'=2,'x'=4,'y'=8,'z_hi'=4,'core'=2] {'z_lo','x'}, dimensions={0} | all-to-all | bytes 5242880 | tf_op jit(solution)/shard_map/all_to_all | solution.py:307
  54.0 2.6 %shard_map.112 = bf16[2,8,4,56,128]{4,3,2,1,0:T(8,128)(2,1)S(1)} custom-call(bf16[8,256,640]{2,1,0:T(8,128)(2,1)S(1)} %all_to_all.30.gathered), custom_call_target="tpu_custom_call" | custom-call | tf_op jit(solution)/shard_map/pallas_call | solution.py:312
  56.6 0.0 copy-start.2
  56.6 15.8 %all_to_all.31 = bf16[2,8,4,56,128]{4,3,2,1,0:T(8,128)(2,1)S(1)} all-to-all(bf16[2,8,4,56,128]{4,3,2,1,0:T(8,128)(2,1)S(1)} %shard_map.112), channel_id=1, replica_groups=mesh['z_lo'=2,'x'=4,'y'=8,'z_hi'=4,'core'=2] {'core'}, dimensions={0} | all-to-all | bytes 1835008 | tf_op jit(solution)/shard_map/all_to_all | solution.py:322
  72.4 1.1 reduce_sum.36
  73.5 5.4 %all-to-all-start.2 = ((bf16[8,4,56,128]{3,2,1,0:T(8,128)(2,1)}), bf16[8,4,56,128]{3,2,1,0:T(8,128)(2,1)S(1)}, u32[]{:S(2)}, u32[]{:S(2)}) async-start(bf16[8,4,56,128]{3,2,1,0:T(8,128)(2,1)} %reduce_sum.36), calls=%async_computation.2 | async-start | bytes 917504 | tf_op jit(solution)/shard_map/all_to_all | solution.py:327
  78.9 0.0 copy-done.2
  78.9 6.9 %collective-permute-start = (bf16[264,1280]{1,0:T(8,128)(2,1)S(1)}, bf16[264,1280]{1,0:T(8,128)(2,1)S(1)}, u32[]{:S(2)}, u32[]{:S(2)}) collective-permute-start(bf16[264,1280]{1,0:T(8,128)(2,1)S(1)} %copy-done.2), channel_id=1, source_target_pairs={{0,1},{1,2},{2,3},{3,4},{4,5},{5,6},{6,7},{7,8},{8,9},{9,10},{10,1... | collective-permute-start | bytes 2027528 | tf_op jit(solution)/shard_map/ppermute | solution.py:260
  85.8 1.9 %collective-permute-start.1 = (bf16[264,1280]{1,0:T(8,128)(2,1)S(1)}, bf16[264,1280]{1,0:T(8,128)(2,1)S(1)}, u32[]{:S(2)}, u32[]{:S(2)}) collective-permute-start(bf16[264,1280]{1,0:T(8,128)(2,1)S(1)} %copy-done.2), channel_id=1, source_target_pairs={{0,63},{1,0},{2,1},{3,2},{4,3},{5,4},{6,5},{7,6},{8,7},{9,8},{10,9... | collective-permute-start | bytes 2027528 | tf_op jit(solution)/shard_map/ppermute | solution.py:260
  87.7 7.7 %all-to-all-done.2 = bf16[8,4,56,128]{3,2,1,0:T(8,128)(2,1)S(1)} async-done(((bf16[8,4,56,128]{3,2,1,0:T(8,128)(2,1)}), bf16[8,4,56,128]{3,2,1,0:T(8,128)(2,1)S(1)}, u32[]{:S(2)}, u32[]{:S(2)}) %all-to-all-start.2) | async-done | bytes 458784 | tf_op jit(solution)/shard_map/all_to_all | solution.py:327
  95.4 0.1 reduce_sum.37
  95.5 0.7 broadcast_in_dim.12
  96.2 12.0 %all-to-all-start.3 = ((bf16[16,56,128]{2,1,0:T(8,128)(2,1)}), bf16[16,56,128]{2,1,0:T(8,128)(2,1)S(1)}, u32[]{:S(2)}, u32[]{:S(2)}) async-start(bf16[16,56,128]{2,1,0:T(8,128)(2,1)} %bitcast.7), calls=%async_computation.3 | async-start | bytes 458752 | tf_op jit(solution)/shard_map/all_to_all | solution.py:359
  108.2 0.0 all-gather.2.cloned.1.call-done
  108.2 0.0 copy-start.1
  108.2 7.9 %shard_map.113.d_attn = bf16[128,1280]{1,0:T(8,128)(2,1)S(1)} custom-call(bf16[8,160,2560]{2,1,0:T(8,128)(2,1)} %bitcast.14, bf16[128,2560]{1,0:T(8,128)(2,1)} %get-tuple-element.27.grads), custom_call_target="tpu_custom_call" | custom-call | tf_op jit(solution)/shard_map/pallas_call | solution.py:332
  116.1 0.0 collective-permute-done.behind
  116.1 0.0 collective-permute-done.1.ahead
  116.1 0.0 copy-done.1
  116.1 8.9 %shard_map.114 = (bf16[128,1280]{1,0:T(8,128)(2,1)}, f32[2,128,1280]{2,1,0:T(8,128)}, bf16[2,128,1280]{2,1,0:T(8,128)(2,1)}, bf16[2,128,1280]{2,1,0:T(8,128)(2,1)}) custom-call(s32[1]{0:T(128)S(6)} %copy.12.counts, s32[4,12]{1,0:T(4,128)S(1)} %bitcast.13, bf16[128,1280]{1,0:T(8,128)(2,1)S(1)} %shard_map.113.d_attn, ...), custom_call_target="tpu_custom_call" | custom-call | tf_op jit(solution)/shard_map/pallas_call | solution.py:346
  125.0 0.0 all-to-all-done.3
  125.1 0.8 broadcast_in_dim.14
  125.9 4.9 %all-to-all-start.4 = ((bf16[8,4,56,128]{3,2,1,0:T(8,128)(2,1)}), bf16[8,4,56,128]{3,2,1,0:T(8,128)(2,1)S(1)}, u32[]{:S(2)}, u32[]{:S(2)}) async-start(bf16[8,4,56,128]{3,2,1,0:T(8,128)(2,1)} %broadcast_in_dim.14), calls=%async_computation.4 | async-start | bytes 917504 | tf_op jit(solution)/shard_map/all_to_all | solution.py:362
  130.8 0.0 copy-start
  130.8 4.1 %collective-permute-start.2 = (bf16[2,128,1280]{2,1,0:T(8,128)(2,1)}, bf16[2,128,1280]{2,1,0:T(8,128)(2,1)S(1)}, u32[]{:S(2)}, u32[]{:S(2)}) collective-permute-start(bf16[2,128,1280]{2,1,0:T(8,128)(2,1)} %get-tuple-element.35), channel_id=1, source_target_pairs={{0,1},{1,2},{2,3},{3,4},{4,5},{5,6},{6,7},{7,8},{8,9},{9,10},{10,1... | collective-permute-start | bytes 1966088 | tf_op jit(solution)/shard_map/ppermute | solution.py:260
  134.9 1.9 %collective-permute-start.3 = (bf16[2,128,1280]{2,1,0:T(8,128)(2,1)}, bf16[2,128,1280]{2,1,0:T(8,128)(2,1)S(1)}, u32[]{:S(2)}, u32[]{:S(2)}) collective-permute-start(bf16[2,128,1280]{2,1,0:T(8,128)(2,1)} %get-tuple-element.36), channel_id=1, source_target_pairs={{0,63},{1,0},{2,1},{3,2},{4,3},{5,4},{6,5},{7,6},{8,7},{9,8},{10,9... | collective-permute-start | bytes 1966088 | tf_op jit(solution)/shard_map/ppermute | solution.py:260
  136.9 9.7 %all-to-all-done.4 = bf16[8,4,56,128]{3,2,1,0:T(8,128)(2,1)S(1)} async-done(((bf16[8,4,56,128]{3,2,1,0:T(8,128)(2,1)}), bf16[8,4,56,128]{3,2,1,0:T(8,128)(2,1)S(1)}, u32[]{:S(2)}, u32[]{:S(2)}) %all-to-all-start.4) | async-done | bytes 458784 | tf_op jit(solution)/shard_map/all_to_all | solution.py:362
  146.6 0.1 broadcast_in_dim.30
  146.7 5.4 %all_to_all.32.both = bf16[2,8,4,56,128]{4,3,2,1,0:T(8,128)(2,1)S(1)} all-to-all(bf16[2,8,4,56,128]{4,3,2,1,0:T(8,128)(2,1)S(1)} %broadcast_in_dim.30), channel_id=1, replica_groups=mesh['z_lo'=2,'x'=4,'y'=8,'z_hi'=4,'core'=2] {'core'}, dimensions={0} | all-to-all | bytes 1835008 | tf_op jit(solution)/shard_map/all_to_all | solution.py:363
  152.1 1.0 shard_map.115
  153.1 0.0 collective-permute-done.2.from_behind
  153.1 3.3 %collective-permute-done.3.from_ahead = bf16[2,128,1280]{2,1,0:T(8,128)(2,1)S(1)} collective-permute-done((bf16[2,128,1280]{2,1,0:T(8,128)(2,1)}, bf16[2,128,1280]{2,1,0:T(8,128)(2,1)S(1)}, u32[]{:S(2)}, u32[]{:S(2)}) %collective-permute-start.3) | collective-permute-done | bytes 655392 | tf_op jit(solution)/shard_map/ppermute | solution.py:260
  156.4 0.0 copy-done
  156.4 1.0 shard_map.116
  (1 shorter events, 0.0 us)
Async XLA Ops:
  7.2 101.0 %all-gather.2.cloned.1.call-start = ((), (), s32[]{:S(2)}) async-start(), calls=%async_computation.6 | async-start | bytes 6963200 | tf_op jit(solution)/shard_map/all_gather | solution.py:305
  56.6 22.3 %copy-start.2 = (bf16[264,1280]{1,0:T(8,128)(2,1)S(1)}, bf16[264,1280]{1,0:T(8,128)(2,1)}, u32[]{:S(2)}) copy-start(bf16[264,1280]{1,0:T(8,128)(2,1)} %get-tuple-element.28) | copy-start | bytes 2027524
  73.5 22.0 %all-to-all-start.2 = ((bf16[8,4,56,128]{3,2,1,0:T(8,128)(2,1)}), bf16[8,4,56,128]{3,2,1,0:T(8,128)(2,1)S(1)}, u32[]{:S(2)}, u32[]{:S(2)}) async-start(bf16[8,4,56,128]{3,2,1,0:T(8,128)(2,1)} %reduce_sum.36), calls=%async_computation.2 | async-start | bytes 917504 | tf_op jit(solution)/shard_map/all_to_all | solution.py:327
  78.9 37.2 %collective-permute-start = (bf16[264,1280]{1,0:T(8,128)(2,1)S(1)}, bf16[264,1280]{1,0:T(8,128)(2,1)S(1)}, u32[]{:S(2)}, u32[]{:S(2)}) collective-permute-start(bf16[264,1280]{1,0:T(8,128)(2,1)S(1)} %copy-done.2), channel_id=1, source_target_pairs={{0,1},{1,2},{2,3},{3,4},{4,5},{5,6},{6,7},{7,8},{8,9},{9,10},{10,1... | collective-permute-start | bytes 2027528 | tf_op jit(solution)/shard_map/ppermute | solution.py:260
  85.8 30.3 %collective-permute-start.1 = (bf16[264,1280]{1,0:T(8,128)(2,1)S(1)}, bf16[264,1280]{1,0:T(8,128)(2,1)S(1)}, u32[]{:S(2)}, u32[]{:S(2)}) collective-permute-start(bf16[264,1280]{1,0:T(8,128)(2,1)S(1)} %copy-done.2), channel_id=1, source_target_pairs={{0,63},{1,0},{2,1},{3,2},{4,3},{5,4},{6,5},{7,6},{8,7},{9,8},{10,9... | collective-permute-start | bytes 2027528 | tf_op jit(solution)/shard_map/ppermute | solution.py:260
  96.2 28.8 %all-to-all-start.3 = ((bf16[16,56,128]{2,1,0:T(8,128)(2,1)}), bf16[16,56,128]{2,1,0:T(8,128)(2,1)S(1)}, u32[]{:S(2)}, u32[]{:S(2)}) async-start(bf16[16,56,128]{2,1,0:T(8,128)(2,1)} %bitcast.7), calls=%async_computation.3 | async-start | bytes 458752 | tf_op jit(solution)/shard_map/all_to_all | solution.py:359
  108.2 7.9 %copy-start.1 = (s32[1,4,12]{2,1,0:T(4,128)S(1)}, s32[1,4,12]{2,1,0:T(4,128)}, u32[]{:S(2)}) copy-start(s32[1,4,12]{2,1,0:T(4,128)} %param.14) | copy-start | bytes 580
  125.9 20.6 %all-to-all-start.4 = ((bf16[8,4,56,128]{3,2,1,0:T(8,128)(2,1)}), bf16[8,4,56,128]{3,2,1,0:T(8,128)(2,1)S(1)}, u32[]{:S(2)}, u32[]{:S(2)}) async-start(bf16[8,4,56,128]{3,2,1,0:T(8,128)(2,1)} %broadcast_in_dim.14), calls=%async_computation.4 | async-start | bytes 917504 | tf_op jit(solution)/shard_map/all_to_all | solution.py:362
  130.8 25.6 %copy-start = (f32[2,128,1280]{2,1,0:T(8,128)S(1)}, f32[2,128,1280]{2,1,0:T(8,128)}, u32[]{:S(2)}) copy-start(f32[2,128,1280]{2,1,0:T(8,128)} %get-tuple-element.34.own) | copy-start | bytes 3932164
  130.8 22.3 %collective-permute-start.2 = (bf16[2,128,1280]{2,1,0:T(8,128)(2,1)}, bf16[2,128,1280]{2,1,0:T(8,128)(2,1)S(1)}, u32[]{:S(2)}, u32[]{:S(2)}) collective-permute-start(bf16[2,128,1280]{2,1,0:T(8,128)(2,1)} %get-tuple-element.35), channel_id=1, source_target_pairs={{0,1},{1,2},{2,3},{3,4},{4,5},{5,6},{6,7},{7,8},{8,9},{9,10},{10,1... | collective-permute-start | bytes 1966088 | tf_op jit(solution)/shard_map/ppermute | solution.py:260
  134.9 21.4 %collective-permute-start.3 = (bf16[2,128,1280]{2,1,0:T(8,128)(2,1)}, bf16[2,128,1280]{2,1,0:T(8,128)(2,1)S(1)}, u32[]{:S(2)}, u32[]{:S(2)}) collective-permute-start(bf16[2,128,1280]{2,1,0:T(8,128)(2,1)} %get-tuple-element.36), channel_id=1, source_target_pairs={{0,63},{1,0},{2,1},{3,2},{4,3},{5,4},{6,5},{7,6},{8,7},{9,8},{10,9... | collective-permute-start | bytes 1966088 | tf_op jit(solution)/shard_map/ppermute | solution.py:260
Sparse Core Ops, SparseCore 0:
  11.5 70.2 all-gather.1

commit v7 on v6

--- a/solution.py
+++ b/solution.py
@@ -321,14 +321,7 @@
 
     pair = lax.all_to_all(weight, "core", 0, 0)
     terms = jnp.sum(pair.astype(F32), axis=0).astype(BF)
-    terms, halo = lax.optimization_barrier((terms, halo))
-    behind = shift(halo, 1)
-    ahead = shift(halo, -1)
-    terms = lax.all_to_all(terms, "y", 0, 0)
-    terms = jnp.sum(terms.astype(F32), axis=0).astype(BF)
-    terms = jnp.broadcast_to(terms[:, None], (down, across, share, LANES))
-    terms = terms.reshape(down * across, share, LANES)
-    terms, grads = lax.optimization_barrier((terms, grads))
+    terms, halo, grads = lax.optimization_barrier((terms, halo, grads))
     (d_attn,) = call(
         project_body,
         [((rows, hw), BF)],
@@ -340,6 +333,14 @@
             pltpu.SemaphoreType.DMA((1,)),
         ],
     )(in_hbm(w_all.reshape(HEADS, HD, width)), in_hbm(grads))
+    behind = shift(halo, 1)
+    ahead = shift(halo, -1)
+    terms = lax.all_to_all(terms, "y", 0, 0)
+    terms, d_attn = lax.optimization_barrier((terms, d_attn))
+    terms = jnp.sum(terms.astype(F32), axis=0).astype(BF)
+    terms = jnp.broadcast_to(terms[:, None], (down, across, share, LANES))
+    terms = terms.reshape(down * across, share, LANES)
+    terms, d_attn = lax.optimization_barrier((terms, d_attn))
     operands = (queries, keys, attn_out, values)
     pairs = (2, rows, hw)
     results = (((rows, hw), BF), (pairs, F32), (pairs, BF), (pairs, BF))

time: 166 us -> 164 us (0.988)
  waiting for transfers between devices: 20.7 us -> 13.1 us
  blocking collectives: 63.8 us -> 66.9 us
  starting transfers between devices: 37.2 us -> 39.7 us
    all_to_all x1, waiting for transfers between devices: 7.71 us -> 0.01 us  [local(): terms = lax.all_to_all(terms, 'y', 0, 0)]
    all_to_all x1, waiting for transfers between devices: 9.69 us -> 5.4 us  [local(): total = lax.all_to_all(spread_out(total, chips), 'y', 0, 0)]
    ppermute x4, waiting for transfers between devices: 3.26 us -> 7.27 us  [shift(): lax.ppermute(value, REGION, [(i, (i + by) % length) for i in range(length)])]
    all_to_all x1, blocking collectives: 5.39 us -> 8.52 us  [local(): both = lax.all_to_all(spread_out(total, cores), 'core', 0, 0)]
  transfers between devices with their start and end apart: 8 -> 8, of which waited for: 3 -> 4; matrix products, arithmetic and copies ran while one was open for 1% -> 1% of each run, Pallas kernels for 12% -> 13%
where the time goes in v7:
time: 164 us; the launch traced here: 162 us
  blocking collectives  66.9 us (41%)
  starting transfers between devices  39.7 us (24%)
  Pallas kernels  24.8 us (15%)
  between operations  14.8 us (9%)
  waiting for transfers between devices  13.1 us (8%)
  local copies, waits for them, and re-layouts  1.68 us (1%)
    all_to_all x1, blocking collectives, local(): gathered = lax.all_to_all(spread, DP, 0, 0)  42.6 us
    ppermute x4, starting transfers between devices, shift(): lax.ppermute(value, REGION, [(i, (i + by) % length) for i in range(length)])  16 us
    all_to_all x1, blocking collectives, local(): pair = lax.all_to_all(weight, 'core', 0, 0)  15.8 us
    all_to_all x1, starting transfers between devices, local(): lax.all_to_all(terms, ('x', 'z_hi'), 0, 0)  11.7 us
    pallas_call x1, Pallas kernels, local(): pl.pallas_call(attention_body, out_shape=tuple((pltpu.HBM(shape, dtype) f...  8.9 us
    all_to_all x1, blocking collectives, local(): both = lax.all_to_all(spread_out(total, cores), 'core', 0, 0)  8.52 us
    pallas_call x1, Pallas kernels, local(): call(project_body, [((rows, hw), BF)], [hbm(), hbm()], [pltpu.VMEM((HEADS...  7.87 us
    ppermute x4, waiting for transfers between devices, shift(): lax.ppermute(value, REGION, [(i, (i + by) % length) for i in range(length)])  7.27 us
  transfers between devices with their start and end apart: 8, of which 4 were waited for; matrix products, arithmetic and copies ran while one was open for 1% of the time, Pallas kernels for 13%

profile of v7, /device:TPU:1, one launch (start us, length us, event | category | flops | bytes accessed | tf_op | source)
XLA Modules:
  0.0 162.3 jit_solution(1063403476757683861)
XLA Ops:
  7.2 0.0 all-gather.2.cloned.1.call-start
  7.9 3.5 %shard_map.111 = (bf16[80,2560]{1,0:T(8,128)(2,1)}, bf16[8,256,640]{2,1,0:T(8,128)(2,1)}, bf16[128,2560]{1,0:T(8,128)(2,1)}, bf16[264,1280]{1,0:T(8,128)(2,1)}) custom-call(s32[1]{0:T(128)S(6)} %copy.12.counts, s32[1]{0:T(128)} %bitcast.1.core, bf16[128,2560]{1,0:T(8,128)(2,1)} %bitcast.22, bf16[128,1280]{1,0:T(8,128)(2,1)} %bitcast.15, ...), custom_call_target="tpu_custom_call" | custom-call | tf_op jit(solution)/shard_map/pallas_call | solution.py:282
  11.4 0.0 all-gather.2.cloned.1.call-update
  11.4 42.6 %all_to_all.30.gathered = bf16[8,256,640]{2,1,0:T(8,128)(2,1)S(1)} all-to-all(bf16[8,256,640]{2,1,0:T(8,128)(2,1)} %get-tuple-element.25), channel_id=1, replica_groups=mesh['z_lo'=2,'x'=4,'y'=8,'z_hi'=4,'core'=2] {'z_lo','x'}, dimensions={0} | all-to-all | bytes 5242880 | tf_op jit(solution)/shard_map/all_to_all | solution.py:307
  54.0 2.6 %shard_map.112 = bf16[2,8,4,56,128]{4,3,2,1,0:T(8,128)(2,1)S(1)} custom-call(bf16[8,256,640]{2,1,0:T(8,128)(2,1)S(1)} %all_to_all.30.gathered), custom_call_target="tpu_custom_call" | custom-call | tf_op jit(solution)/shard_map/pallas_call | solution.py:312
  56.6 0.0 copy-start.2
  56.6 15.8 %all_to_all.31 = bf16[2,8,4,56,128]{4,3,2,1,0:T(8,128)(2,1)S(1)} all-to-all(bf16[2,8,4,56,128]{4,3,2,1,0:T(8,128)(2,1)S(1)} %shard_map.112), channel_id=1, replica_groups=mesh['z_lo'=2,'x'=4,'y'=8,'z_hi'=4,'core'=2] {'core'}, dimensions={0} | all-to-all | bytes 1835008 | tf_op jit(solution)/shard_map/all_to_all | solution.py:322
  72.4 1.1 reduce_sum.36
  73.5 5.4 %all-to-all-start.2 = ((bf16[8,4,56,128]{3,2,1,0:T(8,128)(2,1)}), bf16[8,4,56,128]{3,2,1,0:T(8,128)(2,1)S(1)}, u32[]{:S(2)}, u32[]{:S(2)}) async-start(bf16[8,4,56,128]{3,2,1,0:T(8,128)(2,1)} %reduce_sum.36), calls=%async_computation.2 | async-start | bytes 917504 | tf_op jit(solution)/shard_map/all_to_all | solution.py:338
  78.9 0.0 copy-done.2
  78.9 6.9 %collective-permute-start = (bf16[264,1280]{1,0:T(8,128)(2,1)S(1)}, bf16[264,1280]{1,0:T(8,128)(2,1)S(1)}, u32[]{:S(2)}, u32[]{:S(2)}) collective-permute-start(bf16[264,1280]{1,0:T(8,128)(2,1)S(1)} %copy-done.2), channel_id=1, source_target_pairs={{0,1},{1,2},{2,3},{3,4},{4,5},{5,6},{6,7},{7,8},{8,9},{9,10},{10,1... | collective-permute-start | bytes 2027528 | tf_op jit(solution)/shard_map/ppermute | solution.py:260
  85.8 1.9 %collective-permute-start.1 = (bf16[264,1280]{1,0:T(8,128)(2,1)S(1)}, bf16[264,1280]{1,0:T(8,128)(2,1)S(1)}, u32[]{:S(2)}, u32[]{:S(2)}) collective-permute-start(bf16[264,1280]{1,0:T(8,128)(2,1)S(1)} %copy-done.2), channel_id=1, source_target_pairs={{0,63},{1,0},{2,1},{3,2},{4,3},{5,4},{6,5},{7,6},{8,7},{9,8},{10,9... | collective-permute-start | bytes 2027528 | tf_op jit(solution)/shard_map/ppermute | solution.py:260
  87.7 0.0 all-gather.2.cloned.1.call-done
  87.7 0.0 copy-start.1
  87.7 7.9 %shard_map.113.d_attn = bf16[128,1280]{1,0:T(8,128)(2,1)S(1)} custom-call(bf16[8,160,2560]{2,1,0:T(8,128)(2,1)} %bitcast.14, bf16[128,2560]{1,0:T(8,128)(2,1)} %get-tuple-element.30.grads), custom_call_target="tpu_custom_call" | custom-call | tf_op jit(solution)/shard_map/pallas_call | solution.py:325
  95.6 0.0 all-to-all-done.2
  95.6 0.1 reduce_sum.37
  95.7 0.7 broadcast_in_dim.12
  96.4 11.7 %all-to-all-start.3 = ((bf16[16,56,128]{2,1,0:T(8,128)(2,1)}), bf16[16,56,128]{2,1,0:T(8,128)(2,1)S(1)}, u32[]{:S(2)}, u32[]{:S(2)}) async-start(bf16[16,56,128]{2,1,0:T(8,128)(2,1)} %bitcast.7), calls=%async_computation.3 | async-start | bytes 458752 | tf_op jit(solution)/shard_map/all_to_all | solution.py:360
  108.2 0.0 collective-permute-done.behind
  108.2 1.9 %collective-permute-done.1.ahead = bf16[264,1280]{1,0:T(8,128)(2,1)S(1)} collective-permute-done((bf16[264,1280]{1,0:T(8,128)(2,1)S(1)}, bf16[264,1280]{1,0:T(8,128)(2,1)S(1)}, u32[]{:S(2)}, u32[]{:S(2)}) %collective-permute-start.1) | collective-permute-done | bytes 675872 | tf_op jit(solution)/shard_map/ppermute | solution.py:260
  110.1 0.0 copy-done.1
  110.1 8.9 %shard_map.114 = (bf16[128,1280]{1,0:T(8,128)(2,1)}, f32[2,128,1280]{2,1,0:T(8,128)}, bf16[2,128,1280]{2,1,0:T(8,128)(2,1)}, bf16[2,128,1280]{2,1,0:T(8,128)(2,1)}) custom-call(s32[1]{0:T(128)S(6)} %copy.12.counts, s32[4,12]{1,0:T(4,128)S(1)} %bitcast.13, bf16[128,1280]{1,0:T(8,128)(2,1)S(1)} %shard_map.113.d_attn, ...), custom_call_target="tpu_custom_call" | custom-call | tf_op jit(solution)/shard_map/pallas_call | solution.py:347
  119.0 0.4 all-to-all-done.3
  119.4 0.8 broadcast_in_dim.14
  120.3 6.5 %all-to-all-start.4 = ((bf16[8,4,56,128]{3,2,1,0:T(8,128)(2,1)}), bf16[8,4,56,128]{3,2,1,0:T(8,128)(2,1)S(1)}, u32[]{:S(2)}, u32[]{:S(2)}) async-start(bf16[8,4,56,128]{3,2,1,0:T(8,128)(2,1)} %broadcast_in_dim.14), calls=%async_computation.4 | async-start | bytes 917504 | tf_op jit(solution)/shard_map/all_to_all | solution.py:363
  126.8 0.0 copy-start
  126.8 3.9 %collective-permute-start.2 = (bf16[2,128,1280]{2,1,0:T(8,128)(2,1)}, bf16[2,128,1280]{2,1,0:T(8,128)(2,1)S(1)}, u32[]{:S(2)}, u32[]{:S(2)}) collective-permute-start(bf16[2,128,1280]{2,1,0:T(8,128)(2,1)} %get-tuple-element.41), channel_id=1, source_target_pairs={{0,1},{1,2},{2,3},{3,4},{4,5},{5,6},{6,7},{7,8},{8,9},{9,10},{10,1... | collective-permute-start | bytes 1966088 | tf_op jit(solution)/shard_map/ppermute | solution.py:260
  130.7 3.3 %collective-permute-start.3 = (bf16[2,128,1280]{2,1,0:T(8,128)(2,1)}, bf16[2,128,1280]{2,1,0:T(8,128)(2,1)S(1)}, u32[]{:S(2)}, u32[]{:S(2)}) collective-permute-start(bf16[2,128,1280]{2,1,0:T(8,128)(2,1)} %get-tuple-element.42), channel_id=1, source_target_pairs={{0,63},{1,0},{2,1},{3,2},{4,3},{5,4},{6,5},{7,6},{8,7},{9,8},{10,9... | collective-permute-start | bytes 1966088 | tf_op jit(solution)/shard_map/ppermute | solution.py:260
  134.0 5.4 %all-to-all-done.4 = bf16[8,4,56,128]{3,2,1,0:T(8,128)(2,1)S(1)} async-done(((bf16[8,4,56,128]{3,2,1,0:T(8,128)(2,1)}), bf16[8,4,56,128]{3,2,1,0:T(8,128)(2,1)S(1)}, u32[]{:S(2)}, u32[]{:S(2)}) %all-to-all-start.4) | async-done | bytes 458784 | tf_op jit(solution)/shard_map/all_to_all | solution.py:363
  139.4 0.1 broadcast_in_dim.30
  139.6 8.5 %all_to_all.32.both = bf16[2,8,4,56,128]{4,3,2,1,0:T(8,128)(2,1)S(1)} all-to-all(bf16[2,8,4,56,128]{4,3,2,1,0:T(8,128)(2,1)S(1)} %broadcast_in_dim.30), channel_id=1, replica_groups=mesh['z_lo'=2,'x'=4,'y'=8,'z_hi'=4,'core'=2] {'core'}, dimensions={0} | all-to-all | bytes 1835008 | tf_op jit(solution)/shard_map/all_to_all | solution.py:364
  148.1 1.0 shard_map.115
  149.1 0.0 collective-permute-done.2.from_behind
  149.1 5.4 %collective-permute-done.3.from_ahead = bf16[2,128,1280]{2,1,0:T(8,128)(2,1)S(1)} collective-permute-done((bf16[2,128,1280]{2,1,0:T(8,128)(2,1)}, bf16[2,128,1280]{2,1,0:T(8,128)(2,1)S(1)}, u32[]{:S(2)}, u32[]{:S(2)}) %collective-permute-start.3) | collective-permute-done | bytes 655392 | tf_op jit(solution)/shard_map/ppermute | solution.py:260
  154.5 0.0 copy-done
  154.5 1.0 shard_map.116
  (1 shorter events, 0.0 us)
Async XLA Ops:
  7.2 80.6 %all-gather.2.cloned.1.call-start = ((), (), s32[]{:S(2)}) async-start(), calls=%async_computation.6 | async-start | bytes 6963200 | tf_op jit(solution)/shard_map/all_gather | solution.py:305
  56.6 22.3 %copy-start.2 = (bf16[264,1280]{1,0:T(8,128)(2,1)S(1)}, bf16[264,1280]{1,0:T(8,128)(2,1)}, u32[]{:S(2)}) copy-start(bf16[264,1280]{1,0:T(8,128)(2,1)} %get-tuple-element.34) | copy-start | bytes 2027524
  73.5 22.2 %all-to-all-start.2 = ((bf16[8,4,56,128]{3,2,1,0:T(8,128)(2,1)}), bf16[8,4,56,128]{3,2,1,0:T(8,128)(2,1)S(1)}, u32[]{:S(2)}, u32[]{:S(2)}) async-start(bf16[8,4,56,128]{3,2,1,0:T(8,128)(2,1)} %reduce_sum.36), calls=%async_computation.2 | async-start | bytes 917504 | tf_op jit(solution)/shard_map/all_to_all | solution.py:338
  78.9 29.3 %collective-permute-start = (bf16[264,1280]{1,0:T(8,128)(2,1)S(1)}, bf16[264,1280]{1,0:T(8,128)(2,1)S(1)}, u32[]{:S(2)}, u32[]{:S(2)}) collective-permute-start(bf16[264,1280]{1,0:T(8,128)(2,1)S(1)} %copy-done.2), channel_id=1, source_target_pairs={{0,1},{1,2},{2,3},{3,4},{4,5},{5,6},{6,7},{7,8},{8,9},{9,10},{10,1... | collective-permute-start | bytes 2027528 | tf_op jit(solution)/shard_map/ppermute | solution.py:260
  85.8 24.3 %collective-permute-start.1 = (bf16[264,1280]{1,0:T(8,128)(2,1)S(1)}, bf16[264,1280]{1,0:T(8,128)(2,1)S(1)}, u32[]{:S(2)}, u32[]{:S(2)}) collective-permute-start(bf16[264,1280]{1,0:T(8,128)(2,1)S(1)} %copy-done.2), channel_id=1, source_target_pairs={{0,63},{1,0},{2,1},{3,2},{4,3},{5,4},{6,5},{7,6},{8,7},{9,8},{10,9... | collective-permute-start | bytes 2027528 | tf_op jit(solution)/shard_map/ppermute | solution.py:260
  87.7 22.3 %copy-start.1 = (s32[1,4,12]{2,1,0:T(4,128)S(1)}, s32[1,4,12]{2,1,0:T(4,128)}, u32[]{:S(2)}) copy-start(s32[1,4,12]{2,1,0:T(4,128)} %param.14) | copy-start | bytes 580
  96.4 23.0 %all-to-all-start.3 = ((bf16[16,56,128]{2,1,0:T(8,128)(2,1)}), bf16[16,56,128]{2,1,0:T(8,128)(2,1)S(1)}, u32[]{:S(2)}, u32[]{:S(2)}) async-start(bf16[16,56,128]{2,1,0:T(8,128)(2,1)} %bitcast.7), calls=%async_computation.3 | async-start | bytes 458752 | tf_op jit(solution)/shard_map/all_to_all | solution.py:360
  120.3 19.2 %all-to-all-start.4 = ((bf16[8,4,56,128]{3,2,1,0:T(8,128)(2,1)}), bf16[8,4,56,128]{3,2,1,0:T(8,128)(2,1)S(1)}, u32[]{:S(2)}, u32[]{:S(2)}) async-start(bf16[8,4,56,128]{3,2,1,0:T(8,128)(2,1)} %broadcast_in_dim.14), calls=%async_computation.4 | async-start | bytes 917504 | tf_op jit(solution)/shard_map/all_to_all | solution.py:363
  126.8 27.7 %copy-start = (f32[2,128,1280]{2,1,0:T(8,128)S(1)}, f32[2,128,1280]{2,1,0:T(8,128)}, u32[]{:S(2)}) copy-start(f32[2,128,1280]{2,1,0:T(8,128)} %get-tuple-element.40.own) | copy-start | bytes 3932164
  126.8 22.3 %collective-permute-start.2 = (bf16[2,128,1280]{2,1,0:T(8,128)(2,1)}, bf16[2,128,1280]{2,1,0:T(8,128)(2,1)S(1)}, u32[]{:S(2)}, u32[]{:S(2)}) collective-permute-start(bf16[2,128,1280]{2,1,0:T(8,128)(2,1)} %get-tuple-element.41), channel_id=1, source_target_pairs={{0,1},{1,2},{2,3},{3,4},{4,5},{5,6},{6,7},{7,8},{8,9},{9,10},{10,1... | collective-permute-start | bytes 1966088 | tf_op jit(solution)/shard_map/ppermute | solution.py:260
  130.7 23.8 %collective-permute-start.3 = (bf16[2,128,1280]{2,1,0:T(8,128)(2,1)}, bf16[2,128,1280]{2,1,0:T(8,128)(2,1)S(1)}, u32[]{:S(2)}, u32[]{:S(2)}) collective-permute-start(bf16[2,128,1280]{2,1,0:T(8,128)(2,1)} %get-tuple-element.42), channel_id=1, source_target_pairs={{0,63},{1,0},{2,1},{3,2},{4,3},{5,4},{6,5},{7,6},{8,7},{9,8},{10,9... | collective-permute-start | bytes 1966088 | tf_op jit(solution)/shard_map/ppermute | solution.py:260
Sparse Core Ops, SparseCore 0:
  11.5 70.2 all-gather.1

commit v8 on v7

--- a/solution.py
+++ b/solution.py
@@ -163,8 +163,9 @@
     for w_load in w_loads:
         w_load.start()
     load.wait()
+    for w_load in w_loads:
+        w_load.wait()
     for h in range(HEADS):
-        w_loads[h].wait()
         d_attn[:, h * HD : (h + 1) * HD] = nt(grads_in[...], w_in[h]).astype(BF)
 
 

time: 164 us -> 164 us (level)
  waiting for transfers between devices: 13.1 us -> 17.3 us
  blocking collectives: 66.9 us -> 63.8 us
  Pallas kernels: 24.8 us -> 22.3 us
    all_to_all x1, waiting for transfers between devices: 5.4 us -> 10.7 us  [local(): total = lax.all_to_all(spread_out(total, chips), 'y', 0, 0)]
    ppermute x4, waiting for transfers between devices: 7.27 us -> 3.82 us  [shift(): lax.ppermute(value, REGION, [(i, (i + by) % length) for i in range(length)])]
    all_to_all x1, starting transfers between devices: 6.54 us -> 9.96 us  [local(): total = lax.all_to_all(spread_out(total, chips), 'y', 0, 0)]
    all_to_all x1, blocking collectives: 8.52 us -> 5.42 us  [local(): both = lax.all_to_all(spread_out(total, cores), 'core', 0, 0)]
    pallas_call x1, Pallas kernels: 7.87 us -> 5.32 us  [local(): call(project_body, [((rows, hw), BF)], [hbm(), hbm()], [pltpu.VMEM((HEADS...]
    all_to_all x1, waiting for transfers between devices: 0.01 us -> 2.34 us  [local(): terms = lax.all_to_all(terms, 'y', 0, 0)]
    ppermute x4, starting transfers between devices: 16 us -> 13.9 us  [shift(): lax.ppermute(value, REGION, [(i, (i + by) % length) for i in range(length)])]
  transfers between devices with their start and end apart: 8 -> 8, of which waited for: 4 -> 5; matrix products, arithmetic and copies ran while one was open for 1% -> 1% of each run, Pallas kernels for 13% -> 11%
where the time goes in v8:
time: 164 us; the launch traced here: 162 us
  blocking collectives  63.8 us (39%)
  starting transfers between devices  41.2 us (25%)
  Pallas kernels  22.3 us (14%)
  waiting for transfers between devices  17.3 us (11%)
  between operations  14.8 us (9%)
  local copies, waits for them, and re-layouts  1.68 us (1%)
    all_to_all x1, blocking collectives, local(): gathered = lax.all_to_all(spread, DP, 0, 0)  42.6 us
    all_to_all x1, blocking collectives, local(): pair = lax.all_to_all(weight, 'core', 0, 0)  15.8 us
    ppermute x4, starting transfers between devices, shift(): lax.ppermute(value, REGION, [(i, (i + by) % length) for i in range(length)])  13.9 us
    all_to_all x1, starting transfers between devices, local(): lax.all_to_all(terms, ('x', 'z_hi'), 0, 0)  12 us
    all_to_all x1, waiting for transfers between devices, local(): total = lax.all_to_all(spread_out(total, chips), 'y', 0, 0)  10.7 us
    all_to_all x1, starting transfers between devices, local(): total = lax.all_to_all(spread_out(total, chips), 'y', 0, 0)  9.96 us
    pallas_call x1, Pallas kernels, local(): pl.pallas_call(attention_body, out_shape=tuple((pltpu.HBM(shape, dtype) f...  8.9 us
    all_to_all x1, blocking collectives, local(): both = lax.all_to_all(spread_out(total, cores), 'core', 0, 0)  5.42 us
  transfers between devices with their start and end apart: 8, of which 5 were waited for; matrix products, arithmetic and copies ran while one was open for 1% of the time, Pallas kernels for 11%

profile of v8, /device:TPU:1, one launch (start us, length us, event | category | flops | bytes accessed | tf_op | source)
XLA Modules:
  0.0 162.3 jit_solution(5416464013979542257)
XLA Ops:
  7.2 0.0 all-gather.2.cloned.1.call-start
  7.9 3.5 %shard_map.111 = (bf16[80,2560]{1,0:T(8,128)(2,1)}, bf16[8,256,640]{2,1,0:T(8,128)(2,1)}, bf16[128,2560]{1,0:T(8,128)(2,1)}, bf16[264,1280]{1,0:T(8,128)(2,1)}) custom-call(s32[1]{0:T(128)S(6)} %copy.12.counts, s32[1]{0:T(128)} %bitcast.1.core, bf16[128,2560]{1,0:T(8,128)(2,1)} %bitcast.22, bf16[128,1280]{1,0:T(8,128)(2,1)} %bitcast.15, ...), custom_call_target="tpu_custom_call" | custom-call | tf_op jit(solution)/shard_map/pallas_call | solution.py:283
  11.4 0.0 all-gather.2.cloned.1.call-update
  11.4 42.6 %all_to_all.30.gathered = bf16[8,256,640]{2,1,0:T(8,128)(2,1)S(1)} all-to-all(bf16[8,256,640]{2,1,0:T(8,128)(2,1)} %get-tuple-element.25), channel_id=1, replica_groups=mesh['z_lo'=2,'x'=4,'y'=8,'z_hi'=4,'core'=2] {'z_lo','x'}, dimensions={0} | all-to-all | bytes 5242880 | tf_op jit(solution)/shard_map/all_to_all | solution.py:308
  54.0 2.6 %shard_map.112 = bf16[2,8,4,56,128]{4,3,2,1,0:T(8,128)(2,1)S(1)} custom-call(bf16[8,256,640]{2,1,0:T(8,128)(2,1)S(1)} %all_to_all.30.gathered), custom_call_target="tpu_custom_call" | custom-call | tf_op jit(solution)/shard_map/pallas_call | solution.py:313
  56.6 0.0 copy-start.2
  56.6 15.8 %all_to_all.31 = bf16[2,8,4,56,128]{4,3,2,1,0:T(8,128)(2,1)S(1)} all-to-all(bf16[2,8,4,56,128]{4,3,2,1,0:T(8,128)(2,1)S(1)} %shard_map.112), channel_id=1, replica_groups=mesh['z_lo'=2,'x'=4,'y'=8,'z_hi'=4,'core'=2] {'core'}, dimensions={0} | all-to-all | bytes 1835008 | tf_op jit(solution)/shard_map/all_to_all | solution.py:323
  72.4 1.1 reduce_sum.36
  73.5 5.4 %all-to-all-start.2 = ((bf16[8,4,56,128]{3,2,1,0:T(8,128)(2,1)}), bf16[8,4,56,128]{3,2,1,0:T(8,128)(2,1)S(1)}, u32[]{:S(2)}, u32[]{:S(2)}) async-start(bf16[8,4,56,128]{3,2,1,0:T(8,128)(2,1)} %reduce_sum.36), calls=%async_computation.2 | async-start | bytes 917504 | tf_op jit(solution)/shard_map/all_to_all | solution.py:339
  78.9 0.0 copy-done.2
  78.9 6.9 %collective-permute-start = (bf16[264,1280]{1,0:T(8,128)(2,1)S(1)}, bf16[264,1280]{1,0:T(8,128)(2,1)S(1)}, u32[]{:S(2)}, u32[]{:S(2)}) collective-permute-start(bf16[264,1280]{1,0:T(8,128)(2,1)S(1)} %copy-done.2), channel_id=1, source_target_pairs={{0,1},{1,2},{2,3},{3,4},{4,5},{5,6},{6,7},{7,8},{8,9},{9,10},{10,1... | collective-permute-start | bytes 2027528 | tf_op jit(solution)/shard_map/ppermute | solution.py:261
  85.8 1.9 %collective-permute-start.1 = (bf16[264,1280]{1,0:T(8,128)(2,1)S(1)}, bf16[264,1280]{1,0:T(8,128)(2,1)S(1)}, u32[]{:S(2)}, u32[]{:S(2)}) collective-permute-start(bf16[264,1280]{1,0:T(8,128)(2,1)S(1)} %copy-done.2), channel_id=1, source_target_pairs={{0,63},{1,0},{2,1},{3,2},{4,3},{5,4},{6,5},{7,6},{8,7},{9,8},{10,9... | collective-permute-start | bytes 2027528 | tf_op jit(solution)/shard_map/ppermute | solution.py:261
  87.7 0.0 all-gather.2.cloned.1.call-done
  87.7 0.0 copy-start.1
  87.7 5.3 %shard_map.113.d_attn = bf16[128,1280]{1,0:T(8,128)(2,1)S(1)} custom-call(bf16[8,160,2560]{2,1,0:T(8,128)(2,1)} %bitcast.14, bf16[128,2560]{1,0:T(8,128)(2,1)} %get-tuple-element.30.grads), custom_call_target="tpu_custom_call" | custom-call | tf_op jit(solution)/shard_map/pallas_call | solution.py:326
  93.1 2.3 %all-to-all-done.2 = bf16[8,4,56,128]{3,2,1,0:T(8,128)(2,1)S(1)} async-done(((bf16[8,4,56,128]{3,2,1,0:T(8,128)(2,1)}), bf16[8,4,56,128]{3,2,1,0:T(8,128)(2,1)S(1)}, u32[]{:S(2)}, u32[]{:S(2)}) %all-to-all-start.2) | async-done | bytes 458784 | tf_op jit(solution)/shard_map/all_to_all | solution.py:339
  95.4 0.1 reduce_sum.37
  95.5 0.7 broadcast_in_dim.12
  96.2 12.0 %all-to-all-start.3 = ((bf16[16,56,128]{2,1,0:T(8,128)(2,1)}), bf16[16,56,128]{2,1,0:T(8,128)(2,1)S(1)}, u32[]{:S(2)}, u32[]{:S(2)}) async-start(bf16[16,56,128]{2,1,0:T(8,128)(2,1)} %bitcast.7), calls=%async_computation.3 | async-start | bytes 458752 | tf_op jit(solution)/shard_map/all_to_all | solution.py:361
  108.2 0.0 collective-permute-done.behind
  108.2 1.9 %collective-permute-done.1.ahead = bf16[264,1280]{1,0:T(8,128)(2,1)S(1)} collective-permute-done((bf16[264,1280]{1,0:T(8,128)(2,1)S(1)}, bf16[264,1280]{1,0:T(8,128)(2,1)S(1)}, u32[]{:S(2)}, u32[]{:S(2)}) %collective-permute-start.1) | collective-permute-done | bytes 675872 | tf_op jit(solution)/shard_map/ppermute | solution.py:261
  110.1 0.0 copy-done.1
  110.1 8.9 %shard_map.114 = (bf16[128,1280]{1,0:T(8,128)(2,1)}, f32[2,128,1280]{2,1,0:T(8,128)}, bf16[2,128,1280]{2,1,0:T(8,128)(2,1)}, bf16[2,128,1280]{2,1,0:T(8,128)(2,1)}) custom-call(s32[1]{0:T(128)S(6)} %copy.12.counts, s32[4,12]{1,0:T(4,128)S(1)} %bitcast.13, bf16[128,1280]{1,0:T(8,128)(2,1)S(1)} %shard_map.113.d_attn, ...), custom_call_target="tpu_custom_call" | custom-call | tf_op jit(solution)/shard_map/pallas_call | solution.py:348
  119.0 0.4 all-to-all-done.3
  119.4 0.8 broadcast_in_dim.14
  120.3 10.0 %all-to-all-start.4 = ((bf16[8,4,56,128]{3,2,1,0:T(8,128)(2,1)}), bf16[8,4,56,128]{3,2,1,0:T(8,128)(2,1)S(1)}, u32[]{:S(2)}, u32[]{:S(2)}) async-start(bf16[8,4,56,128]{3,2,1,0:T(8,128)(2,1)} %broadcast_in_dim.14), calls=%async_computation.4 | async-start | bytes 917504 | tf_op jit(solution)/shard_map/all_to_all | solution.py:364
  130.2 0.0 copy-start
  130.2 2.1 %collective-permute-start.2 = (bf16[2,128,1280]{2,1,0:T(8,128)(2,1)}, bf16[2,128,1280]{2,1,0:T(8,128)(2,1)S(1)}, u32[]{:S(2)}, u32[]{:S(2)}) collective-permute-start(bf16[2,128,1280]{2,1,0:T(8,128)(2,1)} %get-tuple-element.41), channel_id=1, source_target_pairs={{0,1},{1,2},{2,3},{3,4},{4,5},{5,6},{6,7},{7,8},{8,9},{9,10},{10,1... | collective-permute-start | bytes 1966088 | tf_op jit(solution)/shard_map/ppermute | solution.py:261
  132.3 3.0 %collective-permute-start.3 = (bf16[2,128,1280]{2,1,0:T(8,128)(2,1)}, bf16[2,128,1280]{2,1,0:T(8,128)(2,1)S(1)}, u32[]{:S(2)}, u32[]{:S(2)}) collective-permute-start(bf16[2,128,1280]{2,1,0:T(8,128)(2,1)} %get-tuple-element.42), channel_id=1, source_target_pairs={{0,63},{1,0},{2,1},{3,2},{4,3},{5,4},{6,5},{7,6},{8,7},{9,8},{10,9... | collective-permute-start | bytes 1966088 | tf_op jit(solution)/shard_map/ppermute | solution.py:261
  135.3 10.7 %all-to-all-done.4 = bf16[8,4,56,128]{3,2,1,0:T(8,128)(2,1)S(1)} async-done(((bf16[8,4,56,128]{3,2,1,0:T(8,128)(2,1)}), bf16[8,4,56,128]{3,2,1,0:T(8,128)(2,1)S(1)}, u32[]{:S(2)}, u32[]{:S(2)}) %all-to-all-start.4) | async-done | bytes 458784 | tf_op jit(solution)/shard_map/all_to_all | solution.py:364
  146.0 0.1 broadcast_in_dim.30
  146.1 5.4 %all_to_all.32.both = bf16[2,8,4,56,128]{4,3,2,1,0:T(8,128)(2,1)S(1)} all-to-all(bf16[2,8,4,56,128]{4,3,2,1,0:T(8,128)(2,1)S(1)} %broadcast_in_dim.30), channel_id=1, replica_groups=mesh['z_lo'=2,'x'=4,'y'=8,'z_hi'=4,'core'=2] {'core'}, dimensions={0} | all-to-all | bytes 1835008 | tf_op jit(solution)/shard_map/all_to_all | solution.py:365
  151.5 1.0 shard_map.115
  152.5 0.0 collective-permute-done.2.from_behind
  152.5 1.9 %collective-permute-done.3.from_ahead = bf16[2,128,1280]{2,1,0:T(8,128)(2,1)S(1)} collective-permute-done((bf16[2,128,1280]{2,1,0:T(8,128)(2,1)}, bf16[2,128,1280]{2,1,0:T(8,128)(2,1)S(1)}, u32[]{:S(2)}, u32[]{:S(2)}) %collective-permute-start.3) | collective-permute-done | bytes 655392 | tf_op jit(solution)/shard_map/ppermute | solution.py:261
  154.5 0.0 copy-done
  154.5 1.0 shard_map.116
  (1 shorter events, 0.0 us)
Async XLA Ops:
  7.2 80.6 %all-gather.2.cloned.1.call-start = ((), (), s32[]{:S(2)}) async-start(), calls=%async_computation.6 | async-start | bytes 6963200 | tf_op jit(solution)/shard_map/all_gather | solution.py:306
  56.6 22.3 %copy-start.2 = (bf16[264,1280]{1,0:T(8,128)(2,1)S(1)}, bf16[264,1280]{1,0:T(8,128)(2,1)}, u32[]{:S(2)}) copy-start(bf16[264,1280]{1,0:T(8,128)(2,1)} %get-tuple-element.34) | copy-start | bytes 2027524
  73.5 22.0 %all-to-all-start.2 = ((bf16[8,4,56,128]{3,2,1,0:T(8,128)(2,1)}), bf16[8,4,56,128]{3,2,1,0:T(8,128)(2,1)S(1)}, u32[]{:S(2)}, u32[]{:S(2)}) async-start(bf16[8,4,56,128]{3,2,1,0:T(8,128)(2,1)} %reduce_sum.36), calls=%async_computation.2 | async-start | bytes 917504 | tf_op jit(solution)/shard_map/all_to_all | solution.py:339
  78.9 29.3 %collective-permute-start = (bf16[264,1280]{1,0:T(8,128)(2,1)S(1)}, bf16[264,1280]{1,0:T(8,128)(2,1)S(1)}, u32[]{:S(2)}, u32[]{:S(2)}) collective-permute-start(bf16[264,1280]{1,0:T(8,128)(2,1)S(1)} %copy-done.2), channel_id=1, source_target_pairs={{0,1},{1,2},{2,3},{3,4},{4,5},{5,6},{6,7},{7,8},{8,9},{9,10},{10,1... | collective-permute-start | bytes 2027528 | tf_op jit(solution)/shard_map/ppermute | solution.py:261
  85.8 24.3 %collective-permute-start.1 = (bf16[264,1280]{1,0:T(8,128)(2,1)S(1)}, bf16[264,1280]{1,0:T(8,128)(2,1)S(1)}, u32[]{:S(2)}, u32[]{:S(2)}) collective-permute-start(bf16[264,1280]{1,0:T(8,128)(2,1)S(1)} %copy-done.2), channel_id=1, source_target_pairs={{0,63},{1,0},{2,1},{3,2},{4,3},{5,4},{6,5},{7,6},{8,7},{9,8},{10,9... | collective-permute-start | bytes 2027528 | tf_op jit(solution)/shard_map/ppermute | solution.py:261
  87.7 22.3 %copy-start.1 = (s32[1,4,12]{2,1,0:T(4,128)S(1)}, s32[1,4,12]{2,1,0:T(4,128)}, u32[]{:S(2)}) copy-start(s32[1,4,12]{2,1,0:T(4,128)} %param.14) | copy-start | bytes 580
  96.2 23.2 %all-to-all-start.3 = ((bf16[16,56,128]{2,1,0:T(8,128)(2,1)}), bf16[16,56,128]{2,1,0:T(8,128)(2,1)S(1)}, u32[]{:S(2)}, u32[]{:S(2)}) async-start(bf16[16,56,128]{2,1,0:T(8,128)(2,1)} %bitcast.7), calls=%async_computation.3 | async-start | bytes 458752 | tf_op jit(solution)/shard_map/all_to_all | solution.py:361
  120.3 25.7 %all-to-all-start.4 = ((bf16[8,4,56,128]{3,2,1,0:T(8,128)(2,1)}), bf16[8,4,56,128]{3,2,1,0:T(8,128)(2,1)S(1)}, u32[]{:S(2)}, u32[]{:S(2)}) async-start(bf16[8,4,56,128]{3,2,1,0:T(8,128)(2,1)} %broadcast_in_dim.14), calls=%async_computation.4 | async-start | bytes 917504 | tf_op jit(solution)/shard_map/all_to_all | solution.py:364
  130.2 24.2 %copy-start = (f32[2,128,1280]{2,1,0:T(8,128)S(1)}, f32[2,128,1280]{2,1,0:T(8,128)}, u32[]{:S(2)}) copy-start(f32[2,128,1280]{2,1,0:T(8,128)} %get-tuple-element.40.own) | copy-start | bytes 3932164
  130.2 22.3 %collective-permute-start.2 = (bf16[2,128,1280]{2,1,0:T(8,128)(2,1)}, bf16[2,128,1280]{2,1,0:T(8,128)(2,1)S(1)}, u32[]{:S(2)}, u32[]{:S(2)}) collective-permute-start(bf16[2,128,1280]{2,1,0:T(8,128)(2,1)} %get-tuple-element.41), channel_id=1, source_target_pairs={{0,1},{1,2},{2,3},{3,4},{4,5},{5,6},{6,7},{7,8},{8,9},{9,10},{10,1... | collective-permute-start | bytes 1966088 | tf_op jit(solution)/shard_map/ppermute | solution.py:261
  132.3 22.2 %collective-permute-start.3 = (bf16[2,128,1280]{2,1,0:T(8,128)(2,1)}, bf16[2,128,1280]{2,1,0:T(8,128)(2,1)S(1)}, u32[]{:S(2)}, u32[]{:S(2)}) collective-permute-start(bf16[2,128,1280]{2,1,0:T(8,128)(2,1)} %get-tuple-element.42), channel_id=1, source_target_pairs={{0,63},{1,0},{2,1},{3,2},{4,3},{5,4},{6,5},{7,6},{8,7},{9,8},{10,9... | collective-permute-start | bytes 1966088 | tf_op jit(solution)/shard_map/ppermute | solution.py:261
Sparse Core Ops, SparseCore 0:
  11.5 70.2 all-gather.1
